TPU v7x, 128 devices: a whole 4x4x4 slice. The times are simulated.
128 devices in a mesh: table: 16 (over z, y_lo, core), dp: 8 (over x, y_hi).
Axes of the slice: x: 4, y: 4 (y_hi: 2, y_lo: 2; y = y_hi * 2 + y_lo), z: 4, core: 2. Of those that a mesh axis runs over, the one named last changes fastest.
Arguments:
- own_table: bfloat16 [20480, 128], P('table'), may hold values from -6 to 6
- own_accum: float32 [20480], P('table'), may hold values from 0.5 to 8
- sectioned_rows: bfloat16 [16, 768, 128], P(None, 'dp'), may hold values from -6 to 6
- sectioned_accum: float32 [16, 768], replicated, may hold values from 0.5 to 8
- fold_pairs: int32 [16], replicated, may hold values from 0 to 15, each once
- slab_ids: int32 [16, 6], replicated, may hold values from 0 to 5, each once within a row
- bag_blocks: int32 [32768, 16, 4], P('dp', 'table'), may hold values from 0 to 15, as said below
- bag_counts: int32 [32768, 16], P('dp', 'table'), may hold values from 1 to 4
- bag_weights: bfloat16 [32768, 16, 4, 128], P('dp', 'table'), may hold values from -0.25 to 0.25
- top_weight: bfloat16 [2048, 1024], replicated, may hold values from -0.125 to 0.125
- hidden_grad: bfloat16 [32768, 1024], P(('dp', 'table')), may hold values from -6 to 6
Outputs:
- new_table: bfloat16 [32768, 128], P('table')
- new_accum: float32 [32768], P(('table', 'dp'))
- hidden: bfloat16 [32768, 1024], P(('dp', 'table'))
Inputs may be any that keep to these rules, and one draw needn't show every extreme that they name: `bag_blocks`: the used slots (k < bag_counts) of one bag in one feature name distinct blocks; block 15 and block 0 are both read by some bag in every draw. Slots k >= bag_counts[b, t] are unused. `fold_pairs`: A permutation. `slab_ids`: each row a permutation.
All inputs are finite; a program needn't handle non-finite values.
Results may differ from a plain program's by a relative error of at most 0.0065.
Values may be sent and summed in bfloat16 or wider, within the bound.
No kernel may reach another device: no remote copies, remote signals or barrier semaphores. Data moves between devices by JAX's collectives and lax.ppermute only.
A program may use at most 128 MiB of HBM per device.

v0:
```python
import jax
import jax.numpy as jnp
from jax import lax
from jax.sharding import PartitionSpec as P

E = 128
BLK = 128
R = 10
SLAB = 6
K = 4


learn_rate = 0.5
ada_epsilon = 1e-08


def gate_slope(preact):
    sigmoid_part = jax.nn.sigmoid(preact)
    return sigmoid_part * (1.0 + preact * (1.0 - sigmoid_part))


def adagrad_rows(rows, accum, row_grad):
    new_accum = accum + jnp.mean(row_grad * row_grad, axis=1)
    step_size = learn_rate / (jnp.sqrt(new_accum) + ada_epsilon)
    new_rows = (rows.astype(jnp.float32) - step_size[:, None] * row_grad).astype(jnp.bfloat16)
    return (new_rows, new_accum)


def shards(
    own_table,
    own_accum,
    sectioned_rows,
    sectioned_accum,
    fold_pairs,
    slab_ids,
    bag_blocks,
    bag_counts,
    bag_weights,
    top_weight,
    hidden_grad,
):
    partner = fold_pairs[lax.axis_index("table")]
    block_order = slab_ids[partner]
    sectioned_piece = lax.dynamic_index_in_dim(sectioned_rows, partner, 0, keepdims=False)
    slab_rows = lax.all_gather(sectioned_piece, "dp", axis=0, tiled=True)
    folded = jnp.take(slab_rows.reshape(SLAB, BLK, E), block_order, axis=0).reshape(SLAB * BLK, E)
    sectioned_state = lax.dynamic_index_in_dim(sectioned_accum, partner, 0, keepdims=False)
    folded_state = jnp.take(sectioned_state.reshape(SLAB, BLK), block_order, axis=0).reshape(
        SLAB * BLK
    )
    table_rows = jnp.concatenate([own_table, folded], axis=0)
    merged_accum = jnp.concatenate([own_accum, folded_state], axis=0)
    bag_total = bag_blocks.shape[0]
    blocks = bag_blocks[:, 0, :]
    counts = bag_counts[:, 0]
    weights = bag_weights[:, 0]
    column = jnp.arange(R + SLAB, dtype=jnp.int32)
    bag_matrix = jnp.zeros((bag_total, R + SLAB, BLK), jnp.bfloat16)
    for slot_index in range(K):
        slot_hit = (blocks[:, slot_index, None] == column) & (counts[:, None] > slot_index)
        bag_matrix = bag_matrix + jnp.where(
            slot_hit[:, :, None], weights[:, slot_index, None, :], jnp.zeros((), jnp.bfloat16)
        )
    bag_matrix = bag_matrix.reshape(bag_total, (R + SLAB) * BLK)
    pooled = jnp.dot(bag_matrix, table_rows, preferred_element_type=jnp.float32)
    pooled = pooled.astype(jnp.bfloat16)
    gathered = lax.all_to_all(pooled[:, None, :], "table", split_axis=0, concat_axis=1, tiled=True)
    local_bags = gathered.shape[0]
    concat_rows = gathered.reshape(local_bags, -1)
    preact = jnp.dot(concat_rows, top_weight, preferred_element_type=jnp.float32)
    hidden = jax.nn.silu(preact).astype(jnp.bfloat16)
    pre_grad = (hidden_grad.astype(jnp.float32) * gate_slope(preact)).astype(jnp.bfloat16)
    concat_grad = lax.dot_general(
        pre_grad, top_weight, (((1,), (1,)), ((), ())), preferred_element_type=jnp.float32
    ).astype(jnp.bfloat16)
    returned = lax.all_to_all(
        concat_grad.reshape(local_bags, -1, E), "table", split_axis=1, concat_axis=0, tiled=True
    )
    pooled_grad = returned.reshape(bag_total, E)
    row_grad = lax.dot_general(
        bag_matrix, pooled_grad, (((0,), (0,)), ((), ())), preferred_element_type=jnp.float32
    )
    share_rows = row_grad.shape[0] // lax.axis_size("dp")
    share_start = lax.axis_index("dp") * share_rows
    total_grad = lax.psum(row_grad.astype(jnp.bfloat16), "dp").astype(jnp.float32)
    new_table, full_accum = adagrad_rows(table_rows, merged_accum, total_grad)
    new_accum = lax.dynamic_slice_in_dim(full_accum, share_start, share_rows, 0)
    return (new_table, new_accum, hidden)


def solution(mesh):
    placed = (
        P("table", None),
        P("table"),
        P(None, "dp", None),
        P(),
        P(),
        P(),
        P("dp", "table", None),
        P("dp", "table"),
        P("dp", "table", None, None),
        P(),
        P(("dp", "table"), None),
    )
    return jax.shard_map(
        shards,
        mesh=mesh,
        in_specs=placed,
        out_specs=(P("table", None), P(("table", "dp")), P(("dp", "table"), None)),
        check_vma=False,
    )
```

profile of v0, /device:TPU:0, one launch (start us, length us, event | category | flops | bytes accessed | tf_op | source)
XLA Modules:
  0.0 274.6 jit_solution(16966038139794237346)
XLA Ops:
  7.2 0.0 copy-start
  7.2 0.0 all-reduce.2.cloned.1.call-start
  7.2 1.3 dynamic_slice.17
  10.5 0.9 dynamic-slice_reduce_fusion
  11.3 1.1 fusion.27
  12.4 0.9 compare_reduce_fusion.3
  13.3 0.1 fusion.22
  13.4 1.4 copy.46
  14.8 1.4 copy.45
  16.3 0.1 fusion.20
  16.4 1.4 copy.44
  17.8 1.4 copy.42
  19.2 2.7 copy.69
  21.9 1.6 slice_bitcast_fusion.3
  23.6 0.0 copy-done
  23.6 34.5 %all-gather = bf16[1,768,128]{2,1,0:T(8,128)(2,1)S(1)} all-gather(bf16[1,96,128]{2,1,0:T(8,128)(2,1)S(1)} %constant_dynamic-slice_fusion), channel_id=2, replica_groups=mesh['table'=16,'dp'=8] {'dp'}, dimensions={1}, use_global_device_ids=true | all-gather | bytes 221184 | tf_op jit(solution)/shard_map/all_gather | solution.py:45
  58.1 0.1 broadcast_bitcast_fusion
  58.1 0.6 gather_fusion
  58.7 0.8 bitcast_select_fusion
  59.6 39.0 %select_add_fusion = bf16[4096,16,128]{2,1,0:T(8,128)(2,1)S(1)} fusion(pred[4096,16]{1,0:T(8,128)(4,1)} %copy.46, pred[4096,16]{1,0:T(8,128)(4,1)} %copy.45, pred[4096,16]{1,0:T(8,128)(4,1)} %copy.44, pred[4096,16]{1,0:T(8,128)(4,1)} %copy.42, bf16[4096,128]{1,0:T(8,128)(2,1)S(1)} %get-tuple-element.10, bf16[4096,128]{1,0:T(8,128)(2,1)} %get-tuple-element.11, ...), kind=kLoop, calls=%fused_computation.6 | loop fusion | flops 58720256 | bytes 21233664 | tf_op jit(solution)/shard_map/add | solution.py:61
  98.6 0.0 copy-start.1
  98.6 5.7 %copy-done.1 = bf16[4096,16,128]{2,1,0:T(8,128)(2,1)} copy-done((bf16[4096,16,128]{2,1,0:T(8,128)(2,1)}, bf16[4096,16,128]{2,1,0:T(8,128)(2,1)S(1)}, u32[]{:S(2)}) %copy-start.1) | copy-done | bytes 16777240
  104.3 5.6 %fusion.9 = bf16[4096,1,128]{2,0,1:T(8,128)(2,1)S(1)} fusion(bf16[512,8,16,128]{3,2,1,0:T(8,128)(2,1)S(1)} %bitcast.62, bf16[768,128]{1,0:T(8,128)(2,1)} %bitcast_select_fusion, bf16[1280,128]{1,0:T(8,128)(2,1)} %param.11), kind=kOutput, calls=%fused_computation.10 | convolution fusion | flops 2149056512 | bytes 18350080 | tf_op jit(solution)/shard_map/dot_general | solution.py:65
  109.9 0.5 broadcast.257
  110.5 1.4 reduce.13
  111.9 0.3 reshape.321
  112.2 22.7 %all_to_all.30 = bf16[16,2,16384]{2,1,0:T(2,128)(2,1)S(1)} all-to-all(bf16[16,2,16384]{2,1,0:T(2,128)(2,1)S(1)} %reshape.321), channel_id=1, replica_groups=mesh['table'=16,'dp'=8] {'table'}, dimensions={0} | all-to-all | bytes 2097152 | tf_op jit(solution)/shard_map/all_to_all | solution.py:67
  134.9 1.0 reshape.322
  135.9 0.1 copy.50
  136.1 0.5 copy.48
  136.6 4.4 %multiply_convert_fusion = (bf16[256,1024]{1,0:T(8,128)(2,1)}, f32[256,1024]{1,0:T(8,128)S(1)}) fusion(bf16[256,2048]{0,1:T(8,128)(2,1)S(1)} %bitcast.67, bf16[2048,1024]{1,0:T(8,128)(2,1)} %param.20), kind=kOutput, calls=%fused_computation.25 | convolution fusion | flops 1075052544 | bytes 6815744 | tf_op jit(solution)/shard_map/dot_general | solution.py:70
  141.0 3.8 %fusion.15 = bf16[32,16,8,128]{3,2,1,0:T(8,128)(2,1)S(1)} fusion(bf16[2048,1024]{1,0:T(8,128)(2,1)} %param.20, f32[256,1024]{1,0:T(8,128)S(1)} %get-tuple-element.18, bf16[256,1024]{1,0:T(8,128)(2,1)} %param.21), kind=kOutput, calls=%fused_computation.14 | convolution fusion | flops 1076887552 | bytes 6815744 | tf_op jit(solution)/shard_map/dot_general | solution.py:73
  144.8 0.3 copy.70
  145.1 19.1 %all_to_all.31 = bf16[256,16,128]{2,0,1:T(8,128)(2,1)S(1)} all-to-all(bf16[256,16,128]{2,0,1:T(8,128)(2,1)S(1)} %bitcast.66), channel_id=1, replica_groups=mesh['table'=16,'dp'=8] {'table'}, dimensions={1} | all-to-all | bytes 2097152 | tf_op jit(solution)/shard_map/all_to_all | solution.py:76
  164.1 0.0 copy-start.4
  164.1 0.0 copy-start.2
  164.2 0.0 copy-start.3
  164.2 14.7 %fusion.12 = bf16[2048,128]{1,0:T(8,128)(2,1)} fusion(bf16[4096,128]{1,0:T(8,128)(2,1)S(1)} %bitcast.68, bf16[512,8,16,128]{3,2,1,0:T(8,128)(2,1)} %bitcast.63), kind=kOutput, calls=%fused_computation.13 | convolution fusion | flops 2147745792 | bytes 18350080 | tf_op jit(solution)/shard_map/dot_general | solution.py:80
  178.9 0.0 all-reduce.2.cloned.1.call-update
  178.9 0.8 dynamic-slice_reduce_fusion.1
  179.7 0.6 gather_fusion.1
  180.2 0.1 bitcast_select_fusion.1
  180.3 83.2 %all-reduce.2.cloned.1.call-done = bf16[2048,128]{1,0:T(8,128)(2,1)} async-done(((bf16[2048,128]{1,0:T(8,128)(2,1)}), bf16[2048,128]{1,0:T(8,128)(2,1)}) %all-reduce.2.cloned.1.call-update) | async-done | bytes 524304 | tf_op jit(solution)/shard_map/psum | solution.py:85
  263.6 1.4 fusion.16
  264.9 0.0 copy-done.4
  265.0 0.6 dynamic_slice.21
  265.6 0.0 copy-done.2
  265.6 0.0 copy-done.3
  265.6 2.2 fusion.18
  (5 shorter events, 0.0 us)
Async XLA Ops:
  7.2 16.4 %copy-start = (bf16[16,96,128]{2,1,0:T(8,128)(2,1)S(1)}, bf16[16,96,128]{2,1,0:T(8,128)(2,1)}, u32[]{:S(2)}) copy-start(bf16[16,96,128]{2,1,0:T(8,128)(2,1)} %param.13) | copy-start | bytes 1179652
  7.2 256.4 %all-reduce.2.cloned.1.call-start = ((), (), s32[]{:S(2)}) async-start(), calls=%async_computation.2 | async-start | bytes 1048576 | tf_op jit(solution)/shard_map/psum | solution.py:85
  98.6 5.7 %copy-start.1 = (bf16[4096,16,128]{2,1,0:T(8,128)(2,1)}, bf16[4096,16,128]{2,1,0:T(8,128)(2,1)S(1)}, u32[]{:S(2)}) copy-start(bf16[4096,16,128]{2,1,0:T(8,128)(2,1)S(1)} %select_add_fusion) | copy-start | bytes 50331652
  164.1 100.8 %copy-start.4 = (f32[1280]{0:T(1024)S(1)}, f32[1280]{0:T(1024)}, u32[]{:S(2)}) copy-start(f32[1280]{0:T(1024)} %param.12) | copy-start | bytes 15364
  164.1 101.5 %copy-start.2 = (bf16[768,128]{1,0:T(8,128)(2,1)S(1)}, bf16[768,128]{1,0:T(8,128)(2,1)}, u32[]{:S(2)}) copy-start(bf16[768,128]{1,0:T(8,128)(2,1)} %bitcast_select_fusion) | copy-start | bytes 589828
  164.2 101.5 %copy-start.3 = (bf16[1280,128]{1,0:T(8,128)(2,1)S(1)}, bf16[1280,128]{1,0:T(8,128)(2,1)}, u32[]{:S(2)}) copy-start(bf16[1280,128]{1,0:T(8,128)(2,1)} %param.11) | copy-start | bytes 983044
Sparse Core Ops, SparseCore 0:
  179.0 84.4 all-reduce.1
where the time goes:
time: 275 us
  waiting for transfers between devices  83.3 us (30%)
  blocking collectives  76.2 us (28%)
  other arithmetic  46.1 us (17%)
  matrix products  28.5 us (10%)
  local copies, waits for them, and re-layouts  24.3 us (9%)
  between operations  16.1 us (6%)
    psum x1, waiting for transfers between devices, shards(): lax.psum(row_grad.astype(jnp.bfloat16), 'dp').astype(jnp.float32)  83.2 us
    add x1, other arithmetic, shards(): bag_matrix + jnp.where(slot_hit[:, :, None], weights[:, slot_index, None,...  39 us
    all_gather x1, blocking collectives, shards(): slab_rows = lax.all_gather(sectioned_piece, 'dp', axis=0, tiled=True)  34.5 us
    all_to_all x1, blocking collectives, shards(): lax.all_to_all(pooled[:, None, :], 'table', split_axis=0, concat_axis=1,...  22.7 us
    all_to_all x1, blocking collectives, shards(): lax.all_to_all(concat_grad.reshape(local_bags, -1, E), 'table', split_axi...  19.1 us
    dot_general x1, matrix products, shards(): lax.dot_general(bag_matrix, pooled_grad, (((0,), (0,)), ((), ())), prefer...  14.7 us
    unnamed x14, local copies, waits for them, and re-layouts  9.92 us
    and x4, local copies, waits for them, and re-layouts, shards(): (blocks[:, slot_index, None] == column) & (counts[:, None] > slot_index)  5.67 us
  transfers between devices with their start and end apart: 1, of which 1 were waited for; matrix products, arithmetic and copies ran while one was open for 1% of the time, Pallas kernels for 0%

commit v1 on v0

v1 whole, which is shorter than its diff:
```python
import functools

import jax
import jax.numpy as jnp
from jax import lax
from jax.experimental import pallas as pl
from jax.experimental.pallas import tpu as pltpu
from jax.sharding import PartitionSpec as P

E = 128
BLK = 128
R = 10
SLAB = 6
K = 4
NB = R + SLAB

learn_rate = 0.5
ada_epsilon = 1e-08


def build_body(rows, sub, blk_ref, cnt_ref, w_ref, m_ref, eff_ref):
    base = pl.multiple_of(pl.program_id(0) * rows, rows)
    blk = blk_ref[:, pl.ds(base, rows)]
    cnt = cnt_ref[:, pl.ds(base, rows)]
    slot = lax.broadcasted_iota(jnp.int32, (K, rows), 0)
    used = jnp.where(slot < cnt, blk, NB).astype(jnp.float32)
    used = jnp.concatenate([used, jnp.full((8 - K, rows), float(NB), jnp.float32)], axis=0)
    eff_ref[...] = used.T

    def group(g, carry):
        at = pl.multiple_of(g * sub, sub)
        cols = eff_ref[pl.ds(at, sub), :]
        names = [jnp.broadcast_to(cols[:, k:k + 1], (sub, BLK)).astype(jnp.bfloat16) for k in range(K)]
        parts = [w_ref[k, pl.ds(at, sub), :] for k in range(K)]
        zero = jnp.zeros((sub, BLK), jnp.bfloat16)
        for m in range(NB):
            acc = zero
            for k in range(K):
                acc = jnp.where(names[k] == jnp.bfloat16(m), parts[k], acc)
            m_ref[pl.ds(at, sub), m * BLK:(m + 1) * BLK] = acc
        return carry
    lax.fori_loop(0, rows // sub, group, 0)

def build(blocks, counts, weights, rows=512, sub=64):
    bags = blocks.shape[1]
    return pl.pallas_call(
        functools.partial(build_body, rows, sub),
        grid=(bags // rows,),
        in_specs=[pl.BlockSpec((K, bags), lambda i: (0, 0)),
                  pl.BlockSpec((1, bags), lambda i: (0, 0)),
                  pl.BlockSpec((K, rows, BLK), lambda i: (0, i, 0))],
        out_specs=pl.BlockSpec((rows, NB * BLK), lambda i: (i, 0)),
        out_shape=jax.ShapeDtypeStruct((bags, NB * BLK), jnp.bfloat16),
        scratch_shapes=[pltpu.VMEM((rows, 8), jnp.float32)],
        cost_estimate=pl.CostEstimate(flops=bags*NB*BLK*8, bytes_accessed=bags*(NB+K)*BLK*2, transcendentals=0),
        name="build",
    )(blocks, counts, weights)

def pool_body(order_ref, m_ref, own_ref, slab_ref, out_ref, table_ref):
    @pl.when(pl.program_id(0) == 0)
    def _():
        table_ref[0:R * BLK, :] = own_ref[...]
        for j in range(SLAB):
            at = pl.multiple_of(order_ref[j] * BLK, BLK)
            table_ref[(R + j) * BLK:(R + j + 1) * BLK, :] = slab_ref[pl.ds(at, BLK), :]
    out_ref[...] = jnp.dot(m_ref[...], table_ref[...], preferred_element_type=jnp.float32).astype(jnp.bfloat16)

def pool(order, matrix, own, slab, rows=1024):
    bags = matrix.shape[0]
    return pl.pallas_call(
        pool_body,
        grid_spec=pltpu.PrefetchScalarGridSpec(
            num_scalar_prefetch=1, grid=(bags // rows,),
            in_specs=[pl.BlockSpec((rows, NB * BLK), lambda i, o: (i, 0)),
                      pl.BlockSpec((R * BLK, E), lambda i, o: (0, 0)),
                      pl.BlockSpec((SLAB * BLK, E), lambda i, o: (0, 0))],
            out_specs=[pl.BlockSpec((rows, E), lambda i, o: (i, 0)),
                       pl.BlockSpec((NB * BLK, E), lambda i, o: (0, 0))]),
        out_shape=[jax.ShapeDtypeStruct((bags, E), jnp.bfloat16),
                   jax.ShapeDtypeStruct((NB * BLK, E), jnp.bfloat16)],
        cost_estimate=pl.CostEstimate(flops=2*bags*NB*BLK*E, bytes_accessed=bags*NB*BLK*2, transcendentals=0),
        name="pool",
    )(order, matrix, own, slab)

def grad_body(m_ref, g_ref, out_ref, acc_ref):
    step = pl.program_id(0)
    part = jnp.dot(g_ref[...].T, m_ref[...], preferred_element_type=jnp.float32)
    @pl.when(step == 0)
    def _():
        acc_ref[...] = part
    @pl.when(step > 0)
    def _():
        acc_ref[...] += part
    @pl.when(step == pl.num_programs(0) - 1)
    def _():
        for m in range(NB):
            out_ref[m * BLK:(m + 1) * BLK, :] = acc_ref[:, m * BLK:(m + 1) * BLK].T.astype(jnp.bfloat16)

def grad(matrix, g, rows=512):
    bags = matrix.shape[0]
    return pl.pallas_call(
        grad_body,
        grid=(bags // rows,),
        in_specs=[pl.BlockSpec((rows, NB * BLK), lambda i: (i, 0)),
                  pl.BlockSpec((rows, E), lambda i: (i, 0))],
        out_specs=pl.BlockSpec((NB * BLK, E), lambda i: (0, 0)),
        out_shape=jax.ShapeDtypeStruct((NB * BLK, E), jnp.bfloat16),
        scratch_shapes=[pltpu.VMEM((E, NB * BLK), jnp.float32)],
        cost_estimate=pl.CostEstimate(flops=2*bags*NB*BLK*E, bytes_accessed=bags*NB*BLK*2, transcendentals=0),
        name="grad",
    )(matrix, g)

def mlp_body(fan, pair, g_ref, tw_hbm, hg_ref, hid_ref, cg_ref, tw_ref, acc_ref, pre_ref, sem):
    wide = pair * E
    steps = fan // pair
    for p in range(steps):
        pltpu.make_async_copy(tw_hbm.at[pl.ds(p * wide, wide), :], tw_ref.at[pl.ds(p * wide, wide), :], sem.at[p]).start()
    for p in range(steps):
        pltpu.make_async_copy(tw_hbm.at[pl.ds(p * wide, wide), :], tw_ref.at[pl.ds(p * wide, wide), :], sem.at[p]).wait()
        left = jnp.concatenate([g_ref[p * pair + q] for q in range(pair)], axis=1)
        part = jnp.dot(left, tw_ref[p * wide:(p + 1) * wide, :], preferred_element_type=jnp.float32)
        if p == 0:
            acc_ref[...] = part
        else:
            acc_ref[...] += part
    pre = acc_ref[...]
    s = jax.nn.sigmoid(pre)
    hid_ref[...] = (pre * s).astype(jnp.bfloat16)
    slope = s * (1.0 + pre * (1.0 - s))
    pre_ref[...] = (hg_ref[...].astype(jnp.float32) * slope).astype(jnp.bfloat16)
    for p in range(steps):
        out = lax.dot_general(pre_ref[...], tw_ref[p * wide:(p + 1) * wide, :], (((1,), (1,)), ((), ())),
                              preferred_element_type=jnp.float32).astype(jnp.bfloat16)
        for q in range(pair):
            cg_ref[p * pair + q] = out[:, q * E:(q + 1) * E]

def mlp(g, tw, hg, pair=2):
    fan, rows, _ = g.shape
    H = tw.shape[1]
    vm = pl.BlockSpec(memory_space=pltpu.VMEM)
    return pl.pallas_call(
        functools.partial(mlp_body, fan, pair),
        in_specs=[vm, pl.BlockSpec(memory_space=pl.ANY), vm],
        out_specs=[vm, vm],
        out_shape=[jax.ShapeDtypeStruct((rows, H), jnp.bfloat16),
                   jax.ShapeDtypeStruct((fan, rows, E), jnp.bfloat16)],
        scratch_shapes=[pltpu.VMEM(tw.shape, jnp.bfloat16), pltpu.VMEM((rows, H), jnp.float32),
                        pltpu.VMEM((rows, H), jnp.bfloat16), pltpu.SemaphoreType.DMA((fan // pair,))],
        cost_estimate=pl.CostEstimate(flops=4*rows*tw.size, bytes_accessed=tw.size*2, transcendentals=rows*H),
        name="mlp",
    )(g, tw, hg)


def everyone(block, axis):
    fan = lax.axis_size(axis)
    copies = jnp.broadcast_to(block[None], (fan,) + block.shape)
    return lax.all_to_all(copies, axis, split_axis=0, concat_axis=0, tiled=True)


def shards(
    own_table,
    own_accum,
    sectioned_rows,
    sectioned_accum,
    fold_pairs,
    slab_ids,
    bag_blocks,
    bag_counts,
    bag_weights,
    top_weight,
    hidden_grad,
):
    tables = lax.axis_size("table")
    parts = lax.axis_size("dp")
    partner = fold_pairs[lax.axis_index("table")]
    block_order = slab_ids[partner]
    piece = lax.dynamic_index_in_dim(sectioned_rows, partner, 0, keepdims=False)
    slab_rows = everyone(piece, "dp").reshape(SLAB * BLK, E)
    bag_total = bag_blocks.shape[0]
    local_bags = bag_total // tables
    matrix = build(
        bag_blocks[:, 0, :].T,
        bag_counts.reshape(1, bag_total),
        jnp.transpose(bag_weights[:, 0], (1, 0, 2)),
    )
    pooled, table_rows = pool(block_order, matrix, own_table, slab_rows)
    gathered = lax.all_to_all(
        pooled.reshape(tables, local_bags, E), "table", split_axis=0, concat_axis=0, tiled=True
    )
    hidden, concat_grad = mlp(gathered, top_weight, hidden_grad)
    returned = lax.all_to_all(concat_grad, "table", split_axis=0, concat_axis=0, tiled=True)
    row_grad = grad(matrix, returned.reshape(bag_total, E))

    share = NB * BLK // parts
    start = lax.axis_index("dp") * share
    state = lax.dynamic_index_in_dim(sectioned_accum, partner, 0, keepdims=False)
    folded_state = jnp.take(state.reshape(SLAB, BLK), block_order, axis=0).reshape(SLAB * BLK)
    merged_accum = jnp.concatenate([own_accum, folded_state], axis=0)
    accum = lax.dynamic_slice_in_dim(merged_accum, start, share, 0)
    rows = lax.dynamic_slice_in_dim(table_rows, start, share, 0)
    received = lax.all_to_all(
        row_grad.reshape(parts, share, E), "dp", split_axis=0, concat_axis=0, tiled=True
    )
    total = jnp.sum(received.astype(jnp.float32), axis=0)
    new_accum = accum + jnp.mean(total * total, axis=1)
    step_size = learn_rate / (jnp.sqrt(new_accum) + ada_epsilon)
    new_rows = (rows.astype(jnp.float32) - step_size[:, None] * total).astype(jnp.bfloat16)
    new_table = everyone(new_rows, "dp").reshape(NB * BLK, E)
    return (new_table, new_accum, hidden)


def solution(mesh):
    placed = (
        P("table", None),
        P("table"),
        P(None, "dp", None),
        P(),
        P(),
        P(),
        P("dp", "table", None),
        P("dp", "table"),
        P("dp", "table", None, None),
        P(),
        P(("dp", "table"), None),
    )
    return jax.shard_map(
        shards,
        mesh=mesh,
        in_specs=placed,
        out_specs=(P("table", None), P(("table", "dp")), P(("dp", "table"), None)),
        check_vma=False,
    )
```

time: 275 us -> 139 us (0.51)
  waiting for transfers between devices: 83.3 us -> 25.7 us
  other arithmetic: 46.1 us -> 1.86 us
  Pallas kernels: 0 us -> 41.8 us
  blocking collectives: 76.2 us -> 36.1 us
  matrix products: 28.5 us -> 0 us
  starting transfers between devices: 0.04 us -> 18.5 us
  between operations: 16.1 us -> 2.7 us
  local copies, waits for them, and re-layouts: 24.3 us -> 11.2 us
    psum x1 -> x0, waiting for transfers between devices: 83.2 us -> none  [shards(): lax.psum(row_grad.astype(jnp.bfloat16), 'dp').astype(jnp.float32)]
    pallas_call x0 -> x4, Pallas kernels: none -> 41.8 us  [the longest x1 14.4 us: build(): pl.pallas_call(functools.partial(build_body, rows, sub), grid=(bags // ro...]
    add x1 -> x0, other arithmetic: 39 us -> none  [shards(): bag_matrix + jnp.where(slot_hit[:, :, None], weights[:, slot_index, None,...]
    all_gather x1 -> x0, blocking collectives: 34.5 us -> none  [shards(): slab_rows = lax.all_gather(sectioned_piece, 'dp', axis=0, tiled=True)]
    dot_general x4 -> x0, matrix products: 28.5 us -> none  [the longest x1 14.7 us: shards(): lax.dot_general(bag_matrix, pooled_grad, (((0,), (0,)), ((), ())), prefer...]
    all_to_all x0 -> x3, waiting for transfers between devices: none -> 25.7 us  [the longest x1 16.5 us: shards(): lax.all_to_all(concat_grad, 'table', split_axis=0, concat_axis=0, tiled=T...]
    all_to_all x0 -> x3, starting transfers between devices: none -> 18.5 us  [the longest x1 7.81 us: shards(): lax.all_to_all(row_grad.reshape(parts, share, E), 'dp', split_axis=0, con...]
    and x4 -> x0, local copies, waits for them, and re-layouts: 5.67 us -> none  [shards(): (blocks[:, slot_index, None] == column) & (counts[:, None] > slot_index)]
  transfers between devices with their start and end apart: 1 -> 3, of which waited for: 1 -> 2; matrix products, arithmetic and copies ran while one was open for 1% -> 5% of each run, Pallas kernels for 0% -> 10%
where the time goes in v1:
time: 139 us; the launch traced here: 138 us
  Pallas kernels  41.8 us (30%)
  blocking collectives  36.1 us (26%)
  waiting for transfers between devices  25.7 us (18%)
  starting transfers between devices  18.5 us (13%)
  local copies, waits for them, and re-layouts  11.2 us (8%)
  between operations  2.7 us (2%)
  other arithmetic  1.86 us (1%)
    all_to_all x1, blocking collectives, shards(): lax.all_to_all(pooled.reshape(tables, local_bags, E), 'table', split_axis...  22.1 us
    all_to_all x1, waiting for transfers between devices, shards(): lax.all_to_all(concat_grad, 'table', split_axis=0, concat_axis=0, tiled=T...  16.5 us
    pallas_call x1, Pallas kernels, build(): pl.pallas_call(functools.partial(build_body, rows, sub), grid=(bags // ro...  14.4 us
    all_to_all x1, blocking collectives, everyone(): return lax.all_to_all(copies, axis, split_axis=0, concat_axis=0, tiled=True)  14 us
    pallas_call x1, Pallas kernels, grad(): pl.pallas_call(grad_body, grid=(bags // rows,), in_specs=[pl.BlockSpec((r...  10.9 us
    pallas_call x1, Pallas kernels, pool(): pl.pallas_call(pool_body, grid_spec=pltpu.PrefetchScalarGridSpec(num_scal...  10.1 us
    all_to_all x1, waiting for transfers between devices, shards(): lax.all_to_all(row_grad.reshape(parts, share, E), 'dp', split_axis=0, con...  9.17 us
    all_to_all x1, starting transfers between devices, shards(): lax.all_to_all(row_grad.reshape(parts, share, E), 'dp', split_axis=0, con...  7.81 us
  transfers between devices with their start and end apart: 3, of which 2 were waited for; matrix products, arithmetic and copies ran while one was open for 5% of the time, Pallas kernels for 10%

profile of v1, /device:TPU:0, one launch (start us, length us, event | category | flops | bytes accessed | tf_op | source)
XLA Modules:
  0.0 137.9 jit_solution(16202745991079591949)
XLA Ops:
  0.6 0.0 copy-start
  0.7 1.3 dynamic_slice.20
  3.9 0.0 copy-done
  3.9 0.7 broadcast_in_dim.26
  4.6 7.0 %all-to-all-start = ((bf16[8,96,128]{2,1,0:T(8,128)(2,1)}), bf16[8,96,128]{2,1,0:T(8,128)(2,1)S(1)}, u32[]{:S(2)}, u32[]{:S(2)}) async-start(bf16[8,96,128]{2,1,0:T(8,128)(2,1)} %broadcast_in_dim.26), calls=%async_computation | async-start | bytes 393216 | tf_op jit(solution)/shard_map/all_to_all | solution.py:157
  11.7 0.0 copy-start.4
  11.7 4.7 %copy.16 = bf16[4096,1,4,128]{3,0,2,1:T(8,128)(2,1)} copy(bf16[4096,1,4,128]{3,2,1,0:T(4,128)(2,1)} %param.19) | data formatting | bytes 8388608 | tf_op args[8]
  16.3 0.0 copy-done.4
  16.3 0.7 dynamic-slice_reduce_fusion.order_ref
  17.0 14.4 %build.1.m_ref = bf16[4096,2048]{1,0:T(8,128)(2,1)} custom-call(s32[4,4096]{1,0:T(4,128)} %bitcast.31, s32[1,4096]{1,0:T(1,128)} %bitcast.32, bf16[4,4096,128]{2,1,0:T(8,128)(2,1)} %bitcast.24), custom_call_target="tpu_custom_call" | custom-call | flops 67108864 | bytes 20971520 | tf_op jit(solution)/shard_map/build/pallas_call | solution.py:46
  31.4 0.0 all-to-all-done
  31.4 0.0 copy-start.2
  31.4 0.7 copy-done.2
  32.1 10.1 %pool.1 = (bf16[4096,128]{1,0:T(8,128)(2,1)}, bf16[2048,128]{1,0:T(8,128)(2,1)}) custom-call(s32[6]{0:T(128)} %dynamic-slice_reduce_fusion.order_ref, bf16[4096,2048]{1,0:T(8,128)(2,1)} %build.1.m_ref, bf16[1280,128]{1,0:T(8,128)(2,1)} %own_ref.1, bf16[768,128]{1,0:T(8,128)(2,1)} %bitcast.29), custom_call_target="tpu_custom_call" | custom-call | flops 2147483648 | bytes 16777216 | tf_op jit(solution)/shard_map/pool/pallas_call | solution.py:70
  42.2 22.1 %all_to_all.25.g_ref = bf16[16,256,128]{2,1,0:T(8,128)(2,1)} all-to-all(bf16[16,256,128]{2,1,0:T(8,128)(2,1)} %bitcast.28), channel_id=1, replica_groups=mesh['table'=16,'dp'=8] {'table'}, dimensions={0} | all-to-all | bytes 2097152 | tf_op jit(solution)/shard_map/all_to_all | solution.py:187
  64.3 0.0 copy-start.5
  64.3 6.4 %mlp.1 = (bf16[256,1024]{1,0:T(8,128)(2,1)}, bf16[16,256,128]{2,1,0:T(8,128)(2,1)}) custom-call(bf16[16,256,128]{2,1,0:T(8,128)(2,1)} %all_to_all.25.g_ref, bf16[2048,1024]{1,0:T(8,128)(2,1)} %tw_hbm.1, bf16[256,1024]{1,0:T(8,128)(2,1)} %hg_ref.1), custom_call_target="tpu_custom_call" | custom-call | flops 2147483648 | bytes 4194304 | tf_op jit(solution)/shard_map/mlp/pallas_call | solution.py:141
  70.7 3.7 %all-to-all-start.2 = ((bf16[16,256,128]{2,1,0:T(8,128)(2,1)}), bf16[16,256,128]{2,1,0:T(8,128)(2,1)S(1)}, u32[]{:S(2)}, u32[]{:S(2)}) async-start(bf16[16,256,128]{2,1,0:T(8,128)(2,1)} %get-tuple-element.9), calls=%async_computation.2 | async-start | bytes 2097152 | tf_op jit(solution)/shard_map/all_to_all | solution.py:191
  74.4 0.0 copy-done.5
  74.4 16.5 %all-to-all-done.2 = bf16[16,256,128]{2,1,0:T(8,128)(2,1)S(1)} async-done(((bf16[16,256,128]{2,1,0:T(8,128)(2,1)}), bf16[16,256,128]{2,1,0:T(8,128)(2,1)S(1)}, u32[]{:S(2)}, u32[]{:S(2)}) %all-to-all-start.2) | async-done | bytes 1048608 | tf_op jit(solution)/shard_map/all_to_all | solution.py:191
  90.9 0.0 copy-start.1
  90.9 1.0 copy-done.1
  91.9 0.0 copy-start.3
  91.9 10.9 %grad.1 = bf16[2048,128]{1,0:T(8,128)(2,1)} custom-call(bf16[4096,2048]{1,0:T(8,128)(2,1)} %build.1.m_ref, bf16[4096,128]{1,0:T(8,128)(2,1)} %bitcast.25), custom_call_target="tpu_custom_call" | custom-call | flops 2147483648 | bytes 16777216 | tf_op jit(solution)/shard_map/grad/pallas_call | solution.py:101
  102.7 7.8 %all-to-all-start.3 = ((bf16[8,256,128]{2,1,0:T(8,128)(2,1)}), bf16[8,256,128]{2,1,0:T(8,128)(2,1)S(1)}, u32[]{:S(2)}, u32[]{:S(2)}) async-start(bf16[8,256,128]{2,1,0:T(8,128)(2,1)} %bitcast.26), calls=%async_computation.3 | async-start | bytes 1048576 | tf_op jit(solution)/shard_map/all_to_all | solution.py:201
  110.6 0.8 dynamic-slice_reduce_fusion.1
  111.3 0.6 gather_fusion
  111.9 0.1 select_bitcast_fusion
  112.0 9.2 %all-to-all-done.3 = bf16[8,256,128]{2,1,0:T(8,128)(2,1)S(1)} async-done(((bf16[8,256,128]{2,1,0:T(8,128)(2,1)}), bf16[8,256,128]{2,1,0:T(8,128)(2,1)S(1)}, u32[]{:S(2)}, u32[]{:S(2)}) %all-to-all-start.3) | async-done | bytes 524320 | tf_op jit(solution)/shard_map/all_to_all | solution.py:201
  121.2 0.1 convert_reduce_fusion
  121.2 0.1 multiply_reduce_fusion
  121.3 0.0 copy-done.3
  121.4 0.7 add_divide_fusion
  122.0 0.9 subtract_convert_fusion
  122.9 0.1 broadcast_in_dim.29
  123.0 14.0 %all_to_all.26 = bf16[8,256,128]{2,1,0:T(8,128)(2,1)S(1)} all-to-all(bf16[8,256,128]{2,1,0:T(8,128)(2,1)S(1)} %broadcast_in_dim.29), channel_id=1, replica_groups=mesh['table'=16,'dp'=8] {'dp'}, dimensions={0} | all-to-all | bytes 1048576 | tf_op jit(solution)/shard_map/all_to_all | solution.py:157
  137.1 0.8 copy.18
  (4 shorter events, 0.0 us)
Async XLA Ops:
  0.6 3.3 %copy-start = (bf16[16,96,128]{2,1,0:T(8,128)(2,1)S(1)}, bf16[16,96,128]{2,1,0:T(8,128)(2,1)}, u32[]{:S(2)}) copy-start(bf16[16,96,128]{2,1,0:T(8,128)(2,1)} %param.13) | copy-start | bytes 1179652
  4.6 26.8 %all-to-all-start = ((bf16[8,96,128]{2,1,0:T(8,128)(2,1)}), bf16[8,96,128]{2,1,0:T(8,128)(2,1)S(1)}, u32[]{:S(2)}, u32[]{:S(2)}) async-start(bf16[8,96,128]{2,1,0:T(8,128)(2,1)} %broadcast_in_dim.26), calls=%async_computation | async-start | bytes 393216 | tf_op jit(solution)/shard_map/all_to_all | solution.py:157
  11.7 4.7 %copy-start.4 = (s32[16,6]{0,1:T(8,128)S(1)}, s32[16,6]{0,1:T(8,128)}, u32[]{:S(2)}) copy-start(s32[16,6]{0,1:T(8,128)} %param.16) | copy-start | bytes 1156
  31.4 0.7 copy-start.2
  64.3 10.1 %copy-start.5 = (s32[6]{0:T(128)S(1)}, s32[6]{0:T(128)}, u32[]{:S(2)}) copy-start(s32[6]{0:T(128)} %dynamic-slice_reduce_fusion.order_ref) | copy-start | bytes 76
  70.7 20.2 %all-to-all-start.2 = ((bf16[16,256,128]{2,1,0:T(8,128)(2,1)}), bf16[16,256,128]{2,1,0:T(8,128)(2,1)S(1)}, u32[]{:S(2)}, u32[]{:S(2)}) async-start(bf16[16,256,128]{2,1,0:T(8,128)(2,1)} %get-tuple-element.9), calls=%async_computation.2 | async-start | bytes 2097152 | tf_op jit(solution)/shard_map/all_to_all | solution.py:191
  90.9 1.0 copy-start.1
  91.9 29.5 %copy-start.3 = (f32[1280]{0:T(1024)S(1)}, f32[1280]{0:T(1024)}, u32[]{:S(2)}) copy-start(f32[1280]{0:T(1024)} %param.12) | copy-start | bytes 15364
  102.7 18.4 %all-to-all-start.3 = ((bf16[8,256,128]{2,1,0:T(8,128)(2,1)}), bf16[8,256,128]{2,1,0:T(8,128)(2,1)S(1)}, u32[]{:S(2)}, u32[]{:S(2)}) async-start(bf16[8,256,128]{2,1,0:T(8,128)(2,1)} %bitcast.26), calls=%async_computation.3 | async-start | bytes 1048576 | tf_op jit(solution)/shard_map/all_to_all | solution.py:201

commit v2 on v0

v2 whole, which is shorter than its diff:
```python
import functools

import jax
import jax.numpy as jnp
from jax import lax
from jax.experimental import pallas as pl
from jax.experimental.pallas import tpu as pltpu
from jax.sharding import PartitionSpec as P

E = 128
BLK = 128
R = 10
SLAB = 6
K = 4
NB = R + SLAB
TILE = 16

learn_rate = 0.5
ada_epsilon = 1e-08

ANY = pl.BlockSpec(memory_space=pl.ANY)
SMEM = pl.BlockSpec(memory_space=pltpu.SMEM)
VMEM = pl.BlockSpec(memory_space=pltpu.VMEM)


def spread_body(half, block_ref, count_ref, weight_ref, out_ref, perm_ref, part_ref):
    step = pl.program_id(0)
    groups = out_ref.shape[0]
    wide = K * BLK

    @pl.when(step == 0)
    def _():
        row = lax.broadcasted_iota(jnp.int32, (wide, BLK), 0)
        lane = lax.broadcasted_iota(jnp.int32, (wide, BLK), 1)
        for k in range(K):
            perm_ref[k] = jnp.where(row == lane * K + k, 1.0, 0.0).astype(jnp.bfloat16)

    for g in range(groups):
        turned = jnp.concatenate([weight_ref[g, BLK * n : BLK * (n + 1), :].T for n in range(K)], axis=1)
        for k in range(0, K, 2):
            right = jnp.concatenate([perm_ref[k], perm_ref[k + 1]], axis=1)
            got = jnp.dot(turned, right, preferred_element_type=jnp.float32).astype(jnp.bfloat16)
            part_ref[g, k] = got[:, :BLK]
            part_ref[g, k + 1] = got[:, BLK:]

    for g in range(groups):
        base = pl.multiple_of(((step * groups + g) * 2 + half) * BLK, BLK)
        blocks = block_ref[:, pl.ds(base, BLK)]
        counts = count_ref[:, pl.ds(base, BLK)]
        names = []
        for k in range(K):
            name = jnp.where(counts > k, blocks[k : k + 1, :], NB).astype(jnp.float32)
            names.append(jnp.broadcast_to(name, (TILE, BLK)).astype(jnp.bfloat16))
        for m in range(NB):
            hits = [names[k] == jnp.bfloat16(m) for k in range(K)]
            for s in range(0, BLK, TILE):
                value = jnp.zeros((TILE, BLK), jnp.bfloat16)
                for k in range(K):
                    value = jnp.where(hits[k], part_ref[g, k, s : s + TILE, :], value)
                out_ref[g, m * BLK + s : m * BLK + s + TILE, :] = value


def spread(blocks, counts, weights, half, join=2):
    bags = blocks.shape[1]
    groups = bags // (2 * BLK)
    return pl.pallas_call(
        functools.partial(spread_body, half),
        grid=(groups // join,),
        in_specs=[
            pl.BlockSpec((K, bags), lambda i: (0, 0)),
            pl.BlockSpec((1, bags), lambda i: (0, 0)),
            pl.BlockSpec((join, None, K * BLK, BLK), lambda i: (i, half, 0, 0)),
        ],
        out_specs=pl.BlockSpec((join, NB * BLK, BLK), lambda i: (i, 0, 0)),
        out_shape=jax.ShapeDtypeStruct((groups, NB * BLK, BLK), jnp.bfloat16),
        scratch_shapes=[
            pltpu.VMEM((K, K * BLK, BLK), jnp.bfloat16),
            pltpu.VMEM((join, K, BLK, BLK), jnp.bfloat16),
        ],
        cost_estimate=pl.CostEstimate(
            flops=bags * NB * BLK * 64, bytes_accessed=bags * (NB + K) * BLK, transcendentals=0
        ),
        name="spread",
    )(blocks, counts, weights.reshape(groups, 2, K * BLK, BLK))


def merge(order_ref, own_ref, slab_ref, table_ref, turned_ref):
    table_ref[0 : R * BLK, :] = own_ref[...]
    for j in range(SLAB):
        at = pl.multiple_of(order_ref[j] * BLK, BLK)
        table_ref[(R + j) * BLK : (R + j + 1) * BLK, :] = slab_ref[pl.ds(at, BLK), :]
    for m in range(NB):
        turned_ref[:, m * BLK : (m + 1) * BLK] = table_ref[m * BLK : (m + 1) * BLK, :].T


def pool_body(first, *refs):
    if first:
        order_ref, own_ref, slab_ref, matrix_ref, out_ref, table_ref, turned_ref = refs

        @pl.when(pl.program_id(0) == 0)
        def _():
            merge(order_ref, own_ref, slab_ref, table_ref, turned_ref)
    else:
        turned_ref, matrix_ref, out_ref = refs
    join = matrix_ref.shape[0]
    right = jnp.concatenate([matrix_ref[q] for q in range(join)], axis=1)
    got = jnp.dot(turned_ref[...], right, preferred_element_type=jnp.float32)
    got = got.T.astype(jnp.bfloat16)
    for q in range(join):
        out_ref[q] = got[q * BLK : (q + 1) * BLK, :]


def pool(source, matrix, first, join=4):
    groups = matrix.shape[0]
    whole = lambda *shape: pl.BlockSpec(shape, lambda i: (0, 0))
    turned = whole(E, NB * BLK)
    ins = [SMEM, whole(R * BLK, E), whole(SLAB * BLK, E)] if first else [turned]
    outs = [pl.BlockSpec((join, BLK, E), lambda i: (i, 0, 0))]
    shapes = [jax.ShapeDtypeStruct((groups, BLK, E), jnp.bfloat16)]
    if first:
        outs += [whole(NB * BLK, E), turned]
        shapes += [
            jax.ShapeDtypeStruct((NB * BLK, E), jnp.bfloat16),
            jax.ShapeDtypeStruct((E, NB * BLK), jnp.bfloat16),
        ]
    return pl.pallas_call(
        functools.partial(pool_body, first),
        grid=(groups // join,),
        in_specs=ins + [pl.BlockSpec((join, NB * BLK, BLK), lambda i: (i, 0, 0))],
        out_specs=outs,
        out_shape=shapes,
        cost_estimate=pl.CostEstimate(
            flops=2 * matrix.size * E, bytes_accessed=matrix.size * 2, transcendentals=0
        ),
        name="pool",
    )(*source, matrix)


def layer_body(pair, start, *refs):
    if start:
        hid_before, fan_ref, top_hbm, cot_ref, hid_ref, out_ref, top_ref, sum_ref, pre_ref, sem = refs
    else:
        fan_ref, top_hbm, cot_ref, hid_ref, out_ref, top_ref, sum_ref, pre_ref, sem = refs
    fan, rows, _ = fan_ref.shape
    wide = pair * E
    steps = fan // pair

    def fetch(p):
        span = pl.ds(p * wide, wide)
        return pltpu.make_async_copy(top_hbm.at[span, :], top_ref.at[span, :], sem.at[p])

    for p in range(steps):
        fetch(p).start()
    if start:
        hid_ref[0:start, :] = hid_before[...]
    for p in range(steps):
        left = jnp.concatenate([fan_ref[p * pair + q] for q in range(pair)], axis=1)
        fetch(p).wait()
        part = jnp.dot(left, top_ref[p * wide : (p + 1) * wide, :], preferred_element_type=jnp.float32)
        if p == 0:
            sum_ref[...] = part
        else:
            sum_ref[...] += part
    preact = sum_ref[...]
    gate = jax.nn.sigmoid(preact)
    hid_ref[start : start + rows, :] = (preact * gate).astype(jnp.bfloat16)
    slope = gate * (1.0 + preact * (1.0 - gate))
    cot = cot_ref[start : start + rows, :].astype(jnp.float32)
    pre_ref[...] = (cot * slope).astype(jnp.bfloat16)
    for p in range(steps):
        back = lax.dot_general(
            pre_ref[...],
            top_ref[p * wide : (p + 1) * wide, :],
            (((1,), (1,)), ((), ())),
            preferred_element_type=jnp.float32,
        ).astype(jnp.bfloat16)
        for q in range(pair):
            out_ref[p * pair + q] = back[:, q * E : (q + 1) * E]


def layer(fan, top_weight, cotangent, before=(), pair=2):
    tables, rows, _ = fan.shape
    hidden = top_weight.shape[1]
    start = before[0].shape[0] if before else 0
    return pl.pallas_call(
        functools.partial(layer_body, pair, start),
        in_specs=[VMEM] * len(before) + [VMEM, ANY, VMEM],
        out_specs=[VMEM, VMEM],
        out_shape=[
            jax.ShapeDtypeStruct((start + rows, hidden), jnp.bfloat16),
            jax.ShapeDtypeStruct((tables, rows, E), jnp.bfloat16),
        ],
        scratch_shapes=[
            pltpu.VMEM(top_weight.shape, jnp.bfloat16),
            pltpu.VMEM((rows, hidden), jnp.float32),
            pltpu.VMEM((rows, hidden), jnp.bfloat16),
            pltpu.SemaphoreType.DMA((tables // pair,)),
        ],
        cost_estimate=pl.CostEstimate(
            flops=4 * rows * top_weight.size, bytes_accessed=rows * hidden * 6, transcendentals=rows * hidden
        ),
        name="layer",
    )(*before, fan, top_weight, cotangent)


def grad_body(more, *refs):
    if more:
        before_ref, matrix_ref, grad_ref, out_ref = refs
    else:
        matrix_ref, grad_ref, out_ref = refs
    left = jnp.concatenate([matrix_ref[q] for q in range(matrix_ref.shape[0])], axis=1)
    total = jnp.dot(left, grad_ref[...], preferred_element_type=jnp.float32)
    if more:
        total = total + before_ref[...]
    out_ref[...] = total.astype(out_ref.dtype)


def grad(matrix, pooled_grad, before=(), tile=256):
    groups = matrix.shape[0]
    block = pl.BlockSpec((tile, E), lambda i: (i, 0))
    return pl.pallas_call(
        functools.partial(grad_body, bool(before)),
        grid=(NB * BLK // tile,),
        in_specs=[block] * len(before)
        + [
            pl.BlockSpec((groups, tile, BLK), lambda i: (0, i, 0)),
            pl.BlockSpec((groups * BLK, E), lambda i: (0, 0)),
        ],
        out_specs=block,
        out_shape=jax.ShapeDtypeStruct((NB * BLK, E), jnp.bfloat16 if before else jnp.float32),
        cost_estimate=pl.CostEstimate(
            flops=2 * matrix.size * E, bytes_accessed=matrix.size * 2, transcendentals=0
        ),
        name="grad",
    )(*before, matrix, pooled_grad)


def everyone(block, axis):
    fan = lax.axis_size(axis)
    copies = jnp.broadcast_to(block[None], (fan,) + block.shape)
    return lax.all_to_all(copies, axis, split_axis=0, concat_axis=0, tiled=True)


def swap(blocks, axis):
    return lax.all_to_all(blocks, axis, split_axis=0, concat_axis=0, tiled=True)


def shards(
    own_table,
    own_accum,
    sectioned_rows,
    sectioned_accum,
    fold_pairs,
    slab_ids,
    bag_blocks,
    bag_counts,
    bag_weights,
    top_weight,
    hidden_grad,
):
    parts = lax.axis_size("dp")
    partner = fold_pairs[lax.axis_index("table")]
    block_order = slab_ids[partner]
    piece = lax.dynamic_index_in_dim(sectioned_rows, partner, 0, keepdims=False)
    slab_rows = everyone(piece, "dp").reshape(SLAB * BLK, E)
    bag_total = bag_blocks.shape[0]
    blocks = bag_blocks[:, 0, :].T
    counts = bag_counts.reshape(1, bag_total)
    even = spread(blocks, counts, bag_weights, 0)
    pooled, table_rows, turned = pool((block_order, own_table, slab_rows), even, True)
    pooled, blocks = lax.optimization_barrier((pooled, blocks))
    fan_even = swap(pooled, "table")
    odd = spread(blocks, counts, bag_weights, 1)
    (pooled,) = pool((turned,), odd, False)
    fan_odd = swap(pooled, "table")
    hidden, back = layer(fan_even, top_weight, hidden_grad)
    back_even = swap(back, "table")
    hidden, back = layer(fan_odd, top_weight, hidden_grad, (hidden,))
    back_odd = swap(back, "table")
    row_grad = grad(even, back_even.reshape(bag_total // 2, E))
    row_grad = grad(odd, back_odd.reshape(bag_total // 2, E), (row_grad,))

    share = NB * BLK // parts
    start = lax.axis_index("dp") * share
    state = lax.dynamic_index_in_dim(sectioned_accum, partner, 0, keepdims=False)
    folded_state = jnp.take(state.reshape(SLAB, BLK), block_order, axis=0).reshape(SLAB * BLK)
    merged_accum = jnp.concatenate([own_accum, folded_state], axis=0)
    accum = lax.dynamic_slice_in_dim(merged_accum, start, share, 0)
    rows = lax.dynamic_slice_in_dim(table_rows, start, share, 0)
    received = swap(row_grad.reshape(parts, share, E), "dp")
    total = jnp.sum(received.astype(jnp.float32), axis=0)
    new_accum = accum + jnp.mean(total * total, axis=1)
    step_size = learn_rate / (jnp.sqrt(new_accum) + ada_epsilon)
    new_rows = (rows.astype(jnp.float32) - step_size[:, None] * total).astype(jnp.bfloat16)
    new_table = everyone(new_rows, "dp").reshape(NB * BLK, E)
    return (new_table, new_accum, hidden)


def solution(mesh):
    placed = (
        P("table", None),
        P("table"),
        P(None, "dp", None),
        P(),
        P(),
        P(),
        P("dp", "table", None),
        P("dp", "table"),
        P("dp", "table", None, None),
        P(),
        P(("dp", "table"), None),
    )
    return jax.shard_map(
        shards,
        mesh=mesh,
        in_specs=placed,
        out_specs=(P("table", None), P(("table", "dp")), P(("dp", "table"), None)),
        check_vma=False,
    )
```

time: 275 us -> 140 us (0.51)
  waiting for transfers between devices: 83.3 us -> 21 us
  blocking collectives: 76.2 us -> 14 us
  Pallas kernels: 0 us -> 57.9 us
  other arithmetic: 46.1 us -> 1.86 us
  starting transfers between devices: 0.04 us -> 33.3 us
  matrix products: 28.5 us -> 0 us
  local copies, waits for them, and re-layouts: 24.3 us -> 7.07 us
  between operations: 16.1 us -> 2.76 us
    psum x1 -> x0, waiting for transfers between devices: 83.2 us -> none  [shards(): lax.psum(row_grad.astype(jnp.bfloat16), 'dp').astype(jnp.float32)]
    pallas_call x0 -> x8, Pallas kernels: none -> 57.9 us  [the longest x2 17.2 us: spread(): pl.pallas_call(functools.partial(spread_body, half), grid=(groups // join...]
    add x1 -> x0, other arithmetic: 39 us -> none  [shards(): bag_matrix + jnp.where(slot_hit[:, :, None], weights[:, slot_index, None,...]
    all_gather x1 -> x0, blocking collectives: 34.5 us -> none  [shards(): slab_rows = lax.all_gather(sectioned_piece, 'dp', axis=0, tiled=True)]
    all_to_all x0 -> x6, starting transfers between devices: none -> 33.3 us  [the longest x5 26.2 us: swap(): return lax.all_to_all(blocks, axis, split_axis=0, concat_axis=0, tiled=True)]
    dot_general x4 -> x0, matrix products: 28.5 us -> none  [the longest x1 14.7 us: shards(): lax.dot_general(bag_matrix, pooled_grad, (((0,), (0,)), ((), ())), prefer...]
    all_to_all x2 -> x1, blocking collectives: 41.7 us -> 14 us  [everyone(): return lax.all_to_all(copies, axis, split_axis=0, concat_axis=0, tiled=True)]
    all_to_all x0 -> x6, waiting for transfers between devices: none -> 21 us  [the longest x5 21 us: swap(): return lax.all_to_all(blocks, axis, split_axis=0, concat_axis=0, tiled=True)]
  transfers between devices with their start and end apart: 1 -> 6, of which waited for: 1 -> 4; matrix products, arithmetic and copies ran while one was open for 1% -> 2% of each run, Pallas kernels for 0% -> 31%
where the time goes in v2:
time: 140 us; the launch traced here: 138 us
  Pallas kernels  57.9 us (41%)
  starting transfers between devices  33.3 us (24%)
  waiting for transfers between devices  21 us (15%)
  blocking collectives  14 us (10%)
  local copies, waits for them, and re-layouts  7.07 us (5%)
  between operations  2.76 us (2%)
  other arithmetic  1.86 us (1%)
    all_to_all x5, starting transfers between devices, swap(): return lax.all_to_all(blocks, axis, split_axis=0, concat_axis=0, tiled=True)  26.2 us
    all_to_all x5, waiting for transfers between devices, swap(): return lax.all_to_all(blocks, axis, split_axis=0, concat_axis=0, tiled=True)  21 us
    pallas_call x2, Pallas kernels, spread(): pl.pallas_call(functools.partial(spread_body, half), grid=(groups // join...  17.2 us
    pallas_call x2, Pallas kernels, grad(): pl.pallas_call(functools.partial(grad_body, bool(before)), grid=(NB * BLK...  16.9 us
    all_to_all x1, blocking collectives, everyone(): return lax.all_to_all(copies, axis, split_axis=0, concat_axis=0, tiled=True)  14 us
    pallas_call x2, Pallas kernels, pool(): pl.pallas_call(functools.partial(pool_body, first), grid=(groups // join,...  11.9 us
    pallas_call x2, Pallas kernels, layer(): pl.pallas_call(functools.partial(layer_body, pair, start), in_specs=[VMEM...  11.8 us
    all_to_all x1, starting transfers between devices, everyone(): return lax.all_to_all(copies, axis, split_axis=0, concat_axis=0, tiled=True)  7.04 us
  transfers between devices with their start and end apart: 6, of which 4 were waited for; matrix products, arithmetic and copies ran while one was open for 2% of the time, Pallas kernels for 31%

profile of v2, /device:TPU:0, one launch (start us, length us, event | category | flops | bytes accessed | tf_op | source)
XLA Modules:
  0.0 137.9 jit_solution(1987951313047251888)
XLA Ops:
  0.6 0.0 copy-start
  0.7 1.3 dynamic_slice.20
  3.9 0.0 copy-done
  3.9 0.7 broadcast_in_dim.26
  4.6 7.0 %all-to-all-start = ((bf16[8,96,128]{2,1,0:T(8,128)(2,1)}), bf16[8,96,128]{2,1,0:T(8,128)(2,1)S(1)}, u32[]{:S(2)}, u32[]{:S(2)}) async-start(bf16[8,96,128]{2,1,0:T(8,128)(2,1)} %broadcast_in_dim.26), calls=%async_computation | async-start | bytes 393216 | tf_op jit(solution)/shard_map/all_to_all | solution.py:241
  11.7 1.4 %dynamic-slice_reduce_fusion.refs_0_ = s32[6]{0:T(128)} fusion(s32[16,6]{0,1:T(8,128)} %param.16, s32[]{:T(128)S(6)} %select_n.39), kind=kLoop, calls=%fused_computation.9 | loop fusion | bytes 52 | tf_op jit(solution)/shard_map/dynamic_slice | solution.py:263
  13.0 8.7 %spread.2.refs_3_.refs_0_ = bf16[16,2048,128]{2,1,0:T(8,128)(2,1)} custom-call(s32[4,4096]{1,0:T(4,128)} %bitcast.28, s32[1,4096]{1,0:T(1,128)} %bitcast.30, bf16[16,2,512,128]{3,2,1,0:T(8,128)(2,1)} %bitcast.20), custom_call_target="tpu_custom_call" | custom-call | flops 536870912 | bytes 10485760 | tf_op jit(solution)/shard_map/spread/pallas_call | solution.py:66
  21.7 0.0 all-to-all-done
  21.7 0.0 copy-start.5
  21.7 0.7 copy-done.5
  22.4 6.0 %pool.2 = (bf16[16,128,128]{2,1,0:T(8,128)(2,1)}, bf16[2048,128]{1,0:T(8,128)(2,1)}, bf16[128,2048]{1,0:T(8,128)(2,1)}) custom-call(s32[6]{0:T(128)} %dynamic-slice_reduce_fusion.refs_0_, bf16[1280,128]{1,0:T(8,128)(2,1)} %refs_1_.2, bf16[768,128]{1,0:T(8,128)(2,1)} %bitcast.26, bf16[16,2048,128]{2,1,0:T(8,128)(2,1)} %spread.2.refs_3_.refs_0_), custom_call_target="tpu_custom_call" | custom-call | flops 1073741824 | bytes 8388608 | tf_op jit(solution)/shard_map/pool/pallas_call | solution.py:126
  28.4 5.5 %all-to-all-start.1 = ((bf16[16,128,128]{2,1,0:T(8,128)(2,1)}), bf16[16,128,128]{2,1,0:T(8,128)(2,1)S(1)}, u32[]{:S(2)}, u32[]{:S(2)}) async-start(bf16[16,128,128]{2,1,0:T(8,128)(2,1)} %get-tuple-element.14), calls=%async_computation.1 | async-start | bytes 1048576 | tf_op jit(solution)/shard_map/all_to_all | solution.py:245
  34.0 8.6 %spread.3.refs_1_ = bf16[16,2048,128]{2,1,0:T(8,128)(2,1)} custom-call(s32[4,4096]{1,0:T(4,128)} %bitcast.29, s32[1,4096]{1,0:T(1,128)} %bitcast.31, bf16[16,2,512,128]{3,2,1,0:T(8,128)(2,1)} %bitcast.21), custom_call_target="tpu_custom_call" | custom-call | flops 536870912 | bytes 10485760 | tf_op jit(solution)/shard_map/spread/pallas_call | solution.py:66
  42.5 5.9 %pool.3 = bf16[16,128,128]{2,1,0:T(8,128)(2,1)} custom-call(bf16[128,2048]{1,0:T(8,128)(2,1)} %get-tuple-element.18.refs_0_, bf16[16,2048,128]{2,1,0:T(8,128)(2,1)} %spread.3.refs_1_), custom_call_target="tpu_custom_call" | custom-call | flops 1073741824 | bytes 8388608 | tf_op jit(solution)/shard_map/pool/pallas_call | solution.py:126
  48.4 0.0 copy-start.7
  48.4 0.0 all-to-all-done.1.refs_0_
  48.4 0.0 copy-start.2
  48.4 5.7 %all-to-all-start.3 = ((bf16[16,128,128]{2,1,0:T(8,128)(2,1)}), bf16[16,128,128]{2,1,0:T(8,128)(2,1)S(1)}, u32[]{:S(2)}, u32[]{:S(2)}) async-start(bf16[16,128,128]{2,1,0:T(8,128)(2,1)} %pool.3), calls=%async_computation.3 | async-start | bytes 1048576 | tf_op jit(solution)/shard_map/all_to_all | solution.py:245
  54.2 0.0 copy-done.2
  54.2 5.9 %layer.2 = (bf16[128,1024]{1,0:T(8,128)(2,1)}, bf16[16,128,128]{2,1,0:T(8,128)(2,1)}) custom-call(bf16[16,128,128]{2,1,0:T(8,128)(2,1)} %copy-done.2, bf16[2048,1024]{1,0:T(8,128)(2,1)} %refs_2_.3, bf16[256,1024]{1,0:T(8,128)(2,1)} %refs_3_.1), custom_call_target="tpu_custom_call" | custom-call | flops 1073741824 | bytes 786432 | tf_op jit(solution)/shard_map/layer/pallas_call | solution.py:185
  60.0 4.9 %all-to-all-done.3.refs_1_ = bf16[16,128,128]{2,1,0:T(8,128)(2,1)S(1)} async-done(((bf16[16,128,128]{2,1,0:T(8,128)(2,1)}), bf16[16,128,128]{2,1,0:T(8,128)(2,1)S(1)}, u32[]{:S(2)}, u32[]{:S(2)}) %all-to-all-start.3) | async-done | bytes 524320 | tf_op jit(solution)/shard_map/all_to_all | solution.py:245
  65.0 0.0 copy-start.4
  65.0 3.6 %all-to-all-start.2 = ((bf16[16,128,128]{2,1,0:T(8,128)(2,1)}), bf16[16,128,128]{2,1,0:T(8,128)(2,1)S(1)}, u32[]{:S(2)}, u32[]{:S(2)}) async-start(bf16[16,128,128]{2,1,0:T(8,128)(2,1)} %get-tuple-element.15), calls=%async_computation.2 | async-start | bytes 1048576 | tf_op jit(solution)/shard_map/all_to_all | solution.py:245
  68.6 0.0 copy-done.4
  68.6 6.0 %layer.3 = (bf16[256,1024]{1,0:T(8,128)(2,1)}, bf16[16,128,128]{2,1,0:T(8,128)(2,1)}) custom-call(bf16[128,1024]{1,0:T(8,128)(2,1)} %get-tuple-element.17.refs_0_, bf16[16,128,128]{2,1,0:T(8,128)(2,1)} %copy-done.4, bf16[2048,1024]{1,0:T(8,128)(2,1)} %refs_2_.3, bf16[256,1024]{1,0:T(8,128)(2,1)} %refs_3_.1), custom_call_target="tpu_custom_call" | custom-call | flops 1073741824 | bytes 786432 | tf_op jit(solution)/shard_map/layer/pallas_call | solution.py:185
  74.5 4.8 %all-to-all-done.2 = bf16[16,128,128]{2,1,0:T(8,128)(2,1)S(1)} async-done(((bf16[16,128,128]{2,1,0:T(8,128)(2,1)}), bf16[16,128,128]{2,1,0:T(8,128)(2,1)S(1)}, u32[]{:S(2)}, u32[]{:S(2)}) %all-to-all-start.2) | async-done | bytes 524320 | tf_op jit(solution)/shard_map/all_to_all | solution.py:245
  79.4 0.0 copy-start.1
  79.4 3.6 %all-to-all-start.4 = ((bf16[16,128,128]{2,1,0:T(8,128)(2,1)}), bf16[16,128,128]{2,1,0:T(8,128)(2,1)S(1)}, u32[]{:S(2)}, u32[]{:S(2)}) async-start(bf16[16,128,128]{2,1,0:T(8,128)(2,1)} %get-tuple-element.19), calls=%async_computation.4 | async-start | bytes 1048576 | tf_op jit(solution)/shard_map/all_to_all | solution.py:245
  82.9 0.0 copy-done.7
  83.0 0.0 copy-done.1
  83.0 8.4 %grad.2.refs_0_ = f32[2048,128]{1,0:T(8,128)} custom-call(bf16[16,2048,128]{2,1,0:T(8,128)(2,1)} %spread.2.refs_3_.refs_0_, bf16[2048,128]{1,0:T(8,128)(2,1)} %bitcast.23), custom_call_target="tpu_custom_call" | custom-call | flops 1073741824 | bytes 8388608 | tf_op jit(solution)/shard_map/grad/pallas_call | solution.py:221
  91.4 0.0 copy-start.6
  91.4 2.4 %all-to-all-done.4 = bf16[16,128,128]{2,1,0:T(8,128)(2,1)S(1)} async-done(((bf16[16,128,128]{2,1,0:T(8,128)(2,1)}), bf16[16,128,128]{2,1,0:T(8,128)(2,1)S(1)}, u32[]{:S(2)}, u32[]{:S(2)}) %all-to-all-start.4) | async-done | bytes 524320 | tf_op jit(solution)/shard_map/all_to_all | solution.py:245
  93.7 0.0 copy-start.3
  93.7 0.8 copy-done.3
  94.5 8.5 %grad.3 = bf16[2048,128]{1,0:T(8,128)(2,1)} custom-call(f32[2048,128]{1,0:T(8,128)} %grad.2.refs_0_, bf16[16,2048,128]{2,1,0:T(8,128)(2,1)} %spread.3.refs_1_, bf16[2048,128]{1,0:T(8,128)(2,1)} %bitcast.24), custom_call_target="tpu_custom_call" | custom-call | flops 1073741824 | bytes 8388608 | tf_op jit(solution)/shard_map/grad/pallas_call | solution.py:221
  103.0 7.8 %all-to-all-start.5 = ((bf16[8,256,128]{2,1,0:T(8,128)(2,1)}), bf16[8,256,128]{2,1,0:T(8,128)(2,1)S(1)}, u32[]{:S(2)}, u32[]{:S(2)}) async-start(bf16[8,256,128]{2,1,0:T(8,128)(2,1)} %bitcast.22), calls=%async_computation.5 | async-start | bytes 1048576 | tf_op jit(solution)/shard_map/all_to_all | solution.py:245
  110.9 0.8 dynamic-slice_reduce_fusion.1
  111.6 0.6 gather_fusion
  112.2 0.1 select_bitcast_fusion
  112.3 8.9 %all-to-all-done.5 = bf16[8,256,128]{2,1,0:T(8,128)(2,1)S(1)} async-done(((bf16[8,256,128]{2,1,0:T(8,128)(2,1)}), bf16[8,256,128]{2,1,0:T(8,128)(2,1)S(1)}, u32[]{:S(2)}, u32[]{:S(2)}) %all-to-all-start.5) | async-done | bytes 524320 | tf_op jit(solution)/shard_map/all_to_all | solution.py:245
  121.2 0.1 convert_reduce_fusion
  121.2 0.1 multiply_reduce_fusion
  121.3 0.0 copy-done.6
  121.3 0.7 add_divide_fusion
  122.0 0.9 subtract_convert_fusion
  122.9 0.1 broadcast_in_dim.29
  123.0 14.0 %all_to_all.35 = bf16[8,256,128]{2,1,0:T(8,128)(2,1)S(1)} all-to-all(bf16[8,256,128]{2,1,0:T(8,128)(2,1)S(1)} %broadcast_in_dim.29), channel_id=1, replica_groups=mesh['table'=16,'dp'=8] {'dp'}, dimensions={0} | all-to-all | bytes 1048576 | tf_op jit(solution)/shard_map/all_to_all | solution.py:241
  137.1 0.8 copy.15
  (4 shorter events, 0.0 us)
Async XLA Ops:
  0.6 3.3 %copy-start = (bf16[16,96,128]{2,1,0:T(8,128)(2,1)S(1)}, bf16[16,96,128]{2,1,0:T(8,128)(2,1)}, u32[]{:S(2)}) copy-start(bf16[16,96,128]{2,1,0:T(8,128)(2,1)} %param.13) | copy-start | bytes 1179652
  4.6 17.1 %all-to-all-start = ((bf16[8,96,128]{2,1,0:T(8,128)(2,1)}), bf16[8,96,128]{2,1,0:T(8,128)(2,1)S(1)}, u32[]{:S(2)}, u32[]{:S(2)}) async-start(bf16[8,96,128]{2,1,0:T(8,128)(2,1)} %broadcast_in_dim.26), calls=%async_computation | async-start | bytes 393216 | tf_op jit(solution)/shard_map/all_to_all | solution.py:241
  21.7 0.7 copy-start.5
  28.4 20.0 %all-to-all-start.1 = ((bf16[16,128,128]{2,1,0:T(8,128)(2,1)}), bf16[16,128,128]{2,1,0:T(8,128)(2,1)S(1)}, u32[]{:S(2)}, u32[]{:S(2)}) async-start(bf16[16,128,128]{2,1,0:T(8,128)(2,1)} %get-tuple-element.14), calls=%async_computation.1 | async-start | bytes 1048576 | tf_op jit(solution)/shard_map/all_to_all | solution.py:245
  48.4 34.5 %copy-start.7 = (s32[6]{0:T(128)S(1)}, s32[6]{0:T(128)}, u32[]{:S(2)}) copy-start(s32[6]{0:T(128)} %dynamic-slice_reduce_fusion.refs_0_) | copy-start | bytes 76
  48.4 5.7 %copy-start.2 = (bf16[16,128,128]{2,1,0:T(8,128)(2,1)}, bf16[16,128,128]{2,1,0:T(8,128)(2,1)S(1)}, u32[]{:S(2)}) copy-start(bf16[16,128,128]{2,1,0:T(8,128)(2,1)S(1)} %all-to-all-done.1.refs_0_) | copy-start | bytes 1572868
  48.4 16.6 %all-to-all-start.3 = ((bf16[16,128,128]{2,1,0:T(8,128)(2,1)}), bf16[16,128,128]{2,1,0:T(8,128)(2,1)S(1)}, u32[]{:S(2)}, u32[]{:S(2)}) async-start(bf16[16,128,128]{2,1,0:T(8,128)(2,1)} %pool.3), calls=%async_computation.3 | async-start | bytes 1048576 | tf_op jit(solution)/shard_map/all_to_all | solution.py:245
  65.0 3.6 %copy-start.4 = (bf16[16,128,128]{2,1,0:T(8,128)(2,1)}, bf16[16,128,128]{2,1,0:T(8,128)(2,1)S(1)}, u32[]{:S(2)}) copy-start(bf16[16,128,128]{2,1,0:T(8,128)(2,1)S(1)} %all-to-all-done.3.refs_1_) | copy-start | bytes 1572868
  65.0 14.4 %all-to-all-start.2 = ((bf16[16,128,128]{2,1,0:T(8,128)(2,1)}), bf16[16,128,128]{2,1,0:T(8,128)(2,1)S(1)}, u32[]{:S(2)}, u32[]{:S(2)}) async-start(bf16[16,128,128]{2,1,0:T(8,128)(2,1)} %get-tuple-element.15), calls=%async_computation.2 | async-start | bytes 1048576 | tf_op jit(solution)/shard_map/all_to_all | solution.py:245
  79.4 3.6 %copy-start.1 = (bf16[16,128,128]{2,1,0:T(8,128)(2,1)}, bf16[16,128,128]{2,1,0:T(8,128)(2,1)S(1)}, u32[]{:S(2)}) copy-start(bf16[16,128,128]{2,1,0:T(8,128)(2,1)S(1)} %all-to-all-done.2) | copy-start | bytes 1572868
  79.4 14.4 %all-to-all-start.4 = ((bf16[16,128,128]{2,1,0:T(8,128)(2,1)}), bf16[16,128,128]{2,1,0:T(8,128)(2,1)S(1)}, u32[]{:S(2)}, u32[]{:S(2)}) async-start(bf16[16,128,128]{2,1,0:T(8,128)(2,1)} %get-tuple-element.19), calls=%async_computation.4 | async-start | bytes 1048576 | tf_op jit(solution)/shard_map/all_to_all | solution.py:245
  91.4 30.0 %copy-start.6 = (f32[1280]{0:T(1024)S(1)}, f32[1280]{0:T(1024)}, u32[]{:S(2)}) copy-start(f32[1280]{0:T(1024)} %param.12) | copy-start | bytes 15364
  93.7 0.8 copy-start.3
  103.0 18.1 %all-to-all-start.5 = ((bf16[8,256,128]{2,1,0:T(8,128)(2,1)}), bf16[8,256,128]{2,1,0:T(8,128)(2,1)S(1)}, u32[]{:S(2)}, u32[]{:S(2)}) async-start(bf16[8,256,128]{2,1,0:T(8,128)(2,1)} %bitcast.22), calls=%async_computation.5 | async-start | bytes 1048576 | tf_op jit(solution)/shard_map/all_to_all | solution.py:245

commit v3 on v0

v3 whole, which is shorter than its diff:
```python
import functools

import jax
import jax.numpy as jnp
from jax import lax
from jax.experimental import pallas as pl
from jax.experimental.pallas import tpu as pltpu
from jax.sharding import PartitionSpec as P

E = 128
BLK = 128
R = 10
SLAB = 6
K = 4
NB = R + SLAB
TILE = 16
WIDE = K * BLK

learn_rate = 0.5
ada_epsilon = 1e-08

ANY = pl.BlockSpec(memory_space=pl.ANY)
HBM = pl.BlockSpec(memory_space=pltpu.HBM)
SMEM = pl.BlockSpec(memory_space=pltpu.SMEM)
VMEM = pl.BlockSpec(memory_space=pltpu.VMEM)


def fill_perm(perm_ref):
    row = lax.broadcasted_iota(jnp.int32, (WIDE, BLK), 0)
    lane = lax.broadcasted_iota(jnp.int32, (WIDE, BLK), 1)
    for k in range(K):
        perm_ref[k] = jnp.where(row == lane * K + k, 1.0, 0.0).astype(jnp.bfloat16)


def turn(window, at, perm_ref, part_ref):
    turned = jnp.concatenate([window[pl.ds(at + BLK * n, BLK), :].T for n in range(K)], axis=1)
    for k in range(0, K, 2):
        right = jnp.concatenate([perm_ref[k], perm_ref[k + 1]], axis=1)
        got = jnp.dot(turned, right, preferred_element_type=jnp.float32).astype(jnp.bfloat16)
        part_ref[k] = got[:, :BLK]
        part_ref[k + 1] = got[:, BLK:]


def place(block_ref, count_ref, base, part_ref, out_ref, at):
    blocks = block_ref[:, pl.ds(base, BLK)]
    counts = count_ref[:, pl.ds(base, BLK)]
    names = []
    for k in range(K):
        name = jnp.where(counts > k, blocks[k : k + 1, :], NB).astype(jnp.float32)
        names.append(jnp.broadcast_to(name, (TILE, BLK)).astype(jnp.bfloat16))
    for m in range(NB):
        hits = [names[k] == jnp.bfloat16(m) for k in range(K)]
        for s in range(0, BLK, TILE):
            value = jnp.zeros((TILE, BLK), jnp.bfloat16)
            for k in range(K):
                value = jnp.where(hits[k], part_ref[k, s : s + TILE, :], value)
            out_ref[at, m * BLK + s : m * BLK + s + TILE, :] = value


def fetches(source, base, target, sem, pieces):
    size = target.shape[0] // pieces

    def piece(n):
        return pltpu.make_async_copy(
            source.at[pl.ds(base + n * size, size)], target.at[pl.ds(n * size, size)], sem.at[n]
        )

    return piece


def pair_out(matrix, out_hbm, sem, pair):
    span = pl.ds(pl.multiple_of(pair * 2, 2), 2)
    return pltpu.make_async_copy(matrix.at[span], out_hbm.at[span], sem.at[pair])


def early_body(block_ref, count_ref, weight_hbm, out_hbm, window, perm_ref, even_ref, odd_ref, matrix, in_sem, out_sem):
    groups = matrix.shape[0]
    pairs = groups // 2
    fetch = fetches(weight_hbm, 0, window, in_sem, pairs)
    for n in range(pairs):
        fetch(n).start()
    fill_perm(perm_ref)

    def put(group, part_ref):
        place(block_ref, count_ref, pl.multiple_of(group * BLK, BLK), part_ref, matrix, group)

    fetch(0).wait()
    turn(window, 0, perm_ref, even_ref)

    def step(pair, carry):
        group = 2 * pair
        turn(window, pl.multiple_of((group + 1) * WIDE, WIDE), perm_ref, odd_ref)
        put(group, even_ref)

        @pl.when(pair + 1 < pairs)
        def _():
            fetch(pair + 1).wait()

        turn(window, pl.multiple_of(lax.rem(group + 2, groups) * WIDE, WIDE), perm_ref, even_ref)
        put(group + 1, odd_ref)
        pair_out(matrix, out_hbm, out_sem, pair).start()
        return carry

    lax.fori_loop(0, pairs, step, 0)
    for pair in range(pairs):
        pair_out(matrix, out_hbm, out_sem, pair).wait()


def build_scratch(groups):
    return [
        pltpu.VMEM((groups * WIDE, BLK), jnp.bfloat16),
        pltpu.VMEM((K, WIDE, BLK), jnp.bfloat16),
        pltpu.VMEM((K, BLK, BLK), jnp.bfloat16),
        pltpu.VMEM((K, BLK, BLK), jnp.bfloat16),
    ]


def early(blocks, counts, weights, groups):
    return pl.pallas_call(
        early_body,
        in_specs=[VMEM, VMEM, HBM],
        out_specs=ANY,
        out_shape=jax.ShapeDtypeStruct((groups, NB * BLK, BLK), jnp.bfloat16),
        scratch_shapes=build_scratch(groups)
        + [
            pltpu.VMEM((groups, NB * BLK, BLK), jnp.bfloat16),
            pltpu.SemaphoreType.DMA((groups // 2,)),
            pltpu.SemaphoreType.DMA((groups // 2,)),
        ],
        cost_estimate=pl.CostEstimate(
            flops=groups * BLK * NB * BLK * 256, bytes_accessed=groups * WIDE * BLK * 10, transcendentals=0
        ),
        name="early",
    )(blocks, counts, weights)


def pool_body(
    order_ref, block_ref, count_ref, own_ref, slab_ref, weight_hbm, early_hbm,
    out_hbm, matrix, share_ref,
    window, perm_ref, even_ref, odd_ref, table_ref, turned_ref, pooled, in_sem, before_sem, pool_sem,
):
    early_groups = early_hbm.shape[0]
    late_groups = matrix.shape[0] - early_groups
    pairs = late_groups // 2
    fetch = fetches(weight_hbm, early_groups * WIDE, window, in_sem, pairs)
    again = fetches(early_hbm, 0, matrix.at[pl.ds(0, early_groups)], before_sem, early_groups // 2)
    for n in range(max(pairs, early_groups // 2)):
        if n < pairs:
            fetch(n).start()
        if n < early_groups // 2:
            again(n).start()
    fill_perm(perm_ref)
    table_ref[0 : R * BLK, :] = own_ref[...]
    for j in range(SLAB):
        at = pl.multiple_of(order_ref[j] * BLK, BLK)
        table_ref[(R + j) * BLK : (R + j + 1) * BLK, :] = slab_ref[pl.ds(at, BLK), :]
    for m in range(NB):
        turned_ref[:, m * BLK : (m + 1) * BLK] = table_ref[m * BLK : (m + 1) * BLK, :].T
    share = share_ref.shape[0]
    share_ref[...] = table_ref[pl.ds(pl.multiple_of(lax.axis_index("dp") * share, share), share), :]

    def send(first, count):
        span = pl.ds(first * BLK, count * BLK)
        return pltpu.make_async_copy(pooled.at[span, :], out_hbm.at[span, :], pool_sem)

    def sums(at, count):
        right = jnp.concatenate([matrix[at + q] for q in range(count)], axis=1)
        got = jnp.dot(turned_ref[...], right, preferred_element_type=jnp.float32)
        pooled[pl.ds(pl.multiple_of(at * BLK, BLK), count * BLK), :] = got.T.astype(jnp.bfloat16)

    def put(group, part_ref):
        base = pl.multiple_of((early_groups + group) * BLK, BLK)
        place(block_ref, count_ref, base, part_ref, matrix, early_groups + group)

    fetch(0).wait()
    turn(window, 0, perm_ref, even_ref)

    def step(pair, carry):
        group = 2 * pair
        turn(window, pl.multiple_of((group + 1) * WIDE, WIDE), perm_ref, odd_ref)
        put(group, even_ref)

        @pl.when(pair + 1 < pairs)
        def _():
            fetch(pair + 1).wait()

        turn(window, pl.multiple_of(lax.rem(group + 2, late_groups) * WIDE, WIDE), perm_ref, even_ref)
        put(group + 1, odd_ref)
        return carry

    lax.fori_loop(0, pairs, step, 0)
    for n in range(early_groups // 2):
        again(n).wait()

    def rest(n, carry):
        sums(4 * n, 4)
        return carry

    half = matrix.shape[0] // 2
    lax.fori_loop(0, half // 4, rest, 0)
    send(0, half).start()
    lax.fori_loop(half // 4, half // 2, rest, 0)
    send(half, half).start()
    send(0, 2 * half).wait()


def pool(order, blocks, counts, own, slab, weights, before, share):
    bags = blocks.shape[1]
    groups = bags // BLK
    late = groups - before.shape[0]
    return pl.pallas_call(
        pool_body,
        in_specs=[SMEM, VMEM, VMEM, VMEM, VMEM, HBM, HBM],
        out_specs=[ANY, VMEM, VMEM],
        out_shape=[
            jax.ShapeDtypeStruct((bags, E), jnp.bfloat16),
            pltpu.VMEM((groups, NB * BLK, BLK), jnp.bfloat16),
            jax.ShapeDtypeStruct((share, E), jnp.bfloat16),
        ],
        scratch_shapes=build_scratch(late)
        + [
            pltpu.VMEM((NB * BLK, E), jnp.bfloat16),
            pltpu.VMEM((E, NB * BLK), jnp.bfloat16),
            pltpu.VMEM((bags, E), jnp.bfloat16),
            pltpu.SemaphoreType.DMA((late // 2,)),
            pltpu.SemaphoreType.DMA((before.shape[0] // 2,)),
            pltpu.SemaphoreType.DMA,
        ],
        cost_estimate=pl.CostEstimate(
            flops=2 * bags * NB * BLK * E, bytes_accessed=bags * NB * BLK * 2, transcendentals=0
        ),
        compiler_params=pltpu.CompilerParams(vmem_limit_bytes=44 << 20),
        name="pool",
    )(order, blocks, counts, own, slab, weights, before)


def layer_body(pair, fan_hbm, top_hbm, cot_hbm, hid_hbm, out_hbm, fan_ref, top_ref, cot_ref, hid_ref, out_ref, sum_ref, pre_ref, fan_sem, top_sem, cot_sem, out_sem):
    fan, rows, _ = fan_ref.shape
    wide = pair * E
    steps = fan // pair
    fetch_fan = fetches(fan_hbm, 0, fan_ref, fan_sem, steps)
    fetch_top = fetches(top_hbm, 0, top_ref, top_sem, steps)
    fetch_cot = pltpu.make_async_copy(cot_hbm, cot_ref, cot_sem)
    send_hid = pltpu.make_async_copy(hid_ref, hid_hbm, cot_sem)

    def send_out(p):
        span = pl.ds(p * pair, pair)
        return pltpu.make_async_copy(out_ref.at[span], out_hbm.at[span], out_sem)

    for p in range(steps):
        fetch_fan(p).start()
        fetch_top(p).start()
    fetch_cot.start()
    for p in range(steps):
        fetch_fan(p).wait()
        left = jnp.concatenate([fan_ref[p * pair + q] for q in range(pair)], axis=1)
        fetch_top(p).wait()
        part = jnp.dot(left, top_ref[p * wide : (p + 1) * wide, :], preferred_element_type=jnp.float32)
        if p == 0:
            sum_ref[...] = part
        else:
            sum_ref[...] += part
    fetch_cot.wait()
    preact = sum_ref[...]
    gate = jax.nn.sigmoid(preact)
    hid_ref[...] = (preact * gate).astype(jnp.bfloat16)
    send_hid.start()
    slope = gate * (1.0 + preact * (1.0 - gate))
    pre_ref[...] = (cot_ref[...].astype(jnp.float32) * slope).astype(jnp.bfloat16)
    for p in range(steps):
        back = lax.dot_general(
            pre_ref[...],
            top_ref[p * wide : (p + 1) * wide, :],
            (((1,), (1,)), ((), ())),
            preferred_element_type=jnp.float32,
        ).astype(jnp.bfloat16)
        for q in range(pair):
            out_ref[p * pair + q] = back[:, q * E : (q + 1) * E]
        send_out(p).start()
    send_hid.wait()
    pltpu.make_async_copy(out_ref, out_hbm, out_sem).wait()


def layer(fan, top_weight, cotangent, pair=2):
    tables, rows, _ = fan.shape
    hidden = top_weight.shape[1]
    steps = tables // pair
    return pl.pallas_call(
        functools.partial(layer_body, pair),
        in_specs=[ANY, HBM, HBM],
        out_specs=[HBM, ANY],
        out_shape=[
            jax.ShapeDtypeStruct((rows, hidden), jnp.bfloat16),
            jax.ShapeDtypeStruct((tables, rows, E), jnp.bfloat16),
        ],
        scratch_shapes=[
            pltpu.VMEM(fan.shape, jnp.bfloat16),
            pltpu.VMEM(top_weight.shape, jnp.bfloat16),
            pltpu.VMEM((rows, hidden), jnp.bfloat16),
            pltpu.VMEM((rows, hidden), jnp.bfloat16),
            pltpu.VMEM(fan.shape, jnp.bfloat16),
            pltpu.VMEM((rows, hidden), jnp.float32),
            pltpu.VMEM((rows, hidden), jnp.bfloat16),
            pltpu.SemaphoreType.DMA((steps,)),
            pltpu.SemaphoreType.DMA((steps,)),
            pltpu.SemaphoreType.DMA,
            pltpu.SemaphoreType.DMA,
        ],
        cost_estimate=pl.CostEstimate(
            flops=4 * rows * top_weight.size, bytes_accessed=rows * hidden * 6, transcendentals=rows * hidden
        ),
        compiler_params=pltpu.CompilerParams(vmem_limit_bytes=45 << 20),
        name="layer",
    )(fan, top_weight, cotangent)


def grad_body(tile, matrix, grad_ref, out_hbm, out_ref, sem):
    def send(n):
        span = pl.ds(pl.multiple_of(n * tile, tile), tile)
        return pltpu.make_async_copy(out_ref.at[span, :], out_hbm.at[span, :], sem)

    def rows(n, carry):
        span = pl.ds(pl.multiple_of(n * tile, tile), tile)
        left = jnp.concatenate([matrix[q, span, :] for q in range(matrix.shape[0])], axis=1)
        total = jnp.dot(left, grad_ref[...], preferred_element_type=jnp.float32)
        out_ref[span, :] = total.astype(jnp.bfloat16)
        send(n).start()
        return carry

    lax.fori_loop(0, NB * BLK // tile, rows, 0)
    pltpu.make_async_copy(out_ref, out_hbm, sem).wait()


def grad(matrix, pooled_grad, tile=512):
    return pl.pallas_call(
        functools.partial(grad_body, tile),
        in_specs=[VMEM, VMEM],
        out_specs=ANY,
        out_shape=jax.ShapeDtypeStruct((NB * BLK, E), jnp.bfloat16),
        scratch_shapes=[pltpu.VMEM((NB * BLK, E), jnp.bfloat16), pltpu.SemaphoreType.DMA],
        cost_estimate=pl.CostEstimate(
            flops=2 * pooled_grad.size * NB * BLK, bytes_accessed=pooled_grad.size * 4, transcendentals=0
        ),
        compiler_params=pltpu.CompilerParams(vmem_limit_bytes=8 << 20),
        name="grad",
    )(matrix, pooled_grad)


def pick_body(pair_ref, ids_ref, sect_ref, state_ref, accum_ref, copies_ref, order_ref, out_ref):
    partner = pair_ref[lax.axis_index("table")]
    for n in range(copies_ref.shape[0]):
        copies_ref[n] = sect_ref[partner]
    for j in range(SLAB):
        order_ref[j] = ids_ref[j, partner]
    count = out_ref.shape[0]
    for n in range(count):
        block = lax.axis_index("dp") * count + n
        own = accum_ref[pl.ds(jnp.minimum(block, R - 1), 1), :]
        fold = pl.multiple_of(ids_ref[jnp.maximum(block - R, 0), partner] * BLK, BLK)
        states = state_ref[:, pl.ds(fold, BLK)]
        mine = lax.broadcasted_iota(jnp.int32, states.shape, 0) == partner
        other = jnp.sum(jnp.where(mine, states, 0.0), axis=0, keepdims=True)
        out_ref[n : n + 1, :] = jnp.where(block < R, own, other)


def pick(fold_pairs, slab_ids, sectioned_rows, sectioned_accum, own_accum, parts):
    _, size, width = sectioned_rows.shape
    return pl.pallas_call(
        pick_body,
        in_specs=[SMEM, SMEM, VMEM, VMEM, VMEM],
        out_specs=[VMEM, SMEM, VMEM],
        out_shape=[
            jax.ShapeDtypeStruct((parts, size, width), jnp.bfloat16),
            jax.ShapeDtypeStruct((SLAB,), jnp.int32),
            jax.ShapeDtypeStruct((NB // parts, BLK), jnp.float32),
        ],
        name="pick",
    )(fold_pairs, slab_ids.T, sectioned_rows, sectioned_accum, own_accum.reshape(R, BLK))


def update_body(part_ref, row_ref, accum_ref, copies_ref, out_ref):
    for n in range(accum_ref.shape[0]):
        span = slice(n * BLK, (n + 1) * BLK)
        total = part_ref[0, span, :].astype(jnp.float32)
        for q in range(1, part_ref.shape[0]):
            total = total + part_ref[q, span, :].astype(jnp.float32)
        before = jnp.broadcast_to(accum_ref[n : n + 1, :], (BLK, BLK)).T
        accum = before + jnp.mean(total * total, axis=1, keepdims=True)
        out_ref[n : n + 1, :] = accum.T[0:1, :]
        step_size = learn_rate / (jnp.sqrt(accum) + ada_epsilon)
        rows = (row_ref[span, :].astype(jnp.float32) - step_size * total).astype(jnp.bfloat16)
        for q in range(copies_ref.shape[0]):
            copies_ref[q, span, :] = rows


def update(received, rows, accum):
    return pl.pallas_call(
        update_body,
        in_specs=[VMEM, VMEM, VMEM],
        out_specs=[VMEM, VMEM],
        out_shape=[
            jax.ShapeDtypeStruct(received.shape, jnp.bfloat16),
            jax.ShapeDtypeStruct(accum.shape, jnp.float32),
        ],
        name="update",
    )(received, rows, accum)


def swap(blocks, axis):
    return lax.all_to_all(blocks, axis, split_axis=0, concat_axis=0, tiled=True)


def shards(
    own_table,
    own_accum,
    sectioned_rows,
    sectioned_accum,
    fold_pairs,
    slab_ids,
    bag_blocks,
    bag_counts,
    bag_weights,
    top_weight,
    hidden_grad,
):
    tables = lax.axis_size("table")
    parts = lax.axis_size("dp")
    share = NB * BLK // parts
    bag_total = bag_blocks.shape[0]
    copies, order, accum = pick(fold_pairs, slab_ids, sectioned_rows, sectioned_accum, own_accum, parts)
    slab_rows = swap(copies, "dp").reshape(SLAB * BLK, E)
    blocks = bag_blocks[:, 0, :].T
    counts = bag_counts.reshape(1, bag_total)
    weights = bag_weights.reshape(bag_total * K, BLK)
    before = early(blocks, counts, weights, bag_total // (2 * BLK))
    pooled, matrix, rows = pool(order, blocks, counts, own_table, slab_rows, weights, before, share)
    fan = swap(pooled.reshape(tables, bag_total // tables, E), "table")
    hidden, back = layer(fan, top_weight, hidden_grad)
    row_grad = grad(matrix, swap(back, "table").reshape(bag_total, E))
    received = swap(row_grad.reshape(parts, share, E), "dp")
    copies, accum = update(received, rows, accum)
    new_table = swap(copies, "dp").reshape(NB * BLK, E)
    return (new_table, accum.reshape(share), hidden)


def solution(mesh):
    placed = (
        P("table", None),
        P("table"),
        P(None, "dp", None),
        P(),
        P(),
        P(),
        P("dp", "table", None),
        P("dp", "table"),
        P("dp", "table", None, None),
        P(),
        P(("dp", "table"), None),
    )
    return jax.shard_map(
        shards,
        mesh=mesh,
        in_specs=placed,
        out_specs=(P("table", None), P(("table", "dp")), P(("dp", "table"), None)),
        check_vma=False,
    )
```

time: 275 us -> 136 us (0.49)
  waiting for transfers between devices: 83.3 us -> 0.01 us
  other arithmetic: 46.1 us -> 0 us
  Pallas kernels: 0 us -> 39.9 us
  matrix products: 28.5 us -> 0 us
  between operations: 16.1 us -> 0.71 us
  local copies, waits for them, and re-layouts: 24.3 us -> 15.2 us
  starting transfers between devices: 0.04 us -> 7.05 us
  blocking collectives: 76.2 us -> 72.9 us
    psum x1 -> x0, waiting for transfers between devices: 83.2 us -> none  [shards(): lax.psum(row_grad.astype(jnp.bfloat16), 'dp').astype(jnp.float32)]
    pallas_call x0 -> x6, Pallas kernels: none -> 39.9 us  [the longest x1 13.5 us: pool(): pl.pallas_call(pool_body, in_specs=[SMEM, VMEM, VMEM, VMEM, VMEM, HBM, HB...]
    add x1 -> x0, other arithmetic: 39 us -> none  [shards(): bag_matrix + jnp.where(slot_hit[:, :, None], weights[:, slot_index, None,...]
    all_gather x1 -> x0, blocking collectives: 34.5 us -> none  [shards(): slab_rows = lax.all_gather(sectioned_piece, 'dp', axis=0, tiled=True)]
    all_to_all x2 -> x4, blocking collectives: 41.7 us -> 72.9 us  [swap(): return lax.all_to_all(blocks, axis, split_axis=0, concat_axis=0, tiled=True)]
    dot_general x4 -> x0, matrix products: 28.5 us -> none  [the longest x1 14.7 us: shards(): lax.dot_general(bag_matrix, pooled_grad, (((0,), (0,)), ((), ())), prefer...]
    all_to_all x0 -> x1, starting transfers between devices: none -> 7.05 us  [swap(): return lax.all_to_all(blocks, axis, split_axis=0, concat_axis=0, tiled=True)]
    and x4 -> x0, local copies, waits for them, and re-layouts: 5.67 us -> none  [shards(): (blocks[:, slot_index, None] == column) & (counts[:, None] > slot_index)]
  transfers between devices with their start and end apart: 1 -> 1, of which waited for: 1 -> 0; matrix products, arithmetic and copies ran while one was open for 1% -> 0% of each run, Pallas kernels for 0% -> 6%
where the time goes in v3:
time: 136 us
  blocking collectives  72.9 us (54%)
  Pallas kernels  39.9 us (29%)
  local copies, waits for them, and re-layouts  15.2 us (11%)
  starting transfers between devices  7.05 us (5%)
    all_to_all x4, blocking collectives, swap(): return lax.all_to_all(blocks, axis, split_axis=0, concat_axis=0, tiled=True)  72.9 us
    unnamed x11, local copies, waits for them, and re-layouts  15.2 us
    pallas_call x1, Pallas kernels, pool(): pl.pallas_call(pool_body, in_specs=[SMEM, VMEM, VMEM, VMEM, VMEM, HBM, HB...  13.5 us
    pallas_call x1, Pallas kernels, layer(): pl.pallas_call(functools.partial(layer_body, pair), in_specs=[ANY, HBM, H...  8.46 us
    pallas_call x1, Pallas kernels, early(): pl.pallas_call(early_body, in_specs=[VMEM, VMEM, HBM], out_specs=ANY, out...  8.38 us
    all_to_all x1, starting transfers between devices, swap(): return lax.all_to_all(blocks, axis, split_axis=0, concat_axis=0, tiled=True)  7.05 us
    pallas_call x1, Pallas kernels, grad(): pl.pallas_call(functools.partial(grad_body, tile), in_specs=[VMEM, VMEM],...  5.66 us
  transfers between devices with their start and end apart: 1, of which 0 were waited for; matrix products, arithmetic and copies ran while one was open for 0% of the time, Pallas kernels for 6%

profile of v3, /device:TPU:0, one launch (start us, length us, event | category | flops | bytes accessed | tf_op | source)
XLA Modules:
  0.0 135.6 jit_solution(5399407633535871495)
XLA Ops:
  0.6 1.8 %pick.1 = (bf16[8,96,128]{2,1,0:T(8,128)(2,1)}, s32[6]{0:T(128)}, f32[2,128]{1,0:T(2,128)}) custom-call(s32[16]{0:T(128)} %pair_ref.1, s32[6,16]{1,0:T(8,128)} %bitcast.25, bf16[16,96,128]{2,1,0:T(8,128)(2,1)} %sect_ref.1, f32[16,768]{1,0:T(8,128)} %state_ref.1, f32[10,128]{1,0:T(8,128)} %bitcast.24), custom_call_target="tpu_custom_call" | custom-call | tf_op jit(solution)/shard_map/pick/pallas_call | solution.py:368
  2.4 7.1 %all-to-all-start = ((bf16[8,96,128]{2,1,0:T(8,128)(2,1)}), bf16[8,96,128]{2,1,0:T(8,128)(2,1)S(1)}, u32[]{:S(2)}, u32[]{:S(2)}) async-start(bf16[8,96,128]{2,1,0:T(8,128)(2,1)} %get-tuple-element.14), calls=%async_computation | async-start | bytes 393216 | tf_op jit(solution)/shard_map/all_to_all | solution.py:410
  9.5 8.4 %early.1.early_hbm = bf16[16,2048,128]{2,1,0:T(8,128)(2,1)} custom-call(s32[4,4096]{1,0:T(4,128)} %bitcast.20, s32[1,4096]{1,0:T(1,128)} %bitcast.22, bf16[16384,128]{1,0:T(8,128)(2,1)} %bitcast.15), custom_call_target="tpu_custom_call" | custom-call | flops 1073741824 | bytes 10485760 | tf_op jit(solution)/shard_map/early/pallas_call | solution.py:119
  17.9 0.0 copy-start.3
  17.9 0.0 all-to-all-done
  17.9 0.0 copy-start.4
  17.9 0.7 copy-done.4
  18.6 13.5 %pool.1 = (bf16[4096,128]{1,0:T(8,128)(2,1)}, bf16[32,2048,128]{2,1,0:T(8,128)(2,1)S(1)}, bf16[256,128]{1,0:T(8,128)(2,1)}) custom-call(s32[6]{0:T(128)} %get-tuple-element.13.order_ref, s32[4,4096]{1,0:T(4,128)} %bitcast.21, s32[1,4096]{1,0:T(1,128)} %bitcast.23, bf16[1280,128]{1,0:T(8,128)(2,1)} %own_ref.1, bf16[768,128]{1,0:T(8,128)(2,1)} %bitcast.19, ...), custom_call_target="tpu_custom_call" | custom-call | flops 2147483648 | bytes 16777216 | tf_op jit(solution)/shard_map/pool/pallas_call | solution.py:211
  32.0 0.0 copy-start
  32.0 5.7 %copy-done = bf16[32,2048,128]{2,1,0:T(8,128)(2,1)} copy-done((bf16[32,2048,128]{2,1,0:T(8,128)(2,1)}, bf16[32,2048,128]{2,1,0:T(8,128)(2,1)S(1)}, u32[]{:S(2)}) %copy-start) | copy-done | bytes 16777240
  37.8 22.0 %all_to_all.25.fan_hbm = bf16[16,256,128]{2,1,0:T(8,128)(2,1)S(1)} all-to-all(bf16[16,256,128]{2,1,0:T(8,128)(2,1)} %bitcast.18), channel_id=1, replica_groups=mesh['table'=16,'dp'=8] {'table'}, dimensions={0} | all-to-all | bytes 2097152 | tf_op jit(solution)/shard_map/all_to_all | solution.py:410
  59.8 0.0 copy-done.3
  59.8 0.0 copy-start.2
  59.8 2.2 %copy-done.2 = bf16[2048,1024]{1,0:T(8,128)(2,1)S(1)} copy-done((bf16[2048,1024]{1,0:T(8,128)(2,1)S(1)}, bf16[2048,1024]{1,0:T(8,128)(2,1)}, u32[]{:S(2)}) %copy-start.2) | copy-done | bytes 4194328
  61.9 8.5 %layer.1 = (bf16[256,1024]{1,0:T(8,128)(2,1)}, bf16[16,256,128]{2,1,0:T(8,128)(2,1)S(1)}) custom-call(bf16[16,256,128]{2,1,0:T(8,128)(2,1)S(1)} %all_to_all.25.fan_hbm, bf16[2048,1024]{1,0:T(8,128)(2,1)S(1)} %copy-done.2, bf16[256,1024]{1,0:T(8,128)(2,1)S(1)} %copy-done.3), custom_call_target="tpu_custom_call" | custom-call | flops 2147483648 | bytes 1572864 | tf_op jit(solution)/shard_map/layer/pallas_call | solution.py:288
  70.4 19.1 %all_to_all.26 = bf16[16,256,128]{2,1,0:T(8,128)(2,1)S(1)} all-to-all(bf16[16,256,128]{2,1,0:T(8,128)(2,1)S(1)} %get-tuple-element.17), channel_id=1, replica_groups=mesh['table'=16,'dp'=8] {'table'}, dimensions={0} | all-to-all | bytes 2097152 | tf_op jit(solution)/shard_map/all_to_all | solution.py:410
  89.5 0.0 copy-start.1
  89.5 5.8 %copy-done.1 = bf16[32,2048,128]{2,1,0:T(8,128)(2,1)S(1)} copy-done((bf16[32,2048,128]{2,1,0:T(8,128)(2,1)S(1)}, bf16[32,2048,128]{2,1,0:T(8,128)(2,1)}, u32[]{:S(2)}) %copy-start.1) | copy-done | bytes 16777240
  95.3 5.7 %grad.1 = bf16[2048,128]{1,0:T(8,128)(2,1)S(1)} custom-call(bf16[32,2048,128]{2,1,0:T(8,128)(2,1)S(1)} %copy-done.1, bf16[4096,128]{1,0:T(8,128)(2,1)S(1)} %bitcast.13), custom_call_target="tpu_custom_call" | custom-call | flops 2147483648 | bytes 2097152 | tf_op jit(solution)/shard_map/grad/pallas_call | solution.py:335
  100.9 18.4 %all_to_all.27.part_ref = bf16[8,256,128]{2,1,0:T(8,128)(2,1)} all-to-all(bf16[8,256,128]{2,1,0:T(8,128)(2,1)S(1)} %bitcast.14), channel_id=1, replica_groups=mesh['table'=16,'dp'=8] {'dp'}, dimensions={0} | all-to-all | bytes 1048576 | tf_op jit(solution)/shard_map/all_to_all | solution.py:410
  119.3 2.1 %update.1 = (bf16[8,256,128]{2,1,0:T(8,128)(2,1)}, f32[2,128]{1,0:T(2,128)}) custom-call(bf16[8,256,128]{2,1,0:T(8,128)(2,1)} %all_to_all.27.part_ref, bf16[256,128]{1,0:T(8,128)(2,1)} %get-tuple-element.18.row_ref, f32[2,128]{1,0:T(2,128)} %get-tuple-element.19.accum_ref), custom_call_target="tpu_custom_call" | custom-call | tf_op jit(solution)/shard_map/update/pallas_call | solution.py:397
  121.4 13.4 %all_to_all.28 = bf16[8,256,128]{2,1,0:T(8,128)(2,1)S(1)} all-to-all(bf16[8,256,128]{2,1,0:T(8,128)(2,1)} %get-tuple-element.20), channel_id=1, replica_groups=mesh['table'=16,'dp'=8] {'dp'}, dimensions={0} | all-to-all | bytes 1048576 | tf_op jit(solution)/shard_map/all_to_all | solution.py:410
  134.9 0.8 copy.15
Async XLA Ops:
  2.4 15.5 %all-to-all-start = ((bf16[8,96,128]{2,1,0:T(8,128)(2,1)}), bf16[8,96,128]{2,1,0:T(8,128)(2,1)S(1)}, u32[]{:S(2)}, u32[]{:S(2)}) async-start(bf16[8,96,128]{2,1,0:T(8,128)(2,1)} %get-tuple-element.14), calls=%async_computation | async-start | bytes 393216 | tf_op jit(solution)/shard_map/all_to_all | solution.py:410
  17.9 41.9 %copy-start.3 = (bf16[256,1024]{1,0:T(8,128)(2,1)S(1)}, bf16[256,1024]{1,0:T(8,128)(2,1)}, u32[]{:S(2)}) copy-start(bf16[256,1024]{1,0:T(8,128)(2,1)} %cot_hbm.1) | copy-start | bytes 1572868
  17.9 0.7 copy-start.4
  32.0 5.7 %copy-start = (bf16[32,2048,128]{2,1,0:T(8,128)(2,1)}, bf16[32,2048,128]{2,1,0:T(8,128)(2,1)S(1)}, u32[]{:S(2)}) copy-start(bf16[32,2048,128]{2,1,0:T(8,128)(2,1)S(1)} %get-tuple-element.15.matrix) | copy-start | bytes 50331652
  59.8 2.2 %copy-start.2 = (bf16[2048,1024]{1,0:T(8,128)(2,1)S(1)}, bf16[2048,1024]{1,0:T(8,128)(2,1)}, u32[]{:S(2)}) copy-start(bf16[2048,1024]{1,0:T(8,128)(2,1)} %top_hbm.1) | copy-start | bytes 12582916
  89.5 5.8 %copy-start.1 = (bf16[32,2048,128]{2,1,0:T(8,128)(2,1)S(1)}, bf16[32,2048,128]{2,1,0:T(8,128)(2,1)}, u32[]{:S(2)}) copy-start(bf16[32,2048,128]{2,1,0:T(8,128)(2,1)} %copy-done) | copy-start | bytes 50331652

commit v4 on v3

--- a/solution.py
+++ b/solution.py
@@ -81,27 +81,26 @@
         fetch(n).start()
     fill_perm(perm_ref)
 
-    def put(group, part_ref):
-        place(block_ref, count_ref, pl.multiple_of(group * BLK, BLK), part_ref, matrix, group)
-
-    fetch(0).wait()
-    turn(window, 0, perm_ref, even_ref)
+    def put(pair):
+        for part_ref, group in ((even_ref, 2 * pair), (odd_ref, 2 * pair + 1)):
+            place(block_ref, count_ref, pl.multiple_of(group * BLK, BLK), part_ref, matrix, group)
+
+    def ready(pair):
+        turn(window, pl.multiple_of(2 * pair * WIDE, WIDE), perm_ref, even_ref)
+        turn(window, pl.multiple_of((2 * pair + 1) * WIDE, WIDE), perm_ref, odd_ref)
 
     def step(pair, carry):
-        group = 2 * pair
-        turn(window, pl.multiple_of((group + 1) * WIDE, WIDE), perm_ref, odd_ref)
-        put(group, even_ref)
-
-        @pl.when(pair + 1 < pairs)
-        def _():
-            fetch(pair + 1).wait()
-
-        turn(window, pl.multiple_of(lax.rem(group + 2, groups) * WIDE, WIDE), perm_ref, even_ref)
-        put(group + 1, odd_ref)
+        fetch(pair + 1).wait()
+        put(pair)
+        ready(pair + 1)
         pair_out(matrix, out_hbm, out_sem, pair).start()
         return carry
 
-    lax.fori_loop(0, pairs, step, 0)
+    fetch(0).wait()
+    ready(0)
+    lax.fori_loop(0, pairs - 1, step, 0)
+    put(pairs - 1)
+    pair_out(matrix, out_hbm, out_sem, pairs - 1).start()
     for pair in range(pairs):
         pair_out(matrix, out_hbm, out_sem, pair).wait()
 
@@ -136,19 +135,17 @@
 
 def pool_body(
     order_ref, block_ref, count_ref, own_ref, slab_ref, weight_hbm, early_hbm,
-    out_hbm, matrix, share_ref,
+    out_hbm, before, matrix, share_ref,
     window, perm_ref, even_ref, odd_ref, table_ref, turned_ref, pooled, in_sem, before_sem, pool_sem,
 ):
     early_groups = early_hbm.shape[0]
-    late_groups = matrix.shape[0] - early_groups
+    late_groups = matrix.shape[0]
     pairs = late_groups // 2
     fetch = fetches(weight_hbm, early_groups * WIDE, window, in_sem, pairs)
-    again = fetches(early_hbm, 0, matrix.at[pl.ds(0, early_groups)], before_sem, early_groups // 2)
-    for n in range(max(pairs, early_groups // 2)):
-        if n < pairs:
-            fetch(n).start()
-        if n < early_groups // 2:
-            again(n).start()
+    again = fetches(early_hbm, 0, before, before_sem, pairs)
+    for n in range(pairs):
+        fetch(n).start()
+        again(n).start()
     fill_perm(perm_ref)
     table_ref[0 : R * BLK, :] = own_ref[...]
     for j in range(SLAB):
@@ -163,45 +160,45 @@
         span = pl.ds(first * BLK, count * BLK)
         return pltpu.make_async_copy(pooled.at[span, :], out_hbm.at[span, :], pool_sem)
 
-    def sums(at, count):
-        right = jnp.concatenate([matrix[at + q] for q in range(count)], axis=1)
+    def sums(source, at, count, to):
+        right = jnp.concatenate([source[at + q] for q in range(count)], axis=1)
         got = jnp.dot(turned_ref[...], right, preferred_element_type=jnp.float32)
-        pooled[pl.ds(pl.multiple_of(at * BLK, BLK), count * BLK), :] = got.T.astype(jnp.bfloat16)
-
-    def put(group, part_ref):
-        base = pl.multiple_of((early_groups + group) * BLK, BLK)
-        place(block_ref, count_ref, base, part_ref, matrix, early_groups + group)
+        pooled[pl.ds(pl.multiple_of(to * BLK, BLK), count * BLK), :] = got.T.astype(jnp.bfloat16)
+
+    def put(pair):
+        for part_ref, group in ((even_ref, 2 * pair), (odd_ref, 2 * pair + 1)):
+            base = pl.multiple_of((early_groups + group) * BLK, BLK)
+            place(block_ref, count_ref, base, part_ref, matrix, group)
+
+    def ready(pair):
+        turn(window, pl.multiple_of(2 * pair * WIDE, WIDE), perm_ref, even_ref)
+        turn(window, pl.multiple_of((2 * pair + 1) * WIDE, WIDE), perm_ref, odd_ref)
+
+    per = early_groups // pairs
+
+    def step(pair, carry):
+        fetch(pair + 1).wait()
+        again(pair).wait()
+        put(pair)
+        sums(before, per * pair, per, per * pair)
+        ready(pair + 1)
+        return carry
 
     fetch(0).wait()
-    turn(window, 0, perm_ref, even_ref)
-
-    def step(pair, carry):
-        group = 2 * pair
-        turn(window, pl.multiple_of((group + 1) * WIDE, WIDE), perm_ref, odd_ref)
-        put(group, even_ref)
-
-        @pl.when(pair + 1 < pairs)
-        def _():
-            fetch(pair + 1).wait()
-
-        turn(window, pl.multiple_of(lax.rem(group + 2, late_groups) * WIDE, WIDE), perm_ref, even_ref)
-        put(group + 1, odd_ref)
+    ready(0)
+    lax.fori_loop(0, pairs - 1, step, 0)
+    again(pairs - 1).wait()
+    put(pairs - 1)
+    sums(before, per * (pairs - 1), per, per * (pairs - 1))
+    send(0, early_groups).start()
+
+    def rest(n, carry):
+        sums(matrix, 4 * n, 4, early_groups + 4 * n)
         return carry
 
-    lax.fori_loop(0, pairs, step, 0)
-    for n in range(early_groups // 2):
-        again(n).wait()
-
-    def rest(n, carry):
-        sums(4 * n, 4)
-        return carry
-
-    half = matrix.shape[0] // 2
-    lax.fori_loop(0, half // 4, rest, 0)
-    send(0, half).start()
-    lax.fori_loop(half // 4, half // 2, rest, 0)
-    send(half, half).start()
-    send(0, 2 * half).wait()
+    lax.fori_loop(0, late_groups // 4, rest, 0)
+    send(early_groups, late_groups).start()
+    send(0, early_groups + late_groups).wait()
 
 
 def pool(order, blocks, counts, own, slab, weights, before, share):
@@ -211,10 +208,11 @@
     return pl.pallas_call(
         pool_body,
         in_specs=[SMEM, VMEM, VMEM, VMEM, VMEM, HBM, HBM],
-        out_specs=[ANY, VMEM, VMEM],
+        out_specs=[ANY, VMEM, VMEM, VMEM],
         out_shape=[
             jax.ShapeDtypeStruct((bags, E), jnp.bfloat16),
-            pltpu.VMEM((groups, NB * BLK, BLK), jnp.bfloat16),
+            pltpu.VMEM(before.shape, jnp.bfloat16),
+            pltpu.VMEM((late, NB * BLK, BLK), jnp.bfloat16),
             jax.ShapeDtypeStruct((share, E), jnp.bfloat16),
         ],
         scratch_shapes=build_scratch(late)
@@ -223,44 +221,29 @@
             pltpu.VMEM((E, NB * BLK), jnp.bfloat16),
             pltpu.VMEM((bags, E), jnp.bfloat16),
             pltpu.SemaphoreType.DMA((late // 2,)),
-            pltpu.SemaphoreType.DMA((before.shape[0] // 2,)),
+            pltpu.SemaphoreType.DMA((late // 2,)),
             pltpu.SemaphoreType.DMA,
         ],
         cost_estimate=pl.CostEstimate(
             flops=2 * bags * NB * BLK * E, bytes_accessed=bags * NB * BLK * 2, transcendentals=0
         ),
-        compiler_params=pltpu.CompilerParams(vmem_limit_bytes=44 << 20),
+        compiler_params=pltpu.CompilerParams(vmem_limit_bytes=40 << 20),
         name="pool",
     )(order, blocks, counts, own, slab, weights, before)
 
 
-def layer_body(pair, fan_hbm, top_hbm, cot_hbm, hid_hbm, out_hbm, fan_ref, top_ref, cot_ref, hid_ref, out_ref, sum_ref, pre_ref, fan_sem, top_sem, cot_sem, out_sem):
+def layer_body(pair, fan_ref, top_ref, cot_ref, hid_hbm, out_ref, hid_ref, sum_ref, pre_ref, sem):
     fan, rows, _ = fan_ref.shape
     wide = pair * E
     steps = fan // pair
-    fetch_fan = fetches(fan_hbm, 0, fan_ref, fan_sem, steps)
-    fetch_top = fetches(top_hbm, 0, top_ref, top_sem, steps)
-    fetch_cot = pltpu.make_async_copy(cot_hbm, cot_ref, cot_sem)
-    send_hid = pltpu.make_async_copy(hid_ref, hid_hbm, cot_sem)
-
-    def send_out(p):
-        span = pl.ds(p * pair, pair)
-        return pltpu.make_async_copy(out_ref.at[span], out_hbm.at[span], out_sem)
-
+    send_hid = pltpu.make_async_copy(hid_ref, hid_hbm, sem)
     for p in range(steps):
-        fetch_fan(p).start()
-        fetch_top(p).start()
-    fetch_cot.start()
-    for p in range(steps):
-        fetch_fan(p).wait()
         left = jnp.concatenate([fan_ref[p * pair + q] for q in range(pair)], axis=1)
-        fetch_top(p).wait()
         part = jnp.dot(left, top_ref[p * wide : (p + 1) * wide, :], preferred_element_type=jnp.float32)
         if p == 0:
             sum_ref[...] = part
         else:
             sum_ref[...] += part
-    fetch_cot.wait()
     preact = sum_ref[...]
     gate = jax.nn.sigmoid(preact)
     hid_ref[...] = (preact * gate).astype(jnp.bfloat16)
@@ -276,53 +259,43 @@
         ).astype(jnp.bfloat16)
         for q in range(pair):
             out_ref[p * pair + q] = back[:, q * E : (q + 1) * E]
-        send_out(p).start()
     send_hid.wait()
-    pltpu.make_async_copy(out_ref, out_hbm, out_sem).wait()
-
-
-def layer(fan, top_weight, cotangent, pair=2):
+
+
+def layer(fan, top_weight, cotangent, pair=4):
     tables, rows, _ = fan.shape
     hidden = top_weight.shape[1]
-    steps = tables // pair
     return pl.pallas_call(
         functools.partial(layer_body, pair),
-        in_specs=[ANY, HBM, HBM],
-        out_specs=[HBM, ANY],
+        in_specs=[VMEM, VMEM, VMEM],
+        out_specs=[HBM, VMEM],
         out_shape=[
             jax.ShapeDtypeStruct((rows, hidden), jnp.bfloat16),
             jax.ShapeDtypeStruct((tables, rows, E), jnp.bfloat16),
         ],
         scratch_shapes=[
-            pltpu.VMEM(fan.shape, jnp.bfloat16),
-            pltpu.VMEM(top_weight.shape, jnp.bfloat16),
             pltpu.VMEM((rows, hidden), jnp.bfloat16),
-            pltpu.VMEM((rows, hidden), jnp.bfloat16),
-            pltpu.VMEM(fan.shape, jnp.bfloat16),
             pltpu.VMEM((rows, hidden), jnp.float32),
             pltpu.VMEM((rows, hidden), jnp.bfloat16),
-            pltpu.SemaphoreType.DMA((steps,)),
-            pltpu.SemaphoreType.DMA((steps,)),
-            pltpu.SemaphoreType.DMA,
             pltpu.SemaphoreType.DMA,
         ],
         cost_estimate=pl.CostEstimate(
             flops=4 * rows * top_weight.size, bytes_accessed=rows * hidden * 6, transcendentals=rows * hidden
         ),
-        compiler_params=pltpu.CompilerParams(vmem_limit_bytes=45 << 20),
+        compiler_params=pltpu.CompilerParams(vmem_limit_bytes=16 << 20),
         name="layer",
     )(fan, top_weight, cotangent)
 
 
-def grad_body(tile, matrix, grad_ref, out_hbm, out_ref, sem):
+def grad_body(tile, before, after, grad_ref, out_hbm, out_ref, sem):
     def send(n):
         span = pl.ds(pl.multiple_of(n * tile, tile), tile)
         return pltpu.make_async_copy(out_ref.at[span, :], out_hbm.at[span, :], sem)
 
     def rows(n, carry):
         span = pl.ds(pl.multiple_of(n * tile, tile), tile)
-        left = jnp.concatenate([matrix[q, span, :] for q in range(matrix.shape[0])], axis=1)
-        total = jnp.dot(left, grad_ref[...], preferred_element_type=jnp.float32)
+        left = [ref[q, span, :] for ref in (before, after) for q in range(ref.shape[0])]
+        total = jnp.dot(jnp.concatenate(left, axis=1), grad_ref[...], preferred_element_type=jnp.float32)
         out_ref[span, :] = total.astype(jnp.bfloat16)
         send(n).start()
         return carry
@@ -331,10 +304,10 @@
     pltpu.make_async_copy(out_ref, out_hbm, sem).wait()
 
 
-def grad(matrix, pooled_grad, tile=512):
+def grad(before, after, pooled_grad, tile=512):
     return pl.pallas_call(
         functools.partial(grad_body, tile),
-        in_specs=[VMEM, VMEM],
+        in_specs=[VMEM, VMEM, VMEM],
         out_specs=ANY,
         out_shape=jax.ShapeDtypeStruct((NB * BLK, E), jnp.bfloat16),
         scratch_shapes=[pltpu.VMEM((NB * BLK, E), jnp.bfloat16), pltpu.SemaphoreType.DMA],
@@ -343,7 +316,7 @@
         ),
         compiler_params=pltpu.CompilerParams(vmem_limit_bytes=8 << 20),
         name="grad",
-    )(matrix, pooled_grad)
+    )(before, after, pooled_grad)
 
 
 def pick_body(pair_ref, ids_ref, sect_ref, state_ref, accum_ref, copies_ref, order_ref, out_ref):
@@ -433,10 +406,10 @@
     counts = bag_counts.reshape(1, bag_total)
     weights = bag_weights.reshape(bag_total * K, BLK)
     before = early(blocks, counts, weights, bag_total // (2 * BLK))
-    pooled, matrix, rows = pool(order, blocks, counts, own_table, slab_rows, weights, before, share)
+    pooled, before, after, rows = pool(order, blocks, counts, own_table, slab_rows, weights, before, share)
     fan = swap(pooled.reshape(tables, bag_total // tables, E), "table")
     hidden, back = layer(fan, top_weight, hidden_grad)
-    row_grad = grad(matrix, swap(back, "table").reshape(bag_total, E))
+    row_grad = grad(before, after, swap(back, "table").reshape(bag_total, E))
     received = swap(row_grad.reshape(parts, share, E), "dp")
     copies, accum = update(received, rows, accum)
     new_table = swap(copies, "dp").reshape(NB * BLK, E)

time: 136 us -> 115 us (0.85)
  local copies, waits for them, and re-layouts: 15.2 us -> 1.48 us
  Pallas kernels: 39.9 us -> 32.2 us
    unnamed x11 -> x7, local copies, waits for them, and re-layouts: 15.2 us -> 1.48 us
    pallas_call x2, Pallas kernels: 14.1 us -> 8.82 us  [the longest x1 5.66 us: grad(): pl.pallas_call(functools.partial(grad_body, tile), in_specs=[VMEM, VMEM,...]
  transfers between devices with their start and end apart: 1 -> 1, of which waited for: 0 -> 1; matrix products, arithmetic and copies ran while one was open for 0% -> 0% of each run, Pallas kernels for 6% -> 6%
where the time goes in v4:
time: 115 us; the launch traced here: 114 us
  blocking collectives  71.9 us (63%)
  Pallas kernels  32.2 us (28%)
  starting transfers between devices  7.05 us (6%)
  local copies, waits for them, and re-layouts  1.48 us (1%)
    all_to_all x4, blocking collectives, swap(): return lax.all_to_all(blocks, axis, split_axis=0, concat_axis=0, tiled=True)  71.9 us
    pallas_call x1, Pallas kernels, pool(): pl.pallas_call(pool_body, in_specs=[SMEM, VMEM, VMEM, VMEM, VMEM, HBM, HB...  12.3 us
    pallas_call x1, Pallas kernels, early(): pl.pallas_call(early_body, in_specs=[VMEM, VMEM, HBM], out_specs=ANY, out...  7.18 us
    all_to_all x1, starting transfers between devices, swap(): return lax.all_to_all(blocks, axis, split_axis=0, concat_axis=0, tiled=True)  7.05 us
    pallas_call x1, Pallas kernels, grad(): pl.pallas_call(functools.partial(grad_body, tile), in_specs=[VMEM, VMEM,...  5.66 us
    pallas_call x1, Pallas kernels, layer(): pl.pallas_call(functools.partial(layer_body, pair), in_specs=[VMEM, VMEM,...  3.16 us
  transfers between devices with their start and end apart: 1, of which 1 were waited for; matrix products, arithmetic and copies ran while one was open for 0% of the time, Pallas kernels for 6%

profile of v4, /device:TPU:0, one launch (start us, length us, event | category | flops | bytes accessed | tf_op | source)
XLA Modules:
  0.0 114.3 jit_solution(4564447763019265715)
XLA Ops:
  0.6 1.8 %pick.1 = (bf16[8,96,128]{2,1,0:T(8,128)(2,1)}, s32[6]{0:T(128)}, f32[2,128]{1,0:T(2,128)}) custom-call(s32[16]{0:T(128)} %pair_ref.1, s32[6,16]{1,0:T(8,128)} %bitcast.25, bf16[16,96,128]{2,1,0:T(8,128)(2,1)} %sect_ref.1, f32[16,768]{1,0:T(8,128)} %state_ref.1, f32[10,128]{1,0:T(8,128)} %bitcast.24), custom_call_target="tpu_custom_call" | custom-call | tf_op jit(solution)/shard_map/pick/pallas_call | solution.py:341
  2.4 7.1 %all-to-all-start = ((bf16[8,96,128]{2,1,0:T(8,128)(2,1)}), bf16[8,96,128]{2,1,0:T(8,128)(2,1)S(1)}, u32[]{:S(2)}, u32[]{:S(2)}) async-start(bf16[8,96,128]{2,1,0:T(8,128)(2,1)} %get-tuple-element.15), calls=%async_computation | async-start | bytes 393216 | tf_op jit(solution)/shard_map/all_to_all | solution.py:383
  9.5 7.2 %early.1.early_hbm = bf16[16,2048,128]{2,1,0:T(8,128)(2,1)} custom-call(s32[4,4096]{1,0:T(4,128)} %bitcast.20, s32[1,4096]{1,0:T(1,128)} %bitcast.22, bf16[16384,128]{1,0:T(8,128)(2,1)} %bitcast.15), custom_call_target="tpu_custom_call" | custom-call | flops 1073741824 | bytes 10485760 | tf_op jit(solution)/shard_map/early/pallas_call | solution.py:118
  16.7 0.0 copy-start.1
  16.7 1.0 all-to-all-done
  17.6 0.0 copy-start.2
  17.6 0.0 copy-start
  17.6 0.7 copy-done.2
  18.3 12.3 %pool.1 = (bf16[4096,128]{1,0:T(8,128)(2,1)}, bf16[16,2048,128]{2,1,0:T(8,128)(2,1)S(1)}, bf16[16,2048,128]{2,1,0:T(8,128)(2,1)S(1)}, bf16[256,128]{1,0:T(8,128)(2,1)}) custom-call(s32[6]{0:T(128)} %get-tuple-element.14.order_ref, s32[4,4096]{1,0:T(4,128)} %bitcast.21, s32[1,4096]{1,0:T(1,128)} %bitcast.23, bf16[1280,128]{1,0:T(8,128)(2,1)} %own_ref.1, ...), custom_call_target="tpu_custom_call" | custom-call | flops 2147483648 | bytes 16777216 | tf_op jit(solution)/shard_map/pool/pallas_call | solution.py:208
  30.7 22.0 %all_to_all.25.fan_ref = bf16[16,256,128]{2,1,0:T(8,128)(2,1)S(1)} all-to-all(bf16[16,256,128]{2,1,0:T(8,128)(2,1)} %bitcast.18), channel_id=1, replica_groups=mesh['table'=16,'dp'=8] {'table'}, dimensions={0} | all-to-all | bytes 2097152 | tf_op jit(solution)/shard_map/all_to_all | solution.py:383
  52.7 0.0 copy-done.1
  52.7 0.0 copy-done
  52.7 3.2 %layer.1 = (bf16[256,1024]{1,0:T(8,128)(2,1)}, bf16[16,256,128]{2,1,0:T(8,128)(2,1)S(1)}) custom-call(bf16[16,256,128]{2,1,0:T(8,128)(2,1)S(1)} %all_to_all.25.fan_ref, bf16[2048,1024]{1,0:T(8,128)(2,1)S(1)} %copy-done, bf16[256,1024]{1,0:T(8,128)(2,1)S(1)} %copy-done.1), custom_call_target="tpu_custom_call" | custom-call | flops 2147483648 | bytes 1572864 | tf_op jit(solution)/shard_map/layer/pallas_call | solution.py:268
  55.9 19.1 %all_to_all.26 = bf16[16,256,128]{2,1,0:T(8,128)(2,1)S(1)} all-to-all(bf16[16,256,128]{2,1,0:T(8,128)(2,1)S(1)} %get-tuple-element.19), channel_id=1, replica_groups=mesh['table'=16,'dp'=8] {'table'}, dimensions={0} | all-to-all | bytes 2097152 | tf_op jit(solution)/shard_map/all_to_all | solution.py:383
  75.0 5.7 %grad.1 = bf16[2048,128]{1,0:T(8,128)(2,1)S(1)} custom-call(bf16[16,2048,128]{2,1,0:T(8,128)(2,1)S(1)} %get-tuple-element.16.before, bf16[16,2048,128]{2,1,0:T(8,128)(2,1)S(1)} %get-tuple-element.17.after, bf16[4096,128]{1,0:T(8,128)(2,1)S(1)} %bitcast.13), custom_call_target="tpu_custom_call" | custom-call | flops 2147483648 | bytes 2097152 | tf_op jit(solution)/shard_map/grad/pallas_call | solution.py:308
  80.6 17.4 %all_to_all.27.part_ref = bf16[8,256,128]{2,1,0:T(8,128)(2,1)} all-to-all(bf16[8,256,128]{2,1,0:T(8,128)(2,1)S(1)} %bitcast.14), channel_id=1, replica_groups=mesh['table'=16,'dp'=8] {'dp'}, dimensions={0} | all-to-all | bytes 1048576 | tf_op jit(solution)/shard_map/all_to_all | solution.py:383
  98.0 2.1 %update.1 = (bf16[8,256,128]{2,1,0:T(8,128)(2,1)}, f32[2,128]{1,0:T(2,128)}) custom-call(bf16[8,256,128]{2,1,0:T(8,128)(2,1)} %all_to_all.27.part_ref, bf16[256,128]{1,0:T(8,128)(2,1)} %get-tuple-element.20.row_ref, f32[2,128]{1,0:T(2,128)} %get-tuple-element.21.accum_ref), custom_call_target="tpu_custom_call" | custom-call | tf_op jit(solution)/shard_map/update/pallas_call | solution.py:370
  100.1 13.4 %all_to_all.28 = bf16[8,256,128]{2,1,0:T(8,128)(2,1)S(1)} all-to-all(bf16[8,256,128]{2,1,0:T(8,128)(2,1)} %get-tuple-element.22), channel_id=1, replica_groups=mesh['table'=16,'dp'=8] {'dp'}, dimensions={0} | all-to-all | bytes 1048576 | tf_op jit(solution)/shard_map/all_to_all | solution.py:383
  113.5 0.8 copy.15
Async XLA Ops:
  2.4 15.2 %all-to-all-start = ((bf16[8,96,128]{2,1,0:T(8,128)(2,1)}), bf16[8,96,128]{2,1,0:T(8,128)(2,1)S(1)}, u32[]{:S(2)}, u32[]{:S(2)}) async-start(bf16[8,96,128]{2,1,0:T(8,128)(2,1)} %get-tuple-element.15), calls=%async_computation | async-start | bytes 393216 | tf_op jit(solution)/shard_map/all_to_all | solution.py:383
  16.7 36.1 %copy-start.1 = (bf16[256,1024]{1,0:T(8,128)(2,1)S(1)}, bf16[256,1024]{1,0:T(8,128)(2,1)}, u32[]{:S(2)}) copy-start(bf16[256,1024]{1,0:T(8,128)(2,1)} %cot_ref.1) | copy-start | bytes 1572868
  17.6 0.7 copy-start.2
  17.6 35.1 %copy-start = (bf16[2048,1024]{1,0:T(8,128)(2,1)S(1)}, bf16[2048,1024]{1,0:T(8,128)(2,1)}, u32[]{:S(2)}) copy-start(bf16[2048,1024]{1,0:T(8,128)(2,1)} %top_ref.1) | copy-start | bytes 12582916

commit v5 on v4

--- a/solution.py
+++ b/solution.py
@@ -14,6 +14,7 @@
 K = 4
 NB = R + SLAB
 TILE = 16
+EACH = 4
 WIDE = K * BLK
 
 learn_rate = 0.5
@@ -32,16 +33,16 @@
         perm_ref[k] = jnp.where(row == lane * K + k, 1.0, 0.0).astype(jnp.bfloat16)
 
 
-def turn(window, at, perm_ref, part_ref):
+def turn(window, at, perm_ref, part_ref, group):
     turned = jnp.concatenate([window[pl.ds(at + BLK * n, BLK), :].T for n in range(K)], axis=1)
     for k in range(0, K, 2):
         right = jnp.concatenate([perm_ref[k], perm_ref[k + 1]], axis=1)
         got = jnp.dot(turned, right, preferred_element_type=jnp.float32).astype(jnp.bfloat16)
-        part_ref[k] = got[:, :BLK]
-        part_ref[k + 1] = got[:, BLK:]
-
-
-def place(block_ref, count_ref, base, part_ref, out_ref, at):
+        part_ref[group, k] = got[:, :BLK]
+        part_ref[group, k + 1] = got[:, BLK:]
+
+
+def place(block_ref, count_ref, base, part_ref, group, out_ref, at):
     blocks = block_ref[:, pl.ds(base, BLK)]
     counts = count_ref[:, pl.ds(base, BLK)]
     names = []
@@ -53,7 +54,7 @@
         for s in range(0, BLK, TILE):
             value = jnp.zeros((TILE, BLK), jnp.bfloat16)
             for k in range(K):
-                value = jnp.where(hits[k], part_ref[k, s : s + TILE, :], value)
+                value = jnp.where(hits[k], part_ref[group, k, s : s + TILE, :], value)
             out_ref[at, m * BLK + s : m * BLK + s + TILE, :] = value
 
 
@@ -68,85 +69,65 @@
     return piece
 
 
-def pair_out(matrix, out_hbm, sem, pair):
-    span = pl.ds(pl.multiple_of(pair * 2, 2), 2)
-    return pltpu.make_async_copy(matrix.at[span], out_hbm.at[span], sem.at[pair])
-
-
-def early_body(block_ref, count_ref, weight_hbm, out_hbm, window, perm_ref, even_ref, odd_ref, matrix, in_sem, out_sem):
-    groups = matrix.shape[0]
-    pairs = groups // 2
-    fetch = fetches(weight_hbm, 0, window, in_sem, pairs)
-    for n in range(pairs):
+def early_body(weight_hbm, out_hbm, window, perm_ref, part_ref, in_sem, out_sem):
+    groups = part_ref.shape[0]
+    pieces = groups // EACH
+    fetch = fetches(weight_hbm, 0, window, in_sem, pieces)
+
+    def send(piece):
+        span = pl.ds(pl.multiple_of(piece * EACH, EACH), EACH)
+        return pltpu.make_async_copy(part_ref.at[span], out_hbm.at[span], out_sem.at[piece])
+
+    for n in range(pieces):
         fetch(n).start()
     fill_perm(perm_ref)
 
-    def put(pair):
-        for part_ref, group in ((even_ref, 2 * pair), (odd_ref, 2 * pair + 1)):
-            place(block_ref, count_ref, pl.multiple_of(group * BLK, BLK), part_ref, matrix, group)
-
-    def ready(pair):
-        turn(window, pl.multiple_of(2 * pair * WIDE, WIDE), perm_ref, even_ref)
-        turn(window, pl.multiple_of((2 * pair + 1) * WIDE, WIDE), perm_ref, odd_ref)
-
-    def step(pair, carry):
-        fetch(pair + 1).wait()
-        put(pair)
-        ready(pair + 1)
-        pair_out(matrix, out_hbm, out_sem, pair).start()
+    def step(piece, carry):
+        fetch(piece).wait()
+        for g in range(EACH):
+            group = piece * EACH + g
+            turn(window, pl.multiple_of(group * WIDE, WIDE), perm_ref, part_ref, group)
+        send(piece).start()
         return carry
 
-    fetch(0).wait()
-    ready(0)
-    lax.fori_loop(0, pairs - 1, step, 0)
-    put(pairs - 1)
-    pair_out(matrix, out_hbm, out_sem, pairs - 1).start()
-    for pair in range(pairs):
-        pair_out(matrix, out_hbm, out_sem, pair).wait()
-
-
-def build_scratch(groups):
-    return [
-        pltpu.VMEM((groups * WIDE, BLK), jnp.bfloat16),
-        pltpu.VMEM((K, WIDE, BLK), jnp.bfloat16),
-        pltpu.VMEM((K, BLK, BLK), jnp.bfloat16),
-        pltpu.VMEM((K, BLK, BLK), jnp.bfloat16),
-    ]
-
-
-def early(blocks, counts, weights, groups):
+    lax.fori_loop(0, pieces, step, 0)
+    for n in range(pieces):
+        send(n).wait()
+
+
+def early(weights):
+    groups = weights.shape[0] // WIDE
+    parts = (groups, K, BLK, BLK)
+    sem = pltpu.SemaphoreType.DMA((groups // EACH,))
     return pl.pallas_call(
         early_body,
-        in_specs=[VMEM, VMEM, HBM],
+        in_specs=[HBM],
         out_specs=ANY,
-        out_shape=jax.ShapeDtypeStruct((groups, NB * BLK, BLK), jnp.bfloat16),
-        scratch_shapes=build_scratch(groups)
-        + [
-            pltpu.VMEM((groups, NB * BLK, BLK), jnp.bfloat16),
-            pltpu.SemaphoreType.DMA((groups // 2,)),
-            pltpu.SemaphoreType.DMA((groups // 2,)),
+        out_shape=jax.ShapeDtypeStruct(parts, jnp.bfloat16),
+        scratch_shapes=[
+            pltpu.VMEM(weights.shape, jnp.bfloat16),
+            pltpu.VMEM((K, WIDE, BLK), jnp.bfloat16),
+            pltpu.VMEM(parts, jnp.bfloat16),
+            sem,
+            sem,
         ],
         cost_estimate=pl.CostEstimate(
-            flops=groups * BLK * NB * BLK * 256, bytes_accessed=groups * WIDE * BLK * 10, transcendentals=0
+            flops=2 * weights.size * WIDE * 4, bytes_accessed=weights.size * 4, transcendentals=0
         ),
         name="early",
-    )(blocks, counts, weights)
+    )(weights)
 
 
 def pool_body(
-    order_ref, block_ref, count_ref, own_ref, slab_ref, weight_hbm, early_hbm,
-    out_hbm, before, matrix, share_ref,
-    window, perm_ref, even_ref, odd_ref, table_ref, turned_ref, pooled, in_sem, before_sem, pool_sem,
+    order_ref, block_ref, count_ref, own_ref, slab_ref, part_hbm,
+    out_hbm, first, second, share_ref,
+    part_ref, table_ref, turned_ref, pooled, part_sem, pool_sem,
 ):
-    early_groups = early_hbm.shape[0]
-    late_groups = matrix.shape[0]
-    pairs = late_groups // 2
-    fetch = fetches(weight_hbm, early_groups * WIDE, window, in_sem, pairs)
-    again = fetches(early_hbm, 0, before, before_sem, pairs)
-    for n in range(pairs):
+    half = first.shape[0]
+    pieces = 2 * half // EACH
+    fetch = fetches(part_hbm, 0, part_ref, part_sem, pieces)
+    for n in range(pieces):
         fetch(n).start()
-        again(n).start()
-    fill_perm(perm_ref)
     table_ref[0 : R * BLK, :] = own_ref[...]
     for j in range(SLAB):
         at = pl.multiple_of(order_ref[j] * BLK, BLK)
@@ -156,8 +137,8 @@
     share = share_ref.shape[0]
     share_ref[...] = table_ref[pl.ds(pl.multiple_of(lax.axis_index("dp") * share, share), share), :]
 
-    def send(first, count):
-        span = pl.ds(first * BLK, count * BLK)
+    def send(start, count):
+        span = pl.ds(start * BLK, count * BLK)
         return pltpu.make_async_copy(pooled.at[span, :], out_hbm.at[span, :], pool_sem)
 
     def sums(source, at, count, to):
@@ -165,63 +146,61 @@
         got = jnp.dot(turned_ref[...], right, preferred_element_type=jnp.float32)
         pooled[pl.ds(pl.multiple_of(to * BLK, BLK), count * BLK), :] = got.T.astype(jnp.bfloat16)
 
-    def put(pair):
-        for part_ref, group in ((even_ref, 2 * pair), (odd_ref, 2 * pair + 1)):
-            base = pl.multiple_of((early_groups + group) * BLK, BLK)
-            place(block_ref, count_ref, base, part_ref, matrix, group)
-
-    def ready(pair):
-        turn(window, pl.multiple_of(2 * pair * WIDE, WIDE), perm_ref, even_ref)
-        turn(window, pl.multiple_of((2 * pair + 1) * WIDE, WIDE), perm_ref, odd_ref)
-
-    per = early_groups // pairs
-
-    def step(pair, carry):
-        fetch(pair + 1).wait()
-        again(pair).wait()
-        put(pair)
-        sums(before, per * pair, per, per * pair)
-        ready(pair + 1)
+    def put(group, target, at):
+        place(block_ref, count_ref, pl.multiple_of(group * BLK, BLK), part_ref, group, target, at)
+
+    def fill(pair, carry):
+        @pl.when(lax.rem(pair, EACH // 2) == 0)
+        def _():
+            fetch(pair // (EACH // 2)).wait()
+
+        for g in range(2):
+            put(2 * pair + g, first, 2 * pair + g)
         return carry
 
-    fetch(0).wait()
-    ready(0)
-    lax.fori_loop(0, pairs - 1, step, 0)
-    again(pairs - 1).wait()
-    put(pairs - 1)
-    sums(before, per * (pairs - 1), per, per * (pairs - 1))
-    send(0, early_groups).start()
+    lax.fori_loop(0, half // 2, fill, 0)
+
+    def both(pair, carry):
+        @pl.when(lax.rem(pair, EACH // 2) == 0)
+        def _():
+            fetch(half // EACH + pair // (EACH // 2)).wait()
+
+        for g in range(2):
+            put(half + 2 * pair + g, second, 2 * pair + g)
+        sums(first, 2 * pair, 2, 2 * pair)
+        return carry
+
+    lax.fori_loop(0, half // 2, both, 0)
+    send(0, half).start()
 
     def rest(n, carry):
-        sums(matrix, 4 * n, 4, early_groups + 4 * n)
+        sums(second, 4 * n, 4, half + 4 * n)
         return carry
 
-    lax.fori_loop(0, late_groups // 4, rest, 0)
-    send(early_groups, late_groups).start()
-    send(0, early_groups + late_groups).wait()
-
-
-def pool(order, blocks, counts, own, slab, weights, before, share):
+    lax.fori_loop(0, half // 4, rest, 0)
+    send(half, half).start()
+    send(0, 2 * half).wait()
+
+
+def pool(order, blocks, counts, own, slab, parts, share):
     bags = blocks.shape[1]
-    groups = bags // BLK
-    late = groups - before.shape[0]
+    matrix = pltpu.VMEM((bags // (2 * BLK), NB * BLK, BLK), jnp.bfloat16)
     return pl.pallas_call(
         pool_body,
-        in_specs=[SMEM, VMEM, VMEM, VMEM, VMEM, HBM, HBM],
+        in_specs=[SMEM, VMEM, VMEM, VMEM, VMEM, HBM],
         out_specs=[ANY, VMEM, VMEM, VMEM],
         out_shape=[
             jax.ShapeDtypeStruct((bags, E), jnp.bfloat16),
-            pltpu.VMEM(before.shape, jnp.bfloat16),
-            pltpu.VMEM((late, NB * BLK, BLK), jnp.bfloat16),
+            matrix,
+            matrix,
             jax.ShapeDtypeStruct((share, E), jnp.bfloat16),
         ],
-        scratch_shapes=build_scratch(late)
-        + [
+        scratch_shapes=[
+            pltpu.VMEM(parts.shape, jnp.bfloat16),
             pltpu.VMEM((NB * BLK, E), jnp.bfloat16),
             pltpu.VMEM((E, NB * BLK), jnp.bfloat16),
             pltpu.VMEM((bags, E), jnp.bfloat16),
-            pltpu.SemaphoreType.DMA((late // 2,)),
-            pltpu.SemaphoreType.DMA((late // 2,)),
+            pltpu.SemaphoreType.DMA((parts.shape[0] // EACH,)),
             pltpu.SemaphoreType.DMA,
         ],
         cost_estimate=pl.CostEstimate(
@@ -229,7 +208,7 @@
         ),
         compiler_params=pltpu.CompilerParams(vmem_limit_bytes=40 << 20),
         name="pool",
-    )(order, blocks, counts, own, slab, weights, before)
+    )(order, blocks, counts, own, slab, parts)
 
 
 def layer_body(pair, fan_ref, top_ref, cot_ref, hid_hbm, out_ref, hid_ref, sum_ref, pre_ref, sem):
@@ -405,8 +384,8 @@
     blocks = bag_blocks[:, 0, :].T
     counts = bag_counts.reshape(1, bag_total)
     weights = bag_weights.reshape(bag_total * K, BLK)
-    before = early(blocks, counts, weights, bag_total // (2 * BLK))
-    pooled, before, after, rows = pool(order, blocks, counts, own_table, slab_rows, weights, before, share)
+    parts_turned = early(weights)
+    pooled, before, after, rows = pool(order, blocks, counts, own_table, slab_rows, parts_turned, share)
     fan = swap(pooled.reshape(tables, bag_total // tables, E), "table")
     hidden, back = layer(fan, top_weight, hidden_grad)
     row_grad = grad(before, after, swap(back, "table").reshape(bag_total, E))

time: 115 us -> 114 us (level)
  waiting for transfers between devices: 0.97 us -> 2.22 us
  blocking collectives: 71.9 us -> 70.7 us
    all_to_all x4, blocking collectives: 71.9 us -> 70.7 us  [swap(): return lax.all_to_all(blocks, axis, split_axis=0, concat_axis=0, tiled=True)]
    all_to_all x1, waiting for transfers between devices: 0.97 us -> 2.22 us  [swap(): return lax.all_to_all(blocks, axis, split_axis=0, concat_axis=0, tiled=True)]
  transfers between devices with their start and end apart: 1 -> 1, of which waited for: 1 -> 1; matrix products, arithmetic and copies ran while one was open for 0% -> 0% of each run, Pallas kernels for 6% -> 5%
where the time goes in v5:
time: 114 us; the launch traced here: 113 us
  blocking collectives  70.7 us (62%)
  Pallas kernels  31.2 us (27%)
  starting transfers between devices  7.05 us (6%)
  waiting for transfers between devices  2.22 us (2%)
  local copies, waits for them, and re-layouts  1.48 us (1%)
    all_to_all x4, blocking collectives, swap(): return lax.all_to_all(blocks, axis, split_axis=0, concat_axis=0, tiled=True)  70.7 us
    pallas_call x1, Pallas kernels, pool(): pl.pallas_call(pool_body, in_specs=[SMEM, VMEM, VMEM, VMEM, VMEM, HBM], o...  12.5 us
    all_to_all x1, starting transfers between devices, swap(): return lax.all_to_all(blocks, axis, split_axis=0, concat_axis=0, tiled=True)  7.05 us
    pallas_call x1, Pallas kernels, early(): pl.pallas_call(early_body, in_specs=[HBM], out_specs=ANY, out_shape=jax.S...  5.94 us
    pallas_call x1, Pallas kernels, grad(): pl.pallas_call(functools.partial(grad_body, tile), in_specs=[VMEM, VMEM,...  5.66 us
    pallas_call x1, Pallas kernels, layer(): pl.pallas_call(functools.partial(layer_body, pair), in_specs=[VMEM, VMEM,...  3.17 us
  transfers between devices with their start and end apart: 1, of which 1 were waited for; matrix products, arithmetic and copies ran while one was open for 0% of the time, Pallas kernels for 5%

profile of v5, /device:TPU:0, one launch (start us, length us, event | category | flops | bytes accessed | tf_op | source)
XLA Modules:
  0.0 113.3 jit_solution(17396559630990115156)
XLA Ops:
  0.6 1.8 %pick.1 = (bf16[8,96,128]{2,1,0:T(8,128)(2,1)}, s32[6]{0:T(128)}, f32[2,128]{1,0:T(2,128)}) custom-call(s32[16]{0:T(128)} %pair_ref.1, s32[6,16]{1,0:T(8,128)} %bitcast.19, bf16[16,96,128]{2,1,0:T(8,128)(2,1)} %sect_ref.1, f32[16,768]{1,0:T(8,128)} %state_ref.1, f32[10,128]{1,0:T(8,128)} %bitcast.18), custom_call_target="tpu_custom_call" | custom-call | tf_op jit(solution)/shard_map/pick/pallas_call | solution.py:320
  2.4 7.1 %all-to-all-start = ((bf16[8,96,128]{2,1,0:T(8,128)(2,1)}), bf16[8,96,128]{2,1,0:T(8,128)(2,1)S(1)}, u32[]{:S(2)}, u32[]{:S(2)}) async-start(bf16[8,96,128]{2,1,0:T(8,128)(2,1)} %get-tuple-element.15), calls=%async_computation | async-start | bytes 393216 | tf_op jit(solution)/shard_map/all_to_all | solution.py:362
  9.5 5.9 %early.1.part_hbm = bf16[32,4,128,128]{3,2,1,0:T(8,128)(2,1)} custom-call(bf16[16384,128]{1,0:T(8,128)(2,1)} %bitcast.20), custom_call_target="tpu_custom_call" | custom-call | flops 8589934592 | bytes 8388608 | tf_op jit(solution)/shard_map/early/pallas_call | solution.py:102
  15.4 2.2 %all-to-all-done = bf16[8,96,128]{2,1,0:T(8,128)(2,1)S(1)} async-done(((bf16[8,96,128]{2,1,0:T(8,128)(2,1)}), bf16[8,96,128]{2,1,0:T(8,128)(2,1)S(1)}, u32[]{:S(2)}, u32[]{:S(2)}) %all-to-all-start) | async-done | bytes 196640 | tf_op jit(solution)/shard_map/all_to_all | solution.py:362
  17.6 0.0 copy-start.2
  17.6 0.7 copy-done.2
  18.3 0.0 copy-start
  18.3 0.0 copy-start.1
  18.3 12.5 %pool.1 = (bf16[4096,128]{1,0:T(8,128)(2,1)}, bf16[16,2048,128]{2,1,0:T(8,128)(2,1)S(1)}, bf16[16,2048,128]{2,1,0:T(8,128)(2,1)S(1)}, bf16[256,128]{1,0:T(8,128)(2,1)}) custom-call(s32[6]{0:T(128)} %get-tuple-element.14.order_ref, s32[4,4096]{1,0:T(4,128)} %bitcast.21, s32[1,4096]{1,0:T(1,128)} %bitcast.22, bf16[1280,128]{1,0:T(8,128)(2,1)} %own_ref.1, ...), custom_call_target="tpu_custom_call" | custom-call | flops 2147483648 | bytes 16777216 | tf_op jit(solution)/shard_map/pool/pallas_call | solution.py:188
  30.9 22.0 %all_to_all.25.fan_ref = bf16[16,256,128]{2,1,0:T(8,128)(2,1)S(1)} all-to-all(bf16[16,256,128]{2,1,0:T(8,128)(2,1)} %bitcast.16), channel_id=1, replica_groups=mesh['table'=16,'dp'=8] {'table'}, dimensions={0} | all-to-all | bytes 2097152 | tf_op jit(solution)/shard_map/all_to_all | solution.py:362
  52.9 0.0 copy-done
  52.9 0.0 copy-done.1
  52.9 3.2 %layer.1 = (bf16[256,1024]{1,0:T(8,128)(2,1)}, bf16[16,256,128]{2,1,0:T(8,128)(2,1)S(1)}) custom-call(bf16[16,256,128]{2,1,0:T(8,128)(2,1)S(1)} %all_to_all.25.fan_ref, bf16[2048,1024]{1,0:T(8,128)(2,1)S(1)} %copy-done, bf16[256,1024]{1,0:T(8,128)(2,1)S(1)} %copy-done.1), custom_call_target="tpu_custom_call" | custom-call | flops 2147483648 | bytes 1572864 | tf_op jit(solution)/shard_map/layer/pallas_call | solution.py:247
  56.0 19.1 %all_to_all.26 = bf16[16,256,128]{2,1,0:T(8,128)(2,1)S(1)} all-to-all(bf16[16,256,128]{2,1,0:T(8,128)(2,1)S(1)} %get-tuple-element.19), channel_id=1, replica_groups=mesh['table'=16,'dp'=8] {'table'}, dimensions={0} | all-to-all | bytes 2097152 | tf_op jit(solution)/shard_map/all_to_all | solution.py:362
  75.1 5.7 %grad.1 = bf16[2048,128]{1,0:T(8,128)(2,1)S(1)} custom-call(bf16[16,2048,128]{2,1,0:T(8,128)(2,1)S(1)} %get-tuple-element.16.before, bf16[16,2048,128]{2,1,0:T(8,128)(2,1)S(1)} %get-tuple-element.17.after, bf16[4096,128]{1,0:T(8,128)(2,1)S(1)} %bitcast.13), custom_call_target="tpu_custom_call" | custom-call | flops 2147483648 | bytes 2097152 | tf_op jit(solution)/shard_map/grad/pallas_call | solution.py:287
  80.8 16.2 %all_to_all.27.part_ref = bf16[8,256,128]{2,1,0:T(8,128)(2,1)} all-to-all(bf16[8,256,128]{2,1,0:T(8,128)(2,1)S(1)} %bitcast.14), channel_id=1, replica_groups=mesh['table'=16,'dp'=8] {'dp'}, dimensions={0} | all-to-all | bytes 1048576 | tf_op jit(solution)/shard_map/all_to_all | solution.py:362
  96.9 2.1 %update.1 = (bf16[8,256,128]{2,1,0:T(8,128)(2,1)}, f32[2,128]{1,0:T(2,128)}) custom-call(bf16[8,256,128]{2,1,0:T(8,128)(2,1)} %all_to_all.27.part_ref, bf16[256,128]{1,0:T(8,128)(2,1)} %get-tuple-element.20.row_ref, f32[2,128]{1,0:T(2,128)} %get-tuple-element.21.accum_ref), custom_call_target="tpu_custom_call" | custom-call | tf_op jit(solution)/shard_map/update/pallas_call | solution.py:349
  99.1 13.4 %all_to_all.28 = bf16[8,256,128]{2,1,0:T(8,128)(2,1)S(1)} all-to-all(bf16[8,256,128]{2,1,0:T(8,128)(2,1)} %get-tuple-element.22), channel_id=1, replica_groups=mesh['table'=16,'dp'=8] {'dp'}, dimensions={0} | all-to-all | bytes 1048576 | tf_op jit(solution)/shard_map/all_to_all | solution.py:362
  112.5 0.8 copy.15
Async XLA Ops:
  2.4 15.2 %all-to-all-start = ((bf16[8,96,128]{2,1,0:T(8,128)(2,1)}), bf16[8,96,128]{2,1,0:T(8,128)(2,1)S(1)}, u32[]{:S(2)}, u32[]{:S(2)}) async-start(bf16[8,96,128]{2,1,0:T(8,128)(2,1)} %get-tuple-element.15), calls=%async_computation | async-start | bytes 393216 | tf_op jit(solution)/shard_map/all_to_all | solution.py:362
  17.6 0.7 copy-start.2
  18.3 34.6 %copy-start = (bf16[2048,1024]{1,0:T(8,128)(2,1)S(1)}, bf16[2048,1024]{1,0:T(8,128)(2,1)}, u32[]{:S(2)}) copy-start(bf16[2048,1024]{1,0:T(8,128)(2,1)} %top_ref.1) | copy-start | bytes 12582916
  18.3 34.6 %copy-start.1 = (bf16[256,1024]{1,0:T(8,128)(2,1)S(1)}, bf16[256,1024]{1,0:T(8,128)(2,1)}, u32[]{:S(2)}) copy-start(bf16[256,1024]{1,0:T(8,128)(2,1)} %cot_ref.1) | copy-start | bytes 1572868

commit v6 on v5

--- a/solution.py
+++ b/solution.py
@@ -119,16 +119,19 @@
 
 
 def pool_body(
-    order_ref, block_ref, count_ref, own_ref, slab_ref, part_hbm,
+    order_ref, block_ref, count_ref, own_ref, slab_hbm, part_hbm,
     out_hbm, first, second, share_ref,
-    part_ref, table_ref, turned_ref, pooled, part_sem, pool_sem,
+    part_ref, table_ref, turned_ref, pooled, slab_ref, part_sem, pool_sem,
 ):
     half = first.shape[0]
     pieces = 2 * half // EACH
     fetch = fetches(part_hbm, 0, part_ref, part_sem, pieces)
+    slab_copy = pltpu.make_async_copy(slab_hbm, slab_ref, pool_sem)
+    slab_copy.start()
     for n in range(pieces):
         fetch(n).start()
     table_ref[0 : R * BLK, :] = own_ref[...]
+    slab_copy.wait()
     for j in range(SLAB):
         at = pl.multiple_of(order_ref[j] * BLK, BLK)
         table_ref[(R + j) * BLK : (R + j + 1) * BLK, :] = slab_ref[pl.ds(at, BLK), :]
@@ -187,7 +190,7 @@
     matrix = pltpu.VMEM((bags // (2 * BLK), NB * BLK, BLK), jnp.bfloat16)
     return pl.pallas_call(
         pool_body,
-        in_specs=[SMEM, VMEM, VMEM, VMEM, VMEM, HBM],
+        in_specs=[SMEM, VMEM, VMEM, VMEM, ANY, HBM],
         out_specs=[ANY, VMEM, VMEM, VMEM],
         out_shape=[
             jax.ShapeDtypeStruct((bags, E), jnp.bfloat16),
@@ -200,13 +203,14 @@
             pltpu.VMEM((NB * BLK, E), jnp.bfloat16),
             pltpu.VMEM((E, NB * BLK), jnp.bfloat16),
             pltpu.VMEM((bags, E), jnp.bfloat16),
+            pltpu.VMEM(slab.shape, jnp.bfloat16),
             pltpu.SemaphoreType.DMA((parts.shape[0] // EACH,)),
             pltpu.SemaphoreType.DMA,
         ],
         cost_estimate=pl.CostEstimate(
             flops=2 * bags * NB * BLK * E, bytes_accessed=bags * NB * BLK * 2, transcendentals=0
         ),
-        compiler_params=pltpu.CompilerParams(vmem_limit_bytes=40 << 20),
+        compiler_params=pltpu.CompilerParams(vmem_limit_bytes=36 << 20),
         name="pool",
     )(order, blocks, counts, own, slab, parts)
 
@@ -298,10 +302,11 @@
     )(before, after, pooled_grad)
 
 
-def pick_body(pair_ref, ids_ref, sect_ref, state_ref, accum_ref, copies_ref, order_ref, out_ref):
+def pick_body(pair_ref, ids_ref, sect_hbm, state_ref, accum_ref, copies_ref, order_ref, out_ref, sem):
     partner = pair_ref[lax.axis_index("table")]
-    for n in range(copies_ref.shape[0]):
-        copies_ref[n] = sect_ref[partner]
+    copies = [pltpu.make_async_copy(sect_hbm.at[partner], copies_ref.at[n], sem.at[n]) for n in range(copies_ref.shape[0])]
+    for copy in copies:
+        copy.start()
     for j in range(SLAB):
         order_ref[j] = ids_ref[j, partner]
     count = out_ref.shape[0]
@@ -313,24 +318,27 @@
         mine = lax.broadcasted_iota(jnp.int32, states.shape, 0) == partner
         other = jnp.sum(jnp.where(mine, states, 0.0), axis=0, keepdims=True)
         out_ref[n : n + 1, :] = jnp.where(block < R, own, other)
+    for copy in copies:
+        copy.wait()
 
 
 def pick(fold_pairs, slab_ids, sectioned_rows, sectioned_accum, own_accum, parts):
     _, size, width = sectioned_rows.shape
     return pl.pallas_call(
         pick_body,
-        in_specs=[SMEM, SMEM, VMEM, VMEM, VMEM],
+        in_specs=[SMEM, SMEM, HBM, VMEM, VMEM],
         out_specs=[VMEM, SMEM, VMEM],
         out_shape=[
             jax.ShapeDtypeStruct((parts, size, width), jnp.bfloat16),
             jax.ShapeDtypeStruct((SLAB,), jnp.int32),
             jax.ShapeDtypeStruct((NB // parts, BLK), jnp.float32),
         ],
+        scratch_shapes=[pltpu.SemaphoreType.DMA((parts,))],
         name="pick",
     )(fold_pairs, slab_ids.T, sectioned_rows, sectioned_accum, own_accum.reshape(R, BLK))
 
 
-def update_body(part_ref, row_ref, accum_ref, copies_ref, out_ref):
+def update_body(part_ref, row_ref, accum_ref, new_ref, out_ref):
     for n in range(accum_ref.shape[0]):
         span = slice(n * BLK, (n + 1) * BLK)
         total = part_ref[0, span, :].astype(jnp.float32)
@@ -340,9 +348,7 @@
         accum = before + jnp.mean(total * total, axis=1, keepdims=True)
         out_ref[n : n + 1, :] = accum.T[0:1, :]
         step_size = learn_rate / (jnp.sqrt(accum) + ada_epsilon)
-        rows = (row_ref[span, :].astype(jnp.float32) - step_size * total).astype(jnp.bfloat16)
-        for q in range(copies_ref.shape[0]):
-            copies_ref[q, span, :] = rows
+        new_ref[span, :] = (row_ref[span, :].astype(jnp.float32) - step_size * total).astype(jnp.bfloat16)
 
 
 def update(received, rows, accum):
@@ -351,11 +357,43 @@
         in_specs=[VMEM, VMEM, VMEM],
         out_specs=[VMEM, VMEM],
         out_shape=[
-            jax.ShapeDtypeStruct(received.shape, jnp.bfloat16),
+            jax.ShapeDtypeStruct(rows.shape, jnp.bfloat16),
             jax.ShapeDtypeStruct(accum.shape, jnp.float32),
         ],
+        compiler_params=pltpu.CompilerParams(vmem_limit_bytes=8 << 20),
         name="update",
     )(received, rows, accum)
+
+
+def lay_body(near_ref, *refs):
+    out_ref = refs[-1]
+    size = near_ref.shape[0] // 2
+    me = lax.axis_index("dp")
+    across = out_ref.shape[0] // (2 * size)
+    for step, ref in enumerate((near_ref,) + refs[:-1]):
+        there = lax.rem(me // 2 + across - step, across) * 2
+        for half, side in enumerate((lax.rem(me, 2), 1 - lax.rem(me, 2))):
+            at = pl.multiple_of((there + side) * size, size)
+            out_ref[pl.ds(at, size), :] = ref[half * size : (half + 1) * size, :]
+
+
+def spread_rows(rows, parts):
+    def along(block, step):
+        return lax.ppermute(block, "dp", [(n, (n + 2 * step) % parts) for n in range(parts)])
+
+    other = lax.ppermute(rows, "dp", [(n, n ^ 1) for n in range(parts)])
+    near = jnp.concatenate([rows, other], axis=0)
+    across = parts // 2
+    order = [1, across - 1] + list(range(2, across - 1))
+    far = dict((step, along(near, step)) for step in order)
+    return pl.pallas_call(
+        lay_body,
+        in_specs=[VMEM] * across,
+        out_specs=VMEM,
+        out_shape=jax.ShapeDtypeStruct((parts * rows.shape[0], rows.shape[1]), rows.dtype),
+        compiler_params=pltpu.CompilerParams(vmem_limit_bytes=8 << 20),
+        name="lay",
+    )(near, *[far[step] for step in range(1, across)])
 
 
 def swap(blocks, axis):
@@ -390,8 +428,8 @@
     hidden, back = layer(fan, top_weight, hidden_grad)
     row_grad = grad(before, after, swap(back, "table").reshape(bag_total, E))
     received = swap(row_grad.reshape(parts, share, E), "dp")
-    copies, accum = update(received, rows, accum)
-    new_table = swap(copies, "dp").reshape(NB * BLK, E)
+    new_rows, accum = update(received, rows, accum)
+    new_table = spread_rows(new_rows, parts)
     return (new_table, accum.reshape(share), hidden)
 
 

time: 114 us -> 112 us (0.982)
  blocking collectives: 70.7 us -> 57 us
  waiting for transfers between devices: 2.22 us -> 12.8 us
  starting transfers between devices: 7.05 us -> 11.2 us
  local copies, waits for them, and re-layouts: 1.48 us -> 0.06 us
  Pallas kernels: 31.2 us -> 30 us
    all_to_all x4 -> x3, blocking collectives: 70.7 us -> 57 us  [swap(): return lax.all_to_all(blocks, axis, split_axis=0, concat_axis=0, tiled=True)]
    ppermute x0 -> x4, waiting for transfers between devices: none -> 10.7 us  [the longest x3 6.1 us: along(): lax.ppermute(block, 'dp', [(n, (n + 2 * step) % parts) for n in range(par...]
    ppermute x0 -> x4, starting transfers between devices: none -> 4.16 us  [the longest x3 2.95 us: along(): lax.ppermute(block, 'dp', [(n, (n + 2 * step) % parts) for n in range(par...]
    unnamed x7 -> x15, local copies, waits for them, and re-layouts: 1.48 us -> 0.04 us
    pallas_call x1, Pallas kernels: 2.12 us -> 0.82 us  [update(): pl.pallas_call(update_body, in_specs=[VMEM, VMEM, VMEM], out_specs=[VMEM,...]
    pallas_call x2 -> x3, Pallas kernels: 14.3 us -> 14.4 us  [the longest x1 10.7 us: pool(): pl.pallas_call(pool_body, in_specs=[SMEM, VMEM, VMEM, VMEM, ANY, HBM], ou...]
  transfers between devices with their start and end apart: 1 -> 5, of which waited for: 1 -> 5; matrix products, arithmetic and copies ran while one was open for 0% -> 0% of each run, Pallas kernels for 5% -> 5%
where the time goes in v6:
time: 112 us
  blocking collectives  57 us (51%)
  Pallas kernels  30 us (27%)
  waiting for transfers between devices  12.8 us (11%)
  starting transfers between devices  11.2 us (10%)
    all_to_all x3, blocking collectives, swap(): return lax.all_to_all(blocks, axis, split_axis=0, concat_axis=0, tiled=True)  57 us
    pallas_call x1, Pallas kernels, pool(): pl.pallas_call(pool_body, in_specs=[SMEM, VMEM, VMEM, VMEM, ANY, HBM], ou...  10.7 us
    all_to_all x1, starting transfers between devices, swap(): return lax.all_to_all(blocks, axis, split_axis=0, concat_axis=0, tiled=True)  7.05 us
    ppermute x3, waiting for transfers between devices, along(): lax.ppermute(block, 'dp', [(n, (n + 2 * step) % parts) for n in range(par...  6.1 us
    pallas_call x1, Pallas kernels, early(): pl.pallas_call(early_body, in_specs=[HBM], out_specs=ANY, out_shape=jax.S...  6.01 us
    pallas_call x1, Pallas kernels, grad(): pl.pallas_call(functools.partial(grad_body, tile), in_specs=[VMEM, VMEM,...  5.65 us
    ppermute x1, waiting for transfers between devices, spread_rows(): other = lax.ppermute(rows, 'dp', [(n, n ^ 1) for n in range(parts)])  4.56 us
    pallas_call x1, Pallas kernels, layer(): pl.pallas_call(functools.partial(layer_body, pair), in_specs=[VMEM, VMEM,...  3.16 us
  transfers between devices with their start and end apart: 5, of which 5 were waited for; matrix products, arithmetic and copies ran while one was open for 0% of the time, Pallas kernels for 5%

profile of v6, /device:TPU:0, one launch (start us, length us, event | category | flops | bytes accessed | tf_op | source)
XLA Modules:
  0.0 111.8 jit_solution(7572137680625298549)
XLA Ops:
  0.6 2.8 %pick.1 = (bf16[8,96,128]{2,1,0:T(8,128)(2,1)}, s32[6]{0:T(128)}, f32[2,128]{1,0:T(2,128)}) custom-call(s32[16]{0:T(128)} %pair_ref.1, s32[6,16]{1,0:T(8,128)} %bitcast.19, bf16[16,96,128]{2,1,0:T(8,128)(2,1)} %sect_hbm.1, f32[16,768]{1,0:T(8,128)} %state_ref.1, f32[10,128]{1,0:T(8,128)} %bitcast.18), custom_call_target="tpu_custom_call" | custom-call | tf_op jit(solution)/shard_map/pick/pallas_call | solution.py:327
  3.5 7.1 %all-to-all-start = ((bf16[8,96,128]{2,1,0:T(8,128)(2,1)}), bf16[8,96,128]{2,1,0:T(8,128)(2,1)S(1)}, u32[]{:S(2)}, u32[]{:S(2)}) async-start(bf16[8,96,128]{2,1,0:T(8,128)(2,1)} %get-tuple-element.15), calls=%async_computation | async-start | bytes 393216 | tf_op jit(solution)/shard_map/all_to_all | solution.py:400
  10.5 0.0 copy-start.3
  10.5 0.0 copy-start.4
  10.5 0.0 copy-start.5
  10.5 0.0 copy-start.6
  10.5 6.0 %early.1.part_hbm = bf16[32,4,128,128]{3,2,1,0:T(8,128)(2,1)} custom-call(bf16[16384,128]{1,0:T(8,128)(2,1)} %bitcast.20), custom_call_target="tpu_custom_call" | custom-call | flops 8589934592 | bytes 8388608 | tf_op jit(solution)/shard_map/early/pallas_call | solution.py:102
  16.6 2.1 %all-to-all-done = bf16[8,96,128]{2,1,0:T(8,128)(2,1)S(1)} async-done(((bf16[8,96,128]{2,1,0:T(8,128)(2,1)}), bf16[8,96,128]{2,1,0:T(8,128)(2,1)S(1)}, u32[]{:S(2)}, u32[]{:S(2)}) %all-to-all-start) | async-done | bytes 196640 | tf_op jit(solution)/shard_map/all_to_all | solution.py:400
  18.7 0.0 copy-done.3
  18.7 0.0 copy-done.4
  18.7 0.0 copy-done.5
  18.7 0.0 copy-done.6
  18.7 0.0 copy-start.1
  18.7 0.0 copy-start.2
  18.7 10.7 %pool.1 = (bf16[4096,128]{1,0:T(8,128)(2,1)S(1)}, bf16[16,2048,128]{2,1,0:T(8,128)(2,1)S(1)}, bf16[16,2048,128]{2,1,0:T(8,128)(2,1)S(1)}, bf16[256,128]{1,0:T(8,128)(2,1)S(1)}) custom-call(s32[6]{0:T(128)S(1)} %copy-done.6, s32[4,4096]{1,0:T(4,128)S(1)} %bitcast.16, s32[1,4096]{1,0:T(1,128)S(1)} %bitcast.17, bf16[1280,128]{1,0:T(8,128)(2,1)S(1)} %copy-done.3, ...), custom_call_target="tpu_custom_call" | custom-call | flops 2147483648 | bytes 16777216 | tf_op jit(solution)/shard_map/pool/pallas_call | solution.py:191
  29.5 21.8 %all_to_all.20.fan_ref = bf16[16,256,128]{2,1,0:T(8,128)(2,1)S(1)} all-to-all(bf16[16,256,128]{2,1,0:T(8,128)(2,1)S(1)} %bitcast.14), channel_id=1, replica_groups=mesh['table'=16,'dp'=8] {'table'}, dimensions={0} | all-to-all | bytes 2097152 | tf_op jit(solution)/shard_map/all_to_all | solution.py:400
  51.2 0.0 copy-done.1
  51.3 0.0 copy-done.2
  51.3 3.2 %layer.1 = (bf16[256,1024]{1,0:T(8,128)(2,1)}, bf16[16,256,128]{2,1,0:T(8,128)(2,1)S(1)}) custom-call(bf16[16,256,128]{2,1,0:T(8,128)(2,1)S(1)} %all_to_all.20.fan_ref, bf16[2048,1024]{1,0:T(8,128)(2,1)S(1)} %copy-done.1, bf16[256,1024]{1,0:T(8,128)(2,1)S(1)} %copy-done.2), custom_call_target="tpu_custom_call" | custom-call | flops 2147483648 | bytes 1572864 | tf_op jit(solution)/shard_map/layer/pallas_call | solution.py:251
  54.4 19.1 %all_to_all.21 = bf16[16,256,128]{2,1,0:T(8,128)(2,1)S(1)} all-to-all(bf16[16,256,128]{2,1,0:T(8,128)(2,1)S(1)} %get-tuple-element.19), channel_id=1, replica_groups=mesh['table'=16,'dp'=8] {'table'}, dimensions={0} | all-to-all | bytes 2097152 | tf_op jit(solution)/shard_map/all_to_all | solution.py:400
  73.5 0.0 copy-start
  73.5 5.7 %grad.1 = bf16[2048,128]{1,0:T(8,128)(2,1)S(1)} custom-call(bf16[16,2048,128]{2,1,0:T(8,128)(2,1)S(1)} %get-tuple-element.16.before, bf16[16,2048,128]{2,1,0:T(8,128)(2,1)S(1)} %get-tuple-element.17.after, bf16[4096,128]{1,0:T(8,128)(2,1)S(1)} %bitcast.12), custom_call_target="tpu_custom_call" | custom-call | flops 2147483648 | bytes 2097152 | tf_op jit(solution)/shard_map/grad/pallas_call | solution.py:291
  79.2 16.2 %all_to_all.22.part_ref = bf16[8,256,128]{2,1,0:T(8,128)(2,1)S(1)} all-to-all(bf16[8,256,128]{2,1,0:T(8,128)(2,1)S(1)} %bitcast.13), channel_id=1, replica_groups=mesh['table'=16,'dp'=8] {'dp'}, dimensions={0} | all-to-all | bytes 1048576 | tf_op jit(solution)/shard_map/all_to_all | solution.py:400
  95.3 0.0 copy-done
  95.3 0.8 update.1
  96.1 1.2 %collective-permute-start = (bf16[256,128]{1,0:T(8,128)(2,1)S(1)}, bf16[256,128]{1,0:T(8,128)(2,1)S(1)}, u32[]{:S(2)}, u32[]{:S(2)}) collective-permute-start(bf16[256,128]{1,0:T(8,128)(2,1)S(1)} %get-tuple-element.22), channel_id=1, source_target_pairs={{0,1},{1,0},{2,3},{3,2},{4,5},{5,4},{6,7},{7,6},{8,9},{9,8},{10,11... | collective-permute-start | bytes 196616 | tf_op jit(solution)/shard_map/ppermute | solution.py:384
  97.4 4.6 %collective-permute-done = bf16[256,128]{1,0:T(8,128)(2,1)S(1)} collective-permute-done((bf16[256,128]{1,0:T(8,128)(2,1)S(1)}, bf16[256,128]{1,0:T(8,128)(2,1)S(1)}, u32[]{:S(2)}, u32[]{:S(2)}) %collective-permute-start) | collective-permute-done | bytes 65568 | tf_op jit(solution)/shard_map/ppermute | solution.py:384
  101.9 1.2 %collective-permute-start.3 = (bf16[512,128]{1,0:T(8,128)(2,1)S(1)}, bf16[512,128]{1,0:T(8,128)(2,1)S(1)}, u32[]{:S(2)}, u32[]{:S(2)}) collective-permute-start(bf16[512,128]{1,0:T(8,128)(2,1)S(1)} %constant_dynamic-update-slice_fusion.near_ref), channel_id=1, source_target_pairs={{0,6},{1,7},{2,0},{3,1},{4,2},{5,3},{6,4},{7,5},{8,14},{9,15},{10,... | collective-permute-start | bytes 393224 | tf_op jit(solution)/shard_map/ppermute | solution.py:382
  103.1 1.2 %collective-permute-start.2 = (bf16[512,128]{1,0:T(8,128)(2,1)S(1)}, bf16[512,128]{1,0:T(8,128)(2,1)S(1)}, u32[]{:S(2)}, u32[]{:S(2)}) collective-permute-start(bf16[512,128]{1,0:T(8,128)(2,1)S(1)} %constant_dynamic-update-slice_fusion.near_ref), channel_id=1, source_target_pairs={{0,4},{1,5},{2,6},{3,7},{4,0},{5,1},{6,2},{7,3},{8,12},{9,13},{10,... | collective-permute-start | bytes 393224 | tf_op jit(solution)/shard_map/ppermute | solution.py:382
  104.3 0.6 collective-permute-start.1
  104.9 2.1 %collective-permute-done.3.refs_2_ = bf16[512,128]{1,0:T(8,128)(2,1)S(1)} collective-permute-done((bf16[512,128]{1,0:T(8,128)(2,1)S(1)}, bf16[512,128]{1,0:T(8,128)(2,1)S(1)}, u32[]{:S(2)}, u32[]{:S(2)}) %collective-permute-start.3) | collective-permute-done | bytes 131104 | tf_op jit(solution)/shard_map/ppermute | solution.py:382
  107.0 2.7 %collective-permute-done.2.refs_1_ = bf16[512,128]{1,0:T(8,128)(2,1)S(1)} collective-permute-done((bf16[512,128]{1,0:T(8,128)(2,1)S(1)}, bf16[512,128]{1,0:T(8,128)(2,1)S(1)}, u32[]{:S(2)}, u32[]{:S(2)}) %collective-permute-start.2) | collective-permute-done | bytes 131104 | tf_op jit(solution)/shard_map/ppermute | solution.py:382
  109.6 1.4 %collective-permute-done.1.refs_0_ = bf16[512,128]{1,0:T(8,128)(2,1)S(1)} collective-permute-done((bf16[512,128]{1,0:T(8,128)(2,1)S(1)}, bf16[512,128]{1,0:T(8,128)(2,1)S(1)}, u32[]{:S(2)}, u32[]{:S(2)}) %collective-permute-start.1) | collective-permute-done | bytes 131104 | tf_op jit(solution)/shard_map/ppermute | solution.py:382
  111.0 0.8 lay.1
  (2 shorter events, 0.0 us)
Async XLA Ops:
  3.5 15.2 %all-to-all-start = ((bf16[8,96,128]{2,1,0:T(8,128)(2,1)}), bf16[8,96,128]{2,1,0:T(8,128)(2,1)S(1)}, u32[]{:S(2)}, u32[]{:S(2)}) async-start(bf16[8,96,128]{2,1,0:T(8,128)(2,1)} %get-tuple-element.15), calls=%async_computation | async-start | bytes 393216 | tf_op jit(solution)/shard_map/all_to_all | solution.py:400
  10.5 8.2 %copy-start.3 = (bf16[1280,128]{1,0:T(8,128)(2,1)S(1)}, bf16[1280,128]{1,0:T(8,128)(2,1)}, u32[]{:S(2)}) copy-start(bf16[1280,128]{1,0:T(8,128)(2,1)} %own_ref.1) | copy-start | bytes 983044
  10.5 8.2 %copy-start.4 = (s32[4096,1,4]{0,2,1:T(4,128)S(1)}, s32[4096,1,4]{0,2,1:T(4,128)}, u32[]{:S(2)}) copy-start(s32[4096,1,4]{0,2,1:T(4,128)} %param.17) | copy-start | bytes 196612
  10.5 8.2 %copy-start.5 = (s32[4096,1]{0,1:T(1,128)S(1)}, s32[4096,1]{0,1:T(1,128)}, u32[]{:S(2)}) copy-start(s32[4096,1]{0,1:T(1,128)} %param.18) | copy-start | bytes 49156
  10.5 8.2 %copy-start.6 = (s32[6]{0:T(128)S(1)}, s32[6]{0:T(128)}, u32[]{:S(2)}) copy-start(s32[6]{0:T(128)} %get-tuple-element.14.order_ref) | copy-start | bytes 76
  18.7 32.5 %copy-start.1 = (bf16[2048,1024]{1,0:T(8,128)(2,1)S(1)}, bf16[2048,1024]{1,0:T(8,128)(2,1)}, u32[]{:S(2)}) copy-start(bf16[2048,1024]{1,0:T(8,128)(2,1)} %top_ref.1) | copy-start | bytes 12582916
  18.7 32.5 %copy-start.2 = (bf16[256,1024]{1,0:T(8,128)(2,1)S(1)}, bf16[256,1024]{1,0:T(8,128)(2,1)}, u32[]{:S(2)}) copy-start(bf16[256,1024]{1,0:T(8,128)(2,1)} %cot_ref.1) | copy-start | bytes 1572868
  73.5 21.8 %copy-start = (f32[2,128]{1,0:T(2,128)S(1)}, f32[2,128]{1,0:T(2,128)}, u32[]{:S(2)}) copy-start(f32[2,128]{1,0:T(2,128)} %get-tuple-element.21.accum_ref) | copy-start | bytes 3076
  96.1 5.8 %collective-permute-start = (bf16[256,128]{1,0:T(8,128)(2,1)S(1)}, bf16[256,128]{1,0:T(8,128)(2,1)S(1)}, u32[]{:S(2)}, u32[]{:S(2)}) collective-permute-start(bf16[256,128]{1,0:T(8,128)(2,1)S(1)} %get-tuple-element.22), channel_id=1, source_target_pairs={{0,1},{1,0},{2,3},{3,2},{4,5},{5,4},{6,7},{7,6},{8,9},{9,8},{10,11... | collective-permute-start | bytes 196616 | tf_op jit(solution)/shard_map/ppermute | solution.py:384
  101.9 5.0 %collective-permute-start.3 = (bf16[512,128]{1,0:T(8,128)(2,1)S(1)}, bf16[512,128]{1,0:T(8,128)(2,1)S(1)}, u32[]{:S(2)}, u32[]{:S(2)}) collective-permute-start(bf16[512,128]{1,0:T(8,128)(2,1)S(1)} %constant_dynamic-update-slice_fusion.near_ref), channel_id=1, source_target_pairs={{0,6},{1,7},{2,0},{3,1},{4,2},{5,3},{6,4},{7,5},{8,14},{9,15},{10,... | collective-permute-start | bytes 393224 | tf_op jit(solution)/shard_map/ppermute | solution.py:382
  103.1 6.5 %collective-permute-start.2 = (bf16[512,128]{1,0:T(8,128)(2,1)S(1)}, bf16[512,128]{1,0:T(8,128)(2,1)S(1)}, u32[]{:S(2)}, u32[]{:S(2)}) collective-permute-start(bf16[512,128]{1,0:T(8,128)(2,1)S(1)} %constant_dynamic-update-slice_fusion.near_ref), channel_id=1, source_target_pairs={{0,4},{1,5},{2,6},{3,7},{4,0},{5,1},{6,2},{7,3},{8,12},{9,13},{10,... | collective-permute-start | bytes 393224 | tf_op jit(solution)/shard_map/ppermute | solution.py:382
  104.3 6.7 %collective-permute-start.1 = (bf16[512,128]{1,0:T(8,128)(2,1)S(1)}, bf16[512,128]{1,0:T(8,128)(2,1)S(1)}, u32[]{:S(2)}, u32[]{:S(2)}) collective-permute-start(bf16[512,128]{1,0:T(8,128)(2,1)S(1)} %constant_dynamic-update-slice_fusion.near_ref), channel_id=1, source_target_pairs={{0,2},{1,3},{2,4},{3,5},{4,6},{5,7},{6,0},{7,1},{8,10},{9,11},{10,... | collective-permute-start | bytes 393224 | tf_op jit(solution)/shard_map/ppermute | solution.py:382

commit v7 on v6

--- a/solution.py
+++ b/solution.py
@@ -119,19 +119,16 @@
 
 
 def pool_body(
-    order_ref, block_ref, count_ref, own_ref, slab_hbm, part_hbm,
-    out_hbm, first, second, share_ref,
-    part_ref, table_ref, turned_ref, pooled, slab_ref, part_sem, pool_sem,
+    order_ref, block_ref, count_ref, own_ref, slab_ref, part_hbm,
+    pooled, first, second, share_ref,
+    part_ref, table_ref, turned_ref, part_sem,
 ):
     half = first.shape[0]
     pieces = 2 * half // EACH
     fetch = fetches(part_hbm, 0, part_ref, part_sem, pieces)
-    slab_copy = pltpu.make_async_copy(slab_hbm, slab_ref, pool_sem)
-    slab_copy.start()
     for n in range(pieces):
         fetch(n).start()
     table_ref[0 : R * BLK, :] = own_ref[...]
-    slab_copy.wait()
     for j in range(SLAB):
         at = pl.multiple_of(order_ref[j] * BLK, BLK)
         table_ref[(R + j) * BLK : (R + j + 1) * BLK, :] = slab_ref[pl.ds(at, BLK), :]
@@ -140,10 +137,6 @@
     share = share_ref.shape[0]
     share_ref[...] = table_ref[pl.ds(pl.multiple_of(lax.axis_index("dp") * share, share), share), :]
 
-    def send(start, count):
-        span = pl.ds(start * BLK, count * BLK)
-        return pltpu.make_async_copy(pooled.at[span, :], out_hbm.at[span, :], pool_sem)
-
     def sums(source, at, count, to):
         right = jnp.concatenate([source[at + q] for q in range(count)], axis=1)
         got = jnp.dot(turned_ref[...], right, preferred_element_type=jnp.float32)
@@ -174,15 +167,12 @@
         return carry
 
     lax.fori_loop(0, half // 2, both, 0)
-    send(0, half).start()
 
     def rest(n, carry):
         sums(second, 4 * n, 4, half + 4 * n)
         return carry
 
     lax.fori_loop(0, half // 4, rest, 0)
-    send(half, half).start()
-    send(0, 2 * half).wait()
 
 
 def pool(order, blocks, counts, own, slab, parts, share):
@@ -190,8 +180,8 @@
     matrix = pltpu.VMEM((bags // (2 * BLK), NB * BLK, BLK), jnp.bfloat16)
     return pl.pallas_call(
         pool_body,
-        in_specs=[SMEM, VMEM, VMEM, VMEM, ANY, HBM],
-        out_specs=[ANY, VMEM, VMEM, VMEM],
+        in_specs=[SMEM, VMEM, VMEM, VMEM, VMEM, HBM],
+        out_specs=[VMEM, VMEM, VMEM, VMEM],
         out_shape=[
             jax.ShapeDtypeStruct((bags, E), jnp.bfloat16),
             matrix,
@@ -202,10 +192,7 @@
             pltpu.VMEM(parts.shape, jnp.bfloat16),
             pltpu.VMEM((NB * BLK, E), jnp.bfloat16),
             pltpu.VMEM((E, NB * BLK), jnp.bfloat16),
-            pltpu.VMEM((bags, E), jnp.bfloat16),
-            pltpu.VMEM(slab.shape, jnp.bfloat16),
             pltpu.SemaphoreType.DMA((parts.shape[0] // EACH,)),
-            pltpu.SemaphoreType.DMA,
         ],
         cost_estimate=pl.CostEstimate(
             flops=2 * bags * NB * BLK * E, bytes_accessed=bags * NB * BLK * 2, transcendentals=0
@@ -270,30 +257,23 @@
     )(fan, top_weight, cotangent)
 
 
-def grad_body(tile, before, after, grad_ref, out_hbm, out_ref, sem):
-    def send(n):
-        span = pl.ds(pl.multiple_of(n * tile, tile), tile)
-        return pltpu.make_async_copy(out_ref.at[span, :], out_hbm.at[span, :], sem)
-
+def grad_body(tile, before, after, grad_ref, out_ref):
     def rows(n, carry):
         span = pl.ds(pl.multiple_of(n * tile, tile), tile)
         left = [ref[q, span, :] for ref in (before, after) for q in range(ref.shape[0])]
         total = jnp.dot(jnp.concatenate(left, axis=1), grad_ref[...], preferred_element_type=jnp.float32)
         out_ref[span, :] = total.astype(jnp.bfloat16)
-        send(n).start()
         return carry
 
     lax.fori_loop(0, NB * BLK // tile, rows, 0)
-    pltpu.make_async_copy(out_ref, out_hbm, sem).wait()
 
 
 def grad(before, after, pooled_grad, tile=512):
     return pl.pallas_call(
         functools.partial(grad_body, tile),
         in_specs=[VMEM, VMEM, VMEM],
-        out_specs=ANY,
+        out_specs=VMEM,
         out_shape=jax.ShapeDtypeStruct((NB * BLK, E), jnp.bfloat16),
-        scratch_shapes=[pltpu.VMEM((NB * BLK, E), jnp.bfloat16), pltpu.SemaphoreType.DMA],
         cost_estimate=pl.CostEstimate(
             flops=2 * pooled_grad.size * NB * BLK, bytes_accessed=pooled_grad.size * 4, transcendentals=0
         ),
@@ -302,11 +282,10 @@
     )(before, after, pooled_grad)
 
 
-def pick_body(pair_ref, ids_ref, sect_hbm, state_ref, accum_ref, copies_ref, order_ref, out_ref, sem):
+def pick_body(pair_ref, ids_ref, sect_ref, state_ref, accum_ref, copies_ref, order_ref, out_ref):
     partner = pair_ref[lax.axis_index("table")]
-    copies = [pltpu.make_async_copy(sect_hbm.at[partner], copies_ref.at[n], sem.at[n]) for n in range(copies_ref.shape[0])]
-    for copy in copies:
-        copy.start()
+    for n in range(copies_ref.shape[0]):
+        copies_ref[n] = sect_ref[partner]
     for j in range(SLAB):
         order_ref[j] = ids_ref[j, partner]
     count = out_ref.shape[0]
@@ -318,22 +297,19 @@
         mine = lax.broadcasted_iota(jnp.int32, states.shape, 0) == partner
         other = jnp.sum(jnp.where(mine, states, 0.0), axis=0, keepdims=True)
         out_ref[n : n + 1, :] = jnp.where(block < R, own, other)
-    for copy in copies:
-        copy.wait()
 
 
 def pick(fold_pairs, slab_ids, sectioned_rows, sectioned_accum, own_accum, parts):
     _, size, width = sectioned_rows.shape
     return pl.pallas_call(
         pick_body,
-        in_specs=[SMEM, SMEM, HBM, VMEM, VMEM],
+        in_specs=[SMEM, SMEM, VMEM, VMEM, VMEM],
         out_specs=[VMEM, SMEM, VMEM],
         out_shape=[
             jax.ShapeDtypeStruct((parts, size, width), jnp.bfloat16),
             jax.ShapeDtypeStruct((SLAB,), jnp.int32),
             jax.ShapeDtypeStruct((NB // parts, BLK), jnp.float32),
         ],
-        scratch_shapes=[pltpu.SemaphoreType.DMA((parts,))],
         name="pick",
     )(fold_pairs, slab_ids.T, sectioned_rows, sectioned_accum, own_accum.reshape(R, BLK))
 

time: 112 us -> 110 us (0.982)
  Pallas kernels: 30 us -> 28 us
    pallas_call x2, Pallas kernels: 13.6 us -> 12.2 us  [the longest x1 10.4 us: pool(): pl.pallas_call(pool_body, in_specs=[SMEM, VMEM, VMEM, VMEM, VMEM, HBM], o...]
where the time goes in v7:
time: 110 us
  blocking collectives  57 us (52%)
  Pallas kernels  28 us (25%)
  waiting for transfers between devices  12.8 us (12%)
  starting transfers between devices  11.2 us (10%)
    all_to_all x3, blocking collectives, swap(): return lax.all_to_all(blocks, axis, split_axis=0, concat_axis=0, tiled=True)  57 us
    pallas_call x1, Pallas kernels, pool(): pl.pallas_call(pool_body, in_specs=[SMEM, VMEM, VMEM, VMEM, VMEM, HBM], o...  10.4 us
    all_to_all x1, starting transfers between devices, swap(): return lax.all_to_all(blocks, axis, split_axis=0, concat_axis=0, tiled=True)  7.05 us
    ppermute x3, waiting for transfers between devices, along(): lax.ppermute(block, 'dp', [(n, (n + 2 * step) % parts) for n in range(par...  6.1 us
    pallas_call x1, Pallas kernels, early(): pl.pallas_call(early_body, in_specs=[HBM], out_specs=ANY, out_shape=jax.S...  6.01 us
    pallas_call x1, Pallas kernels, grad(): pl.pallas_call(functools.partial(grad_body, tile), in_specs=[VMEM, VMEM,...  4.98 us
    ppermute x1, waiting for transfers between devices, spread_rows(): other = lax.ppermute(rows, 'dp', [(n, n ^ 1) for n in range(parts)])  4.56 us
    pallas_call x1, Pallas kernels, layer(): pl.pallas_call(functools.partial(layer_body, pair), in_specs=[VMEM, VMEM,...  3.17 us
  transfers between devices with their start and end apart: 5, of which 5 were waited for; matrix products, arithmetic and copies ran while one was open for 0% of the time, Pallas kernels for 5%

profile of v7, /device:TPU:0, one launch (start us, length us, event | category | flops | bytes accessed | tf_op | source)
XLA Modules:
  0.0 109.8 jit_solution(13139676621013615207)
XLA Ops:
  0.6 1.8 %pick.1 = (bf16[8,96,128]{2,1,0:T(8,128)(2,1)}, s32[6]{0:T(128)}, f32[2,128]{1,0:T(2,128)}) custom-call(s32[16]{0:T(128)} %pair_ref.1, s32[6,16]{1,0:T(8,128)} %bitcast.19, bf16[16,96,128]{2,1,0:T(8,128)(2,1)} %sect_ref.1, f32[16,768]{1,0:T(8,128)} %state_ref.1, f32[10,128]{1,0:T(8,128)} %bitcast.18), custom_call_target="tpu_custom_call" | custom-call | tf_op jit(solution)/shard_map/pick/pallas_call | solution.py:304
  2.4 7.1 %all-to-all-start = ((bf16[8,96,128]{2,1,0:T(8,128)(2,1)}), bf16[8,96,128]{2,1,0:T(8,128)(2,1)S(1)}, u32[]{:S(2)}, u32[]{:S(2)}) async-start(bf16[8,96,128]{2,1,0:T(8,128)(2,1)} %get-tuple-element.15), calls=%async_computation | async-start | bytes 393216 | tf_op jit(solution)/shard_map/all_to_all | solution.py:376
  9.5 0.0 copy-start.3
  9.5 0.0 copy-start.4
  9.5 0.0 copy-start.5
  9.5 0.0 copy-start.6
  9.5 6.0 %early.1.part_hbm = bf16[32,4,128,128]{3,2,1,0:T(8,128)(2,1)} custom-call(bf16[16384,128]{1,0:T(8,128)(2,1)} %bitcast.20), custom_call_target="tpu_custom_call" | custom-call | flops 8589934592 | bytes 8388608 | tf_op jit(solution)/shard_map/early/pallas_call | solution.py:102
  15.5 2.1 %all-to-all-done = bf16[8,96,128]{2,1,0:T(8,128)(2,1)S(1)} async-done(((bf16[8,96,128]{2,1,0:T(8,128)(2,1)}), bf16[8,96,128]{2,1,0:T(8,128)(2,1)S(1)}, u32[]{:S(2)}, u32[]{:S(2)}) %all-to-all-start) | async-done | bytes 196640 | tf_op jit(solution)/shard_map/all_to_all | solution.py:376
  17.6 0.0 copy-done.3
  17.6 0.0 copy-done.4
  17.6 0.0 copy-done.5
  17.6 0.0 copy-done.6
  17.7 0.0 copy-start.1
  17.7 0.0 copy-start.2
  17.7 10.4 %pool.1 = (bf16[4096,128]{1,0:T(8,128)(2,1)S(1)}, bf16[16,2048,128]{2,1,0:T(8,128)(2,1)S(1)}, bf16[16,2048,128]{2,1,0:T(8,128)(2,1)S(1)}, bf16[256,128]{1,0:T(8,128)(2,1)S(1)}) custom-call(s32[6]{0:T(128)S(1)} %copy-done.6, s32[4,4096]{1,0:T(4,128)S(1)} %bitcast.16, s32[1,4096]{1,0:T(1,128)S(1)} %bitcast.17, bf16[1280,128]{1,0:T(8,128)(2,1)S(1)} %copy-done.3, ...), custom_call_target="tpu_custom_call" | custom-call | flops 2147483648 | bytes 16777216 | tf_op jit(solution)/shard_map/pool/pallas_call | solution.py:181
  28.1 21.8 %all_to_all.20.fan_ref = bf16[16,256,128]{2,1,0:T(8,128)(2,1)S(1)} all-to-all(bf16[16,256,128]{2,1,0:T(8,128)(2,1)S(1)} %bitcast.14), channel_id=1, replica_groups=mesh['table'=16,'dp'=8] {'table'}, dimensions={0} | all-to-all | bytes 2097152 | tf_op jit(solution)/shard_map/all_to_all | solution.py:376
  49.9 0.0 copy-done.1
  49.9 0.0 copy-done.2
  49.9 3.2 %layer.1 = (bf16[256,1024]{1,0:T(8,128)(2,1)}, bf16[16,256,128]{2,1,0:T(8,128)(2,1)S(1)}) custom-call(bf16[16,256,128]{2,1,0:T(8,128)(2,1)S(1)} %all_to_all.20.fan_ref, bf16[2048,1024]{1,0:T(8,128)(2,1)S(1)} %copy-done.1, bf16[256,1024]{1,0:T(8,128)(2,1)S(1)} %copy-done.2), custom_call_target="tpu_custom_call" | custom-call | flops 2147483648 | bytes 1572864 | tf_op jit(solution)/shard_map/layer/pallas_call | solution.py:238
  53.0 19.1 %all_to_all.21 = bf16[16,256,128]{2,1,0:T(8,128)(2,1)S(1)} all-to-all(bf16[16,256,128]{2,1,0:T(8,128)(2,1)S(1)} %get-tuple-element.19), channel_id=1, replica_groups=mesh['table'=16,'dp'=8] {'table'}, dimensions={0} | all-to-all | bytes 2097152 | tf_op jit(solution)/shard_map/all_to_all | solution.py:376
  72.1 0.0 copy-start
  72.1 5.0 %grad.1 = bf16[2048,128]{1,0:T(8,128)(2,1)S(1)} custom-call(bf16[16,2048,128]{2,1,0:T(8,128)(2,1)S(1)} %get-tuple-element.16.before, bf16[16,2048,128]{2,1,0:T(8,128)(2,1)S(1)} %get-tuple-element.17.after, bf16[4096,128]{1,0:T(8,128)(2,1)S(1)} %bitcast.12), custom_call_target="tpu_custom_call" | custom-call | flops 2147483648 | bytes 2097152 | tf_op jit(solution)/shard_map/grad/pallas_call | solution.py:272
  77.1 16.2 %all_to_all.22.part_ref = bf16[8,256,128]{2,1,0:T(8,128)(2,1)S(1)} all-to-all(bf16[8,256,128]{2,1,0:T(8,128)(2,1)S(1)} %bitcast.13), channel_id=1, replica_groups=mesh['table'=16,'dp'=8] {'dp'}, dimensions={0} | all-to-all | bytes 1048576 | tf_op jit(solution)/shard_map/all_to_all | solution.py:376
  93.3 0.0 copy-done
  93.3 0.8 update.1
  94.1 1.2 %collective-permute-start = (bf16[256,128]{1,0:T(8,128)(2,1)S(1)}, bf16[256,128]{1,0:T(8,128)(2,1)S(1)}, u32[]{:S(2)}, u32[]{:S(2)}) collective-permute-start(bf16[256,128]{1,0:T(8,128)(2,1)S(1)} %get-tuple-element.22), channel_id=1, source_target_pairs={{0,1},{1,0},{2,3},{3,2},{4,5},{5,4},{6,7},{7,6},{8,9},{9,8},{10,11... | collective-permute-start | bytes 196616 | tf_op jit(solution)/shard_map/ppermute | solution.py:360
  95.3 4.6 %collective-permute-done = bf16[256,128]{1,0:T(8,128)(2,1)S(1)} collective-permute-done((bf16[256,128]{1,0:T(8,128)(2,1)S(1)}, bf16[256,128]{1,0:T(8,128)(2,1)S(1)}, u32[]{:S(2)}, u32[]{:S(2)}) %collective-permute-start) | collective-permute-done | bytes 65568 | tf_op jit(solution)/shard_map/ppermute | solution.py:360
  99.9 1.2 %collective-permute-start.3 = (bf16[512,128]{1,0:T(8,128)(2,1)S(1)}, bf16[512,128]{1,0:T(8,128)(2,1)S(1)}, u32[]{:S(2)}, u32[]{:S(2)}) collective-permute-start(bf16[512,128]{1,0:T(8,128)(2,1)S(1)} %constant_dynamic-update-slice_fusion.near_ref), channel_id=1, source_target_pairs={{0,6},{1,7},{2,0},{3,1},{4,2},{5,3},{6,4},{7,5},{8,14},{9,15},{10,... | collective-permute-start | bytes 393224 | tf_op jit(solution)/shard_map/ppermute | solution.py:358
  101.1 1.2 %collective-permute-start.2 = (bf16[512,128]{1,0:T(8,128)(2,1)S(1)}, bf16[512,128]{1,0:T(8,128)(2,1)S(1)}, u32[]{:S(2)}, u32[]{:S(2)}) collective-permute-start(bf16[512,128]{1,0:T(8,128)(2,1)S(1)} %constant_dynamic-update-slice_fusion.near_ref), channel_id=1, source_target_pairs={{0,4},{1,5},{2,6},{3,7},{4,0},{5,1},{6,2},{7,3},{8,12},{9,13},{10,... | collective-permute-start | bytes 393224 | tf_op jit(solution)/shard_map/ppermute | solution.py:358
  102.3 0.6 collective-permute-start.1
  102.8 2.1 %collective-permute-done.3.refs_2_ = bf16[512,128]{1,0:T(8,128)(2,1)S(1)} collective-permute-done((bf16[512,128]{1,0:T(8,128)(2,1)S(1)}, bf16[512,128]{1,0:T(8,128)(2,1)S(1)}, u32[]{:S(2)}, u32[]{:S(2)}) %collective-permute-start.3) | collective-permute-done | bytes 131104 | tf_op jit(solution)/shard_map/ppermute | solution.py:358
  104.9 2.7 %collective-permute-done.2.refs_1_ = bf16[512,128]{1,0:T(8,128)(2,1)S(1)} collective-permute-done((bf16[512,128]{1,0:T(8,128)(2,1)S(1)}, bf16[512,128]{1,0:T(8,128)(2,1)S(1)}, u32[]{:S(2)}, u32[]{:S(2)}) %collective-permute-start.2) | collective-permute-done | bytes 131104 | tf_op jit(solution)/shard_map/ppermute | solution.py:358
  107.6 1.4 %collective-permute-done.1.refs_0_ = bf16[512,128]{1,0:T(8,128)(2,1)S(1)} collective-permute-done((bf16[512,128]{1,0:T(8,128)(2,1)S(1)}, bf16[512,128]{1,0:T(8,128)(2,1)S(1)}, u32[]{:S(2)}, u32[]{:S(2)}) %collective-permute-start.1) | collective-permute-done | bytes 131104 | tf_op jit(solution)/shard_map/ppermute | solution.py:358
  108.9 0.8 lay.1
  (2 shorter events, 0.0 us)
Async XLA Ops:
  2.4 15.2 %all-to-all-start = ((bf16[8,96,128]{2,1,0:T(8,128)(2,1)}), bf16[8,96,128]{2,1,0:T(8,128)(2,1)S(1)}, u32[]{:S(2)}, u32[]{:S(2)}) async-start(bf16[8,96,128]{2,1,0:T(8,128)(2,1)} %get-tuple-element.15), calls=%async_computation | async-start | bytes 393216 | tf_op jit(solution)/shard_map/all_to_all | solution.py:376
  9.5 8.2 %copy-start.3 = (bf16[1280,128]{1,0:T(8,128)(2,1)S(1)}, bf16[1280,128]{1,0:T(8,128)(2,1)}, u32[]{:S(2)}) copy-start(bf16[1280,128]{1,0:T(8,128)(2,1)} %own_ref.1) | copy-start | bytes 983044
  9.5 8.2 %copy-start.4 = (s32[4096,1,4]{0,2,1:T(4,128)S(1)}, s32[4096,1,4]{0,2,1:T(4,128)}, u32[]{:S(2)}) copy-start(s32[4096,1,4]{0,2,1:T(4,128)} %param.17) | copy-start | bytes 196612
  9.5 8.2 %copy-start.5 = (s32[4096,1]{0,1:T(1,128)S(1)}, s32[4096,1]{0,1:T(1,128)}, u32[]{:S(2)}) copy-start(s32[4096,1]{0,1:T(1,128)} %param.18) | copy-start | bytes 49156
  9.5 8.2 %copy-start.6 = (s32[6]{0:T(128)S(1)}, s32[6]{0:T(128)}, u32[]{:S(2)}) copy-start(s32[6]{0:T(128)} %get-tuple-element.14.order_ref) | copy-start | bytes 76
  17.7 32.2 %copy-start.1 = (bf16[2048,1024]{1,0:T(8,128)(2,1)S(1)}, bf16[2048,1024]{1,0:T(8,128)(2,1)}, u32[]{:S(2)}) copy-start(bf16[2048,1024]{1,0:T(8,128)(2,1)} %top_ref.1) | copy-start | bytes 12582916
  17.7 32.2 %copy-start.2 = (bf16[256,1024]{1,0:T(8,128)(2,1)S(1)}, bf16[256,1024]{1,0:T(8,128)(2,1)}, u32[]{:S(2)}) copy-start(bf16[256,1024]{1,0:T(8,128)(2,1)} %cot_ref.1) | copy-start | bytes 1572868
  72.1 21.2 %copy-start = (f32[2,128]{1,0:T(2,128)S(1)}, f32[2,128]{1,0:T(2,128)}, u32[]{:S(2)}) copy-start(f32[2,128]{1,0:T(2,128)} %get-tuple-element.21.accum_ref) | copy-start | bytes 3076
  94.1 5.8 %collective-permute-start = (bf16[256,128]{1,0:T(8,128)(2,1)S(1)}, bf16[256,128]{1,0:T(8,128)(2,1)S(1)}, u32[]{:S(2)}, u32[]{:S(2)}) collective-permute-start(bf16[256,128]{1,0:T(8,128)(2,1)S(1)} %get-tuple-element.22), channel_id=1, source_target_pairs={{0,1},{1,0},{2,3},{3,2},{4,5},{5,4},{6,7},{7,6},{8,9},{9,8},{10,11... | collective-permute-start | bytes 196616 | tf_op jit(solution)/shard_map/ppermute | solution.py:360
  99.9 5.0 %collective-permute-start.3 = (bf16[512,128]{1,0:T(8,128)(2,1)S(1)}, bf16[512,128]{1,0:T(8,128)(2,1)S(1)}, u32[]{:S(2)}, u32[]{:S(2)}) collective-permute-start(bf16[512,128]{1,0:T(8,128)(2,1)S(1)} %constant_dynamic-update-slice_fusion.near_ref), channel_id=1, source_target_pairs={{0,6},{1,7},{2,0},{3,1},{4,2},{5,3},{6,4},{7,5},{8,14},{9,15},{10,... | collective-permute-start | bytes 393224 | tf_op jit(solution)/shard_map/ppermute | solution.py:358
  101.1 6.5 %collective-permute-start.2 = (bf16[512,128]{1,0:T(8,128)(2,1)S(1)}, bf16[512,128]{1,0:T(8,128)(2,1)S(1)}, u32[]{:S(2)}, u32[]{:S(2)}) collective-permute-start(bf16[512,128]{1,0:T(8,128)(2,1)S(1)} %constant_dynamic-update-slice_fusion.near_ref), channel_id=1, source_target_pairs={{0,4},{1,5},{2,6},{3,7},{4,0},{5,1},{6,2},{7,3},{8,12},{9,13},{10,... | collective-permute-start | bytes 393224 | tf_op jit(solution)/shard_map/ppermute | solution.py:358
  102.3 6.7 %collective-permute-start.1 = (bf16[512,128]{1,0:T(8,128)(2,1)S(1)}, bf16[512,128]{1,0:T(8,128)(2,1)S(1)}, u32[]{:S(2)}, u32[]{:S(2)}) collective-permute-start(bf16[512,128]{1,0:T(8,128)(2,1)S(1)} %constant_dynamic-update-slice_fusion.near_ref), channel_id=1, source_target_pairs={{0,2},{1,3},{2,4},{3,5},{4,6},{5,7},{6,0},{7,1},{8,10},{9,11},{10,... | collective-permute-start | bytes 393224 | tf_op jit(solution)/shard_map/ppermute | solution.py:358

commit v8 on v7

--- a/solution.py
+++ b/solution.py
@@ -15,6 +15,7 @@
 NB = R + SLAB
 TILE = 16
 EACH = 4
+FRONT = 8
 WIDE = K * BLK
 
 learn_rate = 0.5
@@ -69,64 +70,88 @@
     return piece
 
 
-def early_body(weight_hbm, out_hbm, window, perm_ref, part_ref, in_sem, out_sem):
-    groups = part_ref.shape[0]
-    pieces = groups // EACH
-    fetch = fetches(weight_hbm, 0, window, in_sem, pieces)
-
-    def send(piece):
+def early_body(block_ref, count_ref, weight_hbm, front_hbm, out_hbm, window, perm_ref, near_ref, front, part_ref, in_sem, front_sem, out_sem):
+    ahead = front.shape[0] // EACH
+    rest = part_ref.shape[0] // EACH
+    fetch = fetches(weight_hbm, 0, window, in_sem, ahead + rest)
+
+    def send(source, target, sem, piece):
         span = pl.ds(pl.multiple_of(piece * EACH, EACH), EACH)
-        return pltpu.make_async_copy(part_ref.at[span], out_hbm.at[span], out_sem.at[piece])
-
-    for n in range(pieces):
+        return pltpu.make_async_copy(source.at[span], target.at[span], sem.at[piece])
+
+    for n in range(ahead + rest):
         fetch(n).start()
     fill_perm(perm_ref)
 
-    def step(piece, carry):
+    def lead(piece, carry):
         fetch(piece).wait()
         for g in range(EACH):
+            turn(window, pl.multiple_of((piece * EACH + g) * WIDE, WIDE), perm_ref, near_ref, g)
+        for g in range(EACH):
             group = piece * EACH + g
-            turn(window, pl.multiple_of(group * WIDE, WIDE), perm_ref, part_ref, group)
-        send(piece).start()
-        return carry
-
-    lax.fori_loop(0, pieces, step, 0)
-    for n in range(pieces):
-        send(n).wait()
-
-
-def early(weights):
+            place(block_ref, count_ref, pl.multiple_of(group * BLK, BLK), near_ref, g, front, group)
+        send(front, front_hbm, front_sem, piece).start()
+        return carry
+
+    lax.fori_loop(0, ahead, lead, 0)
+
+    def step(piece, carry):
+        fetch(ahead + piece).wait()
+        for g in range(EACH):
+            group = piece * EACH + g
+            at = pl.multiple_of((ahead * EACH + group) * WIDE, WIDE)
+            turn(window, at, perm_ref, part_ref, group)
+        send(part_ref, out_hbm, out_sem, piece).start()
+        return carry
+
+    lax.fori_loop(0, rest, step, 0)
+    for n in range(ahead):
+        send(front, front_hbm, front_sem, n).wait()
+    for n in range(rest):
+        send(part_ref, out_hbm, out_sem, n).wait()
+
+
+def early(blocks, counts, weights):
     groups = weights.shape[0] // WIDE
-    parts = (groups, K, BLK, BLK)
-    sem = pltpu.SemaphoreType.DMA((groups // EACH,))
+    parts = (groups - FRONT, K, BLK, BLK)
+    front = (FRONT, NB * BLK, BLK)
     return pl.pallas_call(
         early_body,
-        in_specs=[HBM],
-        out_specs=ANY,
-        out_shape=jax.ShapeDtypeStruct(parts, jnp.bfloat16),
+        in_specs=[VMEM, VMEM, HBM],
+        out_specs=[HBM, HBM],
+        out_shape=[jax.ShapeDtypeStruct(front, jnp.bfloat16), jax.ShapeDtypeStruct(parts, jnp.bfloat16)],
         scratch_shapes=[
             pltpu.VMEM(weights.shape, jnp.bfloat16),
             pltpu.VMEM((K, WIDE, BLK), jnp.bfloat16),
+            pltpu.VMEM((EACH, K, BLK, BLK), jnp.bfloat16),
+            pltpu.VMEM(front, jnp.bfloat16),
             pltpu.VMEM(parts, jnp.bfloat16),
-            sem,
-            sem,
+            pltpu.SemaphoreType.DMA((groups // EACH,)),
+            pltpu.SemaphoreType.DMA((FRONT // EACH,)),
+            pltpu.SemaphoreType.DMA((parts[0] // EACH,)),
         ],
         cost_estimate=pl.CostEstimate(
             flops=2 * weights.size * WIDE * 4, bytes_accessed=weights.size * 4, transcendentals=0
         ),
         name="early",
-    )(weights)
+    )(blocks, counts, weights)
 
 
 def pool_body(
-    order_ref, block_ref, count_ref, own_ref, slab_ref, part_hbm,
+    order_ref, block_ref, count_ref, own_ref, slab_ref, front_hbm, part_hbm,
     pooled, first, second, share_ref,
-    part_ref, table_ref, turned_ref, part_sem,
+    part_ref, table_ref, turned_ref, front_sem, part_sem,
 ):
     half = first.shape[0]
-    pieces = 2 * half // EACH
+    pieces = (2 * half - FRONT) // EACH
     fetch = fetches(part_hbm, 0, part_ref, part_sem, pieces)
-    for n in range(pieces):
+    again = fetches(front_hbm, 0, first.at[pl.ds(0, FRONT)], front_sem, FRONT // 2)
+    lead = (half - FRONT) // EACH
+    for n in range(lead):
+        fetch(n).start()
+    for n in range(FRONT // 2):
+        again(n).start()
+    for n in range(lead, pieces):
         fetch(n).start()
     table_ref[0 : R * BLK, :] = own_ref[...]
     for j in range(SLAB):
@@ -143,23 +168,25 @@
         pooled[pl.ds(pl.multiple_of(to * BLK, BLK), count * BLK), :] = got.T.astype(jnp.bfloat16)
 
     def put(group, target, at):
-        place(block_ref, count_ref, pl.multiple_of(group * BLK, BLK), part_ref, group, target, at)
+        place(block_ref, count_ref, pl.multiple_of(group * BLK, BLK), part_ref, group - FRONT, target, at)
 
     def fill(pair, carry):
         @pl.when(lax.rem(pair, EACH // 2) == 0)
         def _():
-            fetch(pair // (EACH // 2)).wait()
+            fetch(pair // (EACH // 2) - FRONT // EACH).wait()
 
         for g in range(2):
             put(2 * pair + g, first, 2 * pair + g)
         return carry
 
-    lax.fori_loop(0, half // 2, fill, 0)
+    lax.fori_loop(FRONT // 2, half // 2, fill, 0)
+    for n in range(FRONT // 2):
+        again(n).wait()
 
     def both(pair, carry):
         @pl.when(lax.rem(pair, EACH // 2) == 0)
         def _():
-            fetch(half // EACH + pair // (EACH // 2)).wait()
+            fetch(lead + pair // (EACH // 2)).wait()
 
         for g in range(2):
             put(half + 2 * pair + g, second, 2 * pair + g)
@@ -175,12 +202,12 @@
     lax.fori_loop(0, half // 4, rest, 0)
 
 
-def pool(order, blocks, counts, own, slab, parts, share):
+def pool(order, blocks, counts, own, slab, front, parts, share):
     bags = blocks.shape[1]
     matrix = pltpu.VMEM((bags // (2 * BLK), NB * BLK, BLK), jnp.bfloat16)
     return pl.pallas_call(
         pool_body,
-        in_specs=[SMEM, VMEM, VMEM, VMEM, VMEM, HBM],
+        in_specs=[SMEM, VMEM, VMEM, VMEM, VMEM, HBM, HBM],
         out_specs=[VMEM, VMEM, VMEM, VMEM],
         out_shape=[
             jax.ShapeDtypeStruct((bags, E), jnp.bfloat16),
@@ -192,6 +219,7 @@
             pltpu.VMEM(parts.shape, jnp.bfloat16),
             pltpu.VMEM((NB * BLK, E), jnp.bfloat16),
             pltpu.VMEM((E, NB * BLK), jnp.bfloat16),
+            pltpu.SemaphoreType.DMA((FRONT // 2,)),
             pltpu.SemaphoreType.DMA((parts.shape[0] // EACH,)),
         ],
         cost_estimate=pl.CostEstimate(
@@ -199,7 +227,7 @@
         ),
         compiler_params=pltpu.CompilerParams(vmem_limit_bytes=36 << 20),
         name="pool",
-    )(order, blocks, counts, own, slab, parts)
+    )(order, blocks, counts, own, slab, front, parts)
 
 
 def layer_body(pair, fan_ref, top_ref, cot_ref, hid_hbm, out_ref, hid_ref, sum_ref, pre_ref, sem):
@@ -342,15 +370,20 @@
 
 
 def lay_body(near_ref, *refs):
-    out_ref = refs[-1]
+    refs, (out_hbm, sem) = refs[:-2], refs[-2:]
     size = near_ref.shape[0] // 2
     me = lax.axis_index("dp")
-    across = out_ref.shape[0] // (2 * size)
-    for step, ref in enumerate((near_ref,) + refs[:-1]):
+    across = out_hbm.shape[0] // (2 * size)
+    copies = []
+    for step, ref in enumerate((near_ref,) + tuple(refs)):
         there = lax.rem(me // 2 + across - step, across) * 2
         for half, side in enumerate((lax.rem(me, 2), 1 - lax.rem(me, 2))):
             at = pl.multiple_of((there + side) * size, size)
-            out_ref[pl.ds(at, size), :] = ref[half * size : (half + 1) * size, :]
+            source = ref.at[pl.ds(half * size, size), :]
+            copies.append(pltpu.make_async_copy(source, out_hbm.at[pl.ds(at, size), :], sem.at[step * 2 + half]))
+            copies[-1].start()
+    for copy in copies:
+        copy.wait()
 
 
 def spread_rows(rows, parts):
@@ -365,7 +398,8 @@
     return pl.pallas_call(
         lay_body,
         in_specs=[VMEM] * across,
-        out_specs=VMEM,
+        out_specs=HBM,
+        scratch_shapes=[pltpu.SemaphoreType.DMA((parts,))],
         out_shape=jax.ShapeDtypeStruct((parts * rows.shape[0], rows.shape[1]), rows.dtype),
         compiler_params=pltpu.CompilerParams(vmem_limit_bytes=8 << 20),
         name="lay",
@@ -398,8 +432,8 @@
     blocks = bag_blocks[:, 0, :].T
     counts = bag_counts.reshape(1, bag_total)
     weights = bag_weights.reshape(bag_total * K, BLK)
-    parts_turned = early(weights)
-    pooled, before, after, rows = pool(order, blocks, counts, own_table, slab_rows, parts_turned, share)
+    front, turned = early(blocks, counts, weights)
+    pooled, before, after, rows = pool(order, blocks, counts, own_table, slab_rows, front, turned, share)
     fan = swap(pooled.reshape(tables, bag_total // tables, E), "table")
     hidden, back = layer(fan, top_weight, hidden_grad)
     row_grad = grad(before, after, swap(back, "table").reshape(bag_total, E))

time: 110 us -> 112 us (1.018)
  Pallas kernels: 28 us -> 29.7 us
  blocking collectives: 57 us -> 58.6 us
  waiting for transfers between devices: 12.8 us -> 11.2 us
    pallas_call x3, Pallas kernels: 17.3 us -> 18.8 us  [the longest x1 10.4 us: pool(): pl.pallas_call(pool_body, in_specs=[SMEM, VMEM, VMEM, VMEM, VMEM, HBM, HB...]
    all_to_all x1, waiting for transfers between devices: 2.11 us -> 0.55 us  [swap(): return lax.all_to_all(blocks, axis, split_axis=0, concat_axis=0, tiled=True)]
    all_to_all x3, blocking collectives: 57 us -> 58.6 us  [swap(): return lax.all_to_all(blocks, axis, split_axis=0, concat_axis=0, tiled=True)]
  transfers between devices with their start and end apart: 5 -> 5, of which waited for: 5 -> 5; matrix products, arithmetic and copies ran while one was open for 0% -> 0% of each run, Pallas kernels for 5% -> 7%
where the time goes in v8:
time: 112 us; the launch traced here: 111 us
  blocking collectives  58.6 us (52%)
  Pallas kernels  29.7 us (27%)
  starting transfers between devices  11.2 us (10%)
  waiting for transfers between devices  11.2 us (10%)
    all_to_all x3, blocking collectives, swap(): return lax.all_to_all(blocks, axis, split_axis=0, concat_axis=0, tiled=True)  58.6 us
    pallas_call x1, Pallas kernels, pool(): pl.pallas_call(pool_body, in_specs=[SMEM, VMEM, VMEM, VMEM, VMEM, HBM, HB...  10.4 us
    pallas_call x1, Pallas kernels, early(): pl.pallas_call(early_body, in_specs=[VMEM, VMEM, HBM], out_specs=[HBM, HB...  7.58 us
    all_to_all x1, starting transfers between devices, swap(): return lax.all_to_all(blocks, axis, split_axis=0, concat_axis=0, tiled=True)  7.05 us
    ppermute x3, waiting for transfers between devices, along(): lax.ppermute(block, 'dp', [(n, (n + 2 * step) % parts) for n in range(par...  6.1 us
    pallas_call x1, Pallas kernels, grad(): pl.pallas_call(functools.partial(grad_body, tile), in_specs=[VMEM, VMEM,...  5.03 us
    ppermute x1, waiting for transfers between devices, spread_rows(): other = lax.ppermute(rows, 'dp', [(n, n ^ 1) for n in range(parts)])  4.56 us
    pallas_call x1, Pallas kernels, layer(): pl.pallas_call(functools.partial(layer_body, pair), in_specs=[VMEM, VMEM,...  3.23 us
  transfers between devices with their start and end apart: 5, of which 5 were waited for; matrix products, arithmetic and copies ran while one was open for 0% of the time, Pallas kernels for 7%

profile of v8, /device:TPU:0, one launch (start us, length us, event | category | flops | bytes accessed | tf_op | source)
XLA Modules:
  0.0 111.5 jit_solution(49088410034142836)
XLA Ops:
  0.6 1.8 %pick.1 = (bf16[8,96,128]{2,1,0:T(8,128)(2,1)}, s32[6]{0:T(128)}, f32[2,128]{1,0:T(2,128)}) custom-call(s32[16]{0:T(128)} %pair_ref.1, s32[6,16]{1,0:T(8,128)} %bitcast.21, bf16[16,96,128]{2,1,0:T(8,128)(2,1)} %sect_ref.1, f32[16,768]{1,0:T(8,128)} %state_ref.1, f32[10,128]{1,0:T(8,128)} %bitcast.20), custom_call_target="tpu_custom_call" | custom-call | tf_op jit(solution)/shard_map/pick/pallas_call | solution.py:332
  2.4 7.1 %all-to-all-start = ((bf16[8,96,128]{2,1,0:T(8,128)(2,1)}), bf16[8,96,128]{2,1,0:T(8,128)(2,1)S(1)}, u32[]{:S(2)}, u32[]{:S(2)}) async-start(bf16[8,96,128]{2,1,0:T(8,128)(2,1)} %get-tuple-element.17), calls=%async_computation | async-start | bytes 393216 | tf_op jit(solution)/shard_map/all_to_all | solution.py:410
  9.5 0.0 copy-start.3
  9.5 0.0 copy-start.4
  9.5 0.0 copy-start.5
  9.5 0.0 copy-start.6
  9.5 7.6 %early.1 = (bf16[8,2048,128]{2,1,0:T(8,128)(2,1)}, bf16[24,4,128,128]{3,2,1,0:T(8,128)(2,1)}) custom-call(s32[4,4096]{1,0:T(4,128)} %bitcast.16, s32[1,4096]{1,0:T(1,128)} %bitcast.18, bf16[16384,128]{1,0:T(8,128)(2,1)} %bitcast.22), custom_call_target="tpu_custom_call" | custom-call | flops 8589934592 | bytes 8388608 | tf_op jit(solution)/shard_map/early/pallas_call | solution.py:118
  17.1 0.5 all-to-all-done
  17.6 0.0 copy-done.3
  17.6 0.0 copy-done.4
  17.6 0.0 copy-done.5
  17.6 0.0 copy-done.6
  17.7 0.0 copy-start.1
  17.7 0.0 copy-start.2
  17.7 10.4 %pool.1 = (bf16[4096,128]{1,0:T(8,128)(2,1)S(1)}, bf16[16,2048,128]{2,1,0:T(8,128)(2,1)S(1)}, bf16[16,2048,128]{2,1,0:T(8,128)(2,1)S(1)}, bf16[256,128]{1,0:T(8,128)(2,1)S(1)}) custom-call(s32[6]{0:T(128)S(1)} %copy-done.6, s32[4,4096]{1,0:T(4,128)S(1)} %bitcast.17, s32[1,4096]{1,0:T(1,128)S(1)} %bitcast.19, bf16[1280,128]{1,0:T(8,128)(2,1)S(1)} %copy-done.3, ...), custom_call_target="tpu_custom_call" | custom-call | flops 2147483648 | bytes 16777216 | tf_op jit(solution)/shard_map/pool/pallas_call | solution.py:208
  28.1 21.8 %all_to_all.20.fan_ref = bf16[16,256,128]{2,1,0:T(8,128)(2,1)S(1)} all-to-all(bf16[16,256,128]{2,1,0:T(8,128)(2,1)S(1)} %bitcast.14), channel_id=1, replica_groups=mesh['table'=16,'dp'=8] {'table'}, dimensions={0} | all-to-all | bytes 2097152 | tf_op jit(solution)/shard_map/all_to_all | solution.py:410
  49.9 0.0 copy-done.1
  49.9 0.0 copy-done.2
  49.9 3.2 %layer.1 = (bf16[256,1024]{1,0:T(8,128)(2,1)}, bf16[16,256,128]{2,1,0:T(8,128)(2,1)S(1)}) custom-call(bf16[16,256,128]{2,1,0:T(8,128)(2,1)S(1)} %all_to_all.20.fan_ref, bf16[2048,1024]{1,0:T(8,128)(2,1)S(1)} %copy-done.1, bf16[256,1024]{1,0:T(8,128)(2,1)S(1)} %copy-done.2), custom_call_target="tpu_custom_call" | custom-call | flops 2147483648 | bytes 1572864 | tf_op jit(solution)/shard_map/layer/pallas_call | solution.py:266
  53.1 19.1 %all_to_all.21 = bf16[16,256,128]{2,1,0:T(8,128)(2,1)S(1)} all-to-all(bf16[16,256,128]{2,1,0:T(8,128)(2,1)S(1)} %get-tuple-element.23), channel_id=1, replica_groups=mesh['table'=16,'dp'=8] {'table'}, dimensions={0} | all-to-all | bytes 2097152 | tf_op jit(solution)/shard_map/all_to_all | solution.py:410
  72.2 0.0 copy-start
  72.2 5.0 %grad.1 = bf16[2048,128]{1,0:T(8,128)(2,1)S(1)} custom-call(bf16[16,2048,128]{2,1,0:T(8,128)(2,1)S(1)} %get-tuple-element.20.before, bf16[16,2048,128]{2,1,0:T(8,128)(2,1)S(1)} %get-tuple-element.21.after, bf16[4096,128]{1,0:T(8,128)(2,1)S(1)} %bitcast.12), custom_call_target="tpu_custom_call" | custom-call | flops 2147483648 | bytes 2097152 | tf_op jit(solution)/shard_map/grad/pallas_call | solution.py:300
  77.2 17.7 %all_to_all.22.part_ref = bf16[8,256,128]{2,1,0:T(8,128)(2,1)S(1)} all-to-all(bf16[8,256,128]{2,1,0:T(8,128)(2,1)S(1)} %bitcast.13), channel_id=1, replica_groups=mesh['table'=16,'dp'=8] {'dp'}, dimensions={0} | all-to-all | bytes 1048576 | tf_op jit(solution)/shard_map/all_to_all | solution.py:410
  94.9 0.0 copy-done
  94.9 0.8 update.1
  95.8 1.2 %collective-permute-start = (bf16[256,128]{1,0:T(8,128)(2,1)S(1)}, bf16[256,128]{1,0:T(8,128)(2,1)S(1)}, u32[]{:S(2)}, u32[]{:S(2)}) collective-permute-start(bf16[256,128]{1,0:T(8,128)(2,1)S(1)} %get-tuple-element.26), channel_id=1, source_target_pairs={{0,1},{1,0},{2,3},{3,2},{4,5},{5,4},{6,7},{7,6},{8,9},{9,8},{10,11... | collective-permute-start | bytes 196616 | tf_op jit(solution)/shard_map/ppermute | solution.py:393
  97.0 4.6 %collective-permute-done = bf16[256,128]{1,0:T(8,128)(2,1)S(1)} collective-permute-done((bf16[256,128]{1,0:T(8,128)(2,1)S(1)}, bf16[256,128]{1,0:T(8,128)(2,1)S(1)}, u32[]{:S(2)}, u32[]{:S(2)}) %collective-permute-start) | collective-permute-done | bytes 65568 | tf_op jit(solution)/shard_map/ppermute | solution.py:393
  101.6 1.2 %collective-permute-start.3 = (bf16[512,128]{1,0:T(8,128)(2,1)S(1)}, bf16[512,128]{1,0:T(8,128)(2,1)S(1)}, u32[]{:S(2)}, u32[]{:S(2)}) collective-permute-start(bf16[512,128]{1,0:T(8,128)(2,1)S(1)} %constant_dynamic-update-slice_fusion.near_ref), channel_id=1, source_target_pairs={{0,6},{1,7},{2,0},{3,1},{4,2},{5,3},{6,4},{7,5},{8,14},{9,15},{10,... | collective-permute-start | bytes 393224 | tf_op jit(solution)/shard_map/ppermute | solution.py:391
  102.7 1.2 %collective-permute-start.2 = (bf16[512,128]{1,0:T(8,128)(2,1)S(1)}, bf16[512,128]{1,0:T(8,128)(2,1)S(1)}, u32[]{:S(2)}, u32[]{:S(2)}) collective-permute-start(bf16[512,128]{1,0:T(8,128)(2,1)S(1)} %constant_dynamic-update-slice_fusion.near_ref), channel_id=1, source_target_pairs={{0,4},{1,5},{2,6},{3,7},{4,0},{5,1},{6,2},{7,3},{8,12},{9,13},{10,... | collective-permute-start | bytes 393224 | tf_op jit(solution)/shard_map/ppermute | solution.py:391
  103.9 0.6 collective-permute-start.1
  104.5 2.1 %collective-permute-done.3.refs_2_ = bf16[512,128]{1,0:T(8,128)(2,1)S(1)} collective-permute-done((bf16[512,128]{1,0:T(8,128)(2,1)S(1)}, bf16[512,128]{1,0:T(8,128)(2,1)S(1)}, u32[]{:S(2)}, u32[]{:S(2)}) %collective-permute-start.3) | collective-permute-done | bytes 131104 | tf_op jit(solution)/shard_map/ppermute | solution.py:391
  106.6 2.7 %collective-permute-done.2.refs_1_ = bf16[512,128]{1,0:T(8,128)(2,1)S(1)} collective-permute-done((bf16[512,128]{1,0:T(8,128)(2,1)S(1)}, bf16[512,128]{1,0:T(8,128)(2,1)S(1)}, u32[]{:S(2)}, u32[]{:S(2)}) %collective-permute-start.2) | collective-permute-done | bytes 131104 | tf_op jit(solution)/shard_map/ppermute | solution.py:391
  109.3 1.4 %collective-permute-done.1.refs_0_ = bf16[512,128]{1,0:T(8,128)(2,1)S(1)} collective-permute-done((bf16[512,128]{1,0:T(8,128)(2,1)S(1)}, bf16[512,128]{1,0:T(8,128)(2,1)S(1)}, u32[]{:S(2)}, u32[]{:S(2)}) %collective-permute-start.1) | collective-permute-done | bytes 131104 | tf_op jit(solution)/shard_map/ppermute | solution.py:391
  110.6 0.8 lay.1
  (2 shorter events, 0.0 us)
Async XLA Ops:
  2.4 15.2 %all-to-all-start = ((bf16[8,96,128]{2,1,0:T(8,128)(2,1)}), bf16[8,96,128]{2,1,0:T(8,128)(2,1)S(1)}, u32[]{:S(2)}, u32[]{:S(2)}) async-start(bf16[8,96,128]{2,1,0:T(8,128)(2,1)} %get-tuple-element.17), calls=%async_computation | async-start | bytes 393216 | tf_op jit(solution)/shard_map/all_to_all | solution.py:410
  9.5 8.2 %copy-start.3 = (bf16[1280,128]{1,0:T(8,128)(2,1)S(1)}, bf16[1280,128]{1,0:T(8,128)(2,1)}, u32[]{:S(2)}) copy-start(bf16[1280,128]{1,0:T(8,128)(2,1)} %own_ref.1) | copy-start | bytes 983044
  9.5 8.2 %copy-start.4 = (s32[4096,1,4]{0,2,1:T(4,128)S(1)}, s32[4096,1,4]{0,2,1:T(4,128)}, u32[]{:S(2)}) copy-start(s32[4096,1,4]{0,2,1:T(4,128)} %param.17) | copy-start | bytes 196612
  9.5 8.2 %copy-start.5 = (s32[4096,1]{0,1:T(1,128)S(1)}, s32[4096,1]{0,1:T(1,128)}, u32[]{:S(2)}) copy-start(s32[4096,1]{0,1:T(1,128)} %param.18) | copy-start | bytes 49156
  9.5 8.2 %copy-start.6 = (s32[6]{0:T(128)S(1)}, s32[6]{0:T(128)}, u32[]{:S(2)}) copy-start(s32[6]{0:T(128)} %get-tuple-element.16.order_ref) | copy-start | bytes 76
  17.7 32.2 %copy-start.1 = (bf16[2048,1024]{1,0:T(8,128)(2,1)S(1)}, bf16[2048,1024]{1,0:T(8,128)(2,1)}, u32[]{:S(2)}) copy-start(bf16[2048,1024]{1,0:T(8,128)(2,1)} %top_ref.1) | copy-start | bytes 12582916
  17.7 32.2 %copy-start.2 = (bf16[256,1024]{1,0:T(8,128)(2,1)S(1)}, bf16[256,1024]{1,0:T(8,128)(2,1)}, u32[]{:S(2)}) copy-start(bf16[256,1024]{1,0:T(8,128)(2,1)} %cot_ref.1) | copy-start | bytes 1572868
  72.2 22.8 %copy-start = (f32[2,128]{1,0:T(2,128)S(1)}, f32[2,128]{1,0:T(2,128)}, u32[]{:S(2)}) copy-start(f32[2,128]{1,0:T(2,128)} %get-tuple-element.25.accum_ref) | copy-start | bytes 3076
  95.8 5.8 %collective-permute-start = (bf16[256,128]{1,0:T(8,128)(2,1)S(1)}, bf16[256,128]{1,0:T(8,128)(2,1)S(1)}, u32[]{:S(2)}, u32[]{:S(2)}) collective-permute-start(bf16[256,128]{1,0:T(8,128)(2,1)S(1)} %get-tuple-element.26), channel_id=1, source_target_pairs={{0,1},{1,0},{2,3},{3,2},{4,5},{5,4},{6,7},{7,6},{8,9},{9,8},{10,11... | collective-permute-start | bytes 196616 | tf_op jit(solution)/shard_map/ppermute | solution.py:393
  101.6 5.0 %collective-permute-start.3 = (bf16[512,128]{1,0:T(8,128)(2,1)S(1)}, bf16[512,128]{1,0:T(8,128)(2,1)S(1)}, u32[]{:S(2)}, u32[]{:S(2)}) collective-permute-start(bf16[512,128]{1,0:T(8,128)(2,1)S(1)} %constant_dynamic-update-slice_fusion.near_ref), channel_id=1, source_target_pairs={{0,6},{1,7},{2,0},{3,1},{4,2},{5,3},{6,4},{7,5},{8,14},{9,15},{10,... | collective-permute-start | bytes 393224 | tf_op jit(solution)/shard_map/ppermute | solution.py:391
  102.7 6.5 %collective-permute-start.2 = (bf16[512,128]{1,0:T(8,128)(2,1)S(1)}, bf16[512,128]{1,0:T(8,128)(2,1)S(1)}, u32[]{:S(2)}, u32[]{:S(2)}) collective-permute-start(bf16[512,128]{1,0:T(8,128)(2,1)S(1)} %constant_dynamic-update-slice_fusion.near_ref), channel_id=1, source_target_pairs={{0,4},{1,5},{2,6},{3,7},{4,0},{5,1},{6,2},{7,3},{8,12},{9,13},{10,... | collective-permute-start | bytes 393224 | tf_op jit(solution)/shard_map/ppermute | solution.py:391
  103.9 6.7 %collective-permute-start.1 = (bf16[512,128]{1,0:T(8,128)(2,1)S(1)}, bf16[512,128]{1,0:T(8,128)(2,1)S(1)}, u32[]{:S(2)}, u32[]{:S(2)}) collective-permute-start(bf16[512,128]{1,0:T(8,128)(2,1)S(1)} %constant_dynamic-update-slice_fusion.near_ref), channel_id=1, source_target_pairs={{0,2},{1,3},{2,4},{3,5},{4,6},{5,7},{6,0},{7,1},{8,10},{9,11},{10,... | collective-permute-start | bytes 393224 | tf_op jit(solution)/shard_map/ppermute | solution.py:391

commit v9 on v7

--- a/solution.py
+++ b/solution.py
@@ -282,10 +282,9 @@
     )(before, after, pooled_grad)
 
 
-def pick_body(pair_ref, ids_ref, sect_ref, state_ref, accum_ref, copies_ref, order_ref, out_ref):
+def pick_body(pair_ref, ids_ref, sect_ref, state_ref, accum_ref, piece_ref, order_ref, out_ref):
     partner = pair_ref[lax.axis_index("table")]
-    for n in range(copies_ref.shape[0]):
-        copies_ref[n] = sect_ref[partner]
+    piece_ref[...] = sect_ref[partner]
     for j in range(SLAB):
         order_ref[j] = ids_ref[j, partner]
     count = out_ref.shape[0]
@@ -306,7 +305,7 @@
         in_specs=[SMEM, SMEM, VMEM, VMEM, VMEM],
         out_specs=[VMEM, SMEM, VMEM],
         out_shape=[
-            jax.ShapeDtypeStruct((parts, size, width), jnp.bfloat16),
+            jax.ShapeDtypeStruct((size, width), jnp.bfloat16),
             jax.ShapeDtypeStruct((SLAB,), jnp.int32),
             jax.ShapeDtypeStruct((NB // parts, BLK), jnp.float32),
         ],
@@ -353,16 +352,18 @@
             out_ref[pl.ds(at, size), :] = ref[half * size : (half + 1) * size, :]
 
 
-def spread_rows(rows, parts):
+def spread_rows(rows, parts, beside=()):
     def along(block, step):
         return lax.ppermute(block, "dp", [(n, (n + 2 * step) % parts) for n in range(parts)])
 
     other = lax.ppermute(rows, "dp", [(n, n ^ 1) for n in range(parts)])
     near = jnp.concatenate([rows, other], axis=0)
+    if beside:
+        near, *beside = lax.optimization_barrier((near, *beside))
     across = parts // 2
     order = [1, across - 1] + list(range(2, across - 1))
     far = dict((step, along(near, step)) for step in order)
-    return pl.pallas_call(
+    laid = pl.pallas_call(
         lay_body,
         in_specs=[VMEM] * across,
         out_specs=VMEM,
@@ -370,6 +371,7 @@
         compiler_params=pltpu.CompilerParams(vmem_limit_bytes=8 << 20),
         name="lay",
     )(near, *[far[step] for step in range(1, across)])
+    return laid, beside
 
 
 def swap(blocks, axis):
@@ -393,11 +395,11 @@
     parts = lax.axis_size("dp")
     share = NB * BLK // parts
     bag_total = bag_blocks.shape[0]
-    copies, order, accum = pick(fold_pairs, slab_ids, sectioned_rows, sectioned_accum, own_accum, parts)
-    slab_rows = swap(copies, "dp").reshape(SLAB * BLK, E)
+    piece, order, accum = pick(fold_pairs, slab_ids, sectioned_rows, sectioned_accum, own_accum, parts)
     blocks = bag_blocks[:, 0, :].T
     counts = bag_counts.reshape(1, bag_total)
     weights = bag_weights.reshape(bag_total * K, BLK)
+    slab_rows, (weights,) = spread_rows(piece, parts, (weights,))
     parts_turned = early(weights)
     pooled, before, after, rows = pool(order, blocks, counts, own_table, slab_rows, parts_turned, share)
     fan = swap(pooled.reshape(tables, bag_total // tables, E), "table")
@@ -405,7 +407,7 @@
     row_grad = grad(before, after, swap(back, "table").reshape(bag_total, E))
     received = swap(row_grad.reshape(parts, share, E), "dp")
     new_rows, accum = update(received, rows, accum)
-    new_table = spread_rows(new_rows, parts)
+    new_table, _ = spread_rows(new_rows, parts)
     return (new_table, accum.reshape(share), hidden)
 
 

time: 110 us -> 113 us (1.027)
  blocking collectives: 57 us -> 58.2 us
    all_to_all x1 -> x0, starting transfers between devices: 7.05 us -> none  [swap(): return lax.all_to_all(blocks, axis, split_axis=0, concat_axis=0, tiled=True)]
    ppermute x3 -> x6, starting transfers between devices: 2.95 us -> 7.58 us  [along(): lax.ppermute(block, 'dp', [(n, (n + 2 * step) % parts) for n in range(par...]
    ppermute x1 -> x2, starting transfers between devices: 1.21 us -> 4.59 us  [spread_rows(): other = lax.ppermute(rows, 'dp', [(n, n ^ 1) for n in range(parts)])]
    ppermute x1 -> x2, waiting for transfers between devices: 4.56 us -> 6.79 us  [spread_rows(): other = lax.ppermute(rows, 'dp', [(n, n ^ 1) for n in range(parts)])]
    all_to_all x1 -> x0, waiting for transfers between devices: 2.11 us -> none  [swap(): return lax.all_to_all(blocks, axis, split_axis=0, concat_axis=0, tiled=True)]
    all_to_all x3, blocking collectives: 57 us -> 58.2 us  [swap(): return lax.all_to_all(blocks, axis, split_axis=0, concat_axis=0, tiled=True)]
    ppermute x3 -> x6, waiting for transfers between devices: 6.1 us -> 6.11 us  [along(): lax.ppermute(block, 'dp', [(n, (n + 2 * step) % parts) for n in range(par...]
  transfers between devices with their start and end apart: 5 -> 8, of which waited for: 5 -> 5; matrix products, arithmetic and copies ran while one was open for 0% -> 0% of each run, Pallas kernels for 5% -> 5%
where the time goes in v9:
time: 113 us
  blocking collectives  58.2 us (52%)
  Pallas kernels  28.1 us (25%)
  waiting for transfers between devices  12.9 us (11%)
  starting transfers between devices  12.2 us (11%)
    all_to_all x3, blocking collectives, swap(): return lax.all_to_all(blocks, axis, split_axis=0, concat_axis=0, tiled=True)  58.2 us
    pallas_call x1, Pallas kernels, pool(): pl.pallas_call(pool_body, in_specs=[SMEM, VMEM, VMEM, VMEM, VMEM, HBM], o...  10.5 us
    ppermute x6, starting transfers between devices, along(): lax.ppermute(block, 'dp', [(n, (n + 2 * step) % parts) for n in range(par...  7.58 us
    ppermute x2, waiting for transfers between devices, spread_rows(): other = lax.ppermute(rows, 'dp', [(n, n ^ 1) for n in range(parts)])  6.79 us
    ppermute x6, waiting for transfers between devices, along(): lax.ppermute(block, 'dp', [(n, (n + 2 * step) % parts) for n in range(par...  6.11 us
    pallas_call x1, Pallas kernels, early(): pl.pallas_call(early_body, in_specs=[HBM], out_specs=ANY, out_shape=jax.S...  5.96 us
    pallas_call x1, Pallas kernels, grad(): pl.pallas_call(functools.partial(grad_body, tile), in_specs=[VMEM, VMEM,...  5.03 us
    ppermute x2, starting transfers between devices, spread_rows(): other = lax.ppermute(rows, 'dp', [(n, n ^ 1) for n in range(parts)])  4.59 us
  transfers between devices with their start and end apart: 8, of which 5 were waited for; matrix products, arithmetic and copies ran while one was open for 0% of the time, Pallas kernels for 5%

profile of v9, /device:TPU:0, one launch (start us, length us, event | category | flops | bytes accessed | tf_op | source)
XLA Modules:
  0.0 112.9 jit_solution(11101054838578957708)
XLA Ops:
  0.6 1.7 %pick.1 = (bf16[96,128]{1,0:T(8,128)(2,1)}, s32[6]{0:T(128)}, f32[2,128]{1,0:T(2,128)}) custom-call(s32[16]{0:T(128)} %pair_ref.1, s32[6,16]{1,0:T(8,128)} %bitcast.17, bf16[16,96,128]{2,1,0:T(8,128)(2,1)} %sect_ref.1, f32[16,768]{1,0:T(8,128)} %state_ref.1, f32[10,128]{1,0:T(8,128)} %bitcast.16), custom_call_target="tpu_custom_call" | custom-call | tf_op jit(solution)/shard_map/pick/pallas_call | solution.py:303
  2.3 3.4 %collective-permute-start = (bf16[96,128]{1,0:T(8,128)(2,1)}, bf16[96,128]{1,0:T(8,128)(2,1)S(1)}, u32[]{:S(2)}, u32[]{:S(2)}) collective-permute-start(bf16[96,128]{1,0:T(8,128)(2,1)} %get-tuple-element.17), channel_id=1, source_target_pairs={{0,1},{1,0},{2,3},{3,2},{4,5},{5,4},{6,7},{7,6},{8,9},{9,8},{10,11... | collective-permute-start | bytes 73736 | tf_op jit(solution)/shard_map/ppermute | solution.py:359
  5.7 2.2 %collective-permute-done = bf16[96,128]{1,0:T(8,128)(2,1)S(1)} collective-permute-done((bf16[96,128]{1,0:T(8,128)(2,1)}, bf16[96,128]{1,0:T(8,128)(2,1)S(1)}, u32[]{:S(2)}, u32[]{:S(2)}) %collective-permute-start) | collective-permute-done | bytes 24608 | tf_op jit(solution)/shard_map/ppermute | solution.py:359
  7.9 0.7 pad_maximum_fusion.near_ref
  8.7 0.0 copy-start.3
  8.7 0.0 copy-start.4
  8.7 0.0 copy-start.5
  8.7 0.0 copy-start.6
  8.7 2.9 %collective-permute-start.3 = (bf16[192,128]{1,0:T(8,128)(2,1)S(1)}, bf16[192,128]{1,0:T(8,128)(2,1)S(1)}, u32[]{:S(2)}, u32[]{:S(2)}) collective-permute-start(bf16[192,128]{1,0:T(8,128)(2,1)S(1)} %pad_maximum_fusion.near_ref), channel_id=1, source_target_pairs={{0,6},{1,7},{2,0},{3,1},{4,2},{5,3},{6,4},{7,5},{8,14},{9,15},{10,... | collective-permute-start | bytes 147464 | tf_op jit(solution)/shard_map/ppermute | solution.py:357
  11.6 0.8 collective-permute-start.2
  12.4 0.9 collective-permute-start.1
  13.3 6.0 %early.1.part_hbm = bf16[32,4,128,128]{3,2,1,0:T(8,128)(2,1)} custom-call(bf16[16384,128]{1,0:T(8,128)(2,1)} %bitcast.18), custom_call_target="tpu_custom_call" | custom-call | flops 8589934592 | bytes 8388608 | tf_op jit(solution)/shard_map/early/pallas_call | solution.py:102
  19.3 0.0 collective-permute-done.3.refs_2_
  19.3 0.0 collective-permute-done.2.refs_1_
  19.3 0.0 collective-permute-done.1.refs_0_
  19.4 0.0 copy-done.3
  19.4 0.0 copy-done.4
  19.4 0.0 copy-done.5
  19.4 0.0 copy-done.6
  19.4 0.0 copy-start.1
  19.4 0.0 copy-start.2
  19.4 10.5 %pool.1 = (bf16[4096,128]{1,0:T(8,128)(2,1)S(1)}, bf16[16,2048,128]{2,1,0:T(8,128)(2,1)S(1)}, bf16[16,2048,128]{2,1,0:T(8,128)(2,1)S(1)}, bf16[256,128]{1,0:T(8,128)(2,1)S(1)}) custom-call(s32[6]{0:T(128)S(1)} %copy-done.6, s32[4,4096]{1,0:T(4,128)S(1)} %bitcast.14, s32[1,4096]{1,0:T(1,128)S(1)} %bitcast.15, bf16[1280,128]{1,0:T(8,128)(2,1)S(1)} %copy-done.3, ...), custom_call_target="tpu_custom_call" | custom-call | flops 2147483648 | bytes 16777216 | tf_op jit(solution)/shard_map/pool/pallas_call | solution.py:181
  30.0 22.7 %all_to_all.15.fan_ref = bf16[16,256,128]{2,1,0:T(8,128)(2,1)S(1)} all-to-all(bf16[16,256,128]{2,1,0:T(8,128)(2,1)S(1)} %bitcast.13), channel_id=1, replica_groups=mesh['table'=16,'dp'=8] {'table'}, dimensions={0} | all-to-all | bytes 2097152 | tf_op jit(solution)/shard_map/all_to_all | solution.py:378
  52.6 0.0 copy-done.1
  52.6 0.0 copy-done.2
  52.6 3.2 %layer.1 = (bf16[256,1024]{1,0:T(8,128)(2,1)}, bf16[16,256,128]{2,1,0:T(8,128)(2,1)S(1)}) custom-call(bf16[16,256,128]{2,1,0:T(8,128)(2,1)S(1)} %all_to_all.15.fan_ref, bf16[2048,1024]{1,0:T(8,128)(2,1)S(1)} %copy-done.1, bf16[256,1024]{1,0:T(8,128)(2,1)S(1)} %copy-done.2), custom_call_target="tpu_custom_call" | custom-call | flops 2147483648 | bytes 1572864 | tf_op jit(solution)/shard_map/layer/pallas_call | solution.py:238
  55.9 19.1 %all_to_all.16 = bf16[16,256,128]{2,1,0:T(8,128)(2,1)S(1)} all-to-all(bf16[16,256,128]{2,1,0:T(8,128)(2,1)S(1)} %get-tuple-element.23), channel_id=1, replica_groups=mesh['table'=16,'dp'=8] {'table'}, dimensions={0} | all-to-all | bytes 2097152 | tf_op jit(solution)/shard_map/all_to_all | solution.py:378
  74.9 0.0 copy-start
  74.9 5.0 %grad.1 = bf16[2048,128]{1,0:T(8,128)(2,1)S(1)} custom-call(bf16[16,2048,128]{2,1,0:T(8,128)(2,1)S(1)} %get-tuple-element.20.before, bf16[16,2048,128]{2,1,0:T(8,128)(2,1)S(1)} %get-tuple-element.21.after, bf16[4096,128]{1,0:T(8,128)(2,1)S(1)} %bitcast.11), custom_call_target="tpu_custom_call" | custom-call | flops 2147483648 | bytes 2097152 | tf_op jit(solution)/shard_map/grad/pallas_call | solution.py:272
  80.0 16.4 %all_to_all.17.part_ref = bf16[8,256,128]{2,1,0:T(8,128)(2,1)S(1)} all-to-all(bf16[8,256,128]{2,1,0:T(8,128)(2,1)S(1)} %bitcast.12), channel_id=1, replica_groups=mesh['table'=16,'dp'=8] {'dp'}, dimensions={0} | all-to-all | bytes 1048576 | tf_op jit(solution)/shard_map/all_to_all | solution.py:378
  96.4 0.0 copy-done
  96.4 0.8 update.1
  97.2 1.2 %collective-permute-start.4 = (bf16[256,128]{1,0:T(8,128)(2,1)S(1)}, bf16[256,128]{1,0:T(8,128)(2,1)S(1)}, u32[]{:S(2)}, u32[]{:S(2)}) collective-permute-start(bf16[256,128]{1,0:T(8,128)(2,1)S(1)} %get-tuple-element.26), channel_id=1, source_target_pairs={{0,1},{1,0},{2,3},{3,2},{4,5},{5,4},{6,7},{7,6},{8,9},{9,8},{10,11... | collective-permute-start | bytes 196616 | tf_op jit(solution)/shard_map/ppermute | solution.py:359
  98.4 4.6 %collective-permute-done.4 = bf16[256,128]{1,0:T(8,128)(2,1)S(1)} collective-permute-done((bf16[256,128]{1,0:T(8,128)(2,1)S(1)}, bf16[256,128]{1,0:T(8,128)(2,1)S(1)}, u32[]{:S(2)}, u32[]{:S(2)}) %collective-permute-start.4) | collective-permute-done | bytes 65568 | tf_op jit(solution)/shard_map/ppermute | solution.py:359
  103.0 1.2 %collective-permute-start.7 = (bf16[512,128]{1,0:T(8,128)(2,1)S(1)}, bf16[512,128]{1,0:T(8,128)(2,1)S(1)}, u32[]{:S(2)}, u32[]{:S(2)}) collective-permute-start(bf16[512,128]{1,0:T(8,128)(2,1)S(1)} %constant_dynamic-update-slice_fusion.near_ref), channel_id=1, source_target_pairs={{0,6},{1,7},{2,0},{3,1},{4,2},{5,3},{6,4},{7,5},{8,14},{9,15},{10,... | collective-permute-start | bytes 393224 | tf_op jit(solution)/shard_map/ppermute | solution.py:357
  104.2 1.2 %collective-permute-start.6 = (bf16[512,128]{1,0:T(8,128)(2,1)S(1)}, bf16[512,128]{1,0:T(8,128)(2,1)S(1)}, u32[]{:S(2)}, u32[]{:S(2)}) collective-permute-start(bf16[512,128]{1,0:T(8,128)(2,1)S(1)} %constant_dynamic-update-slice_fusion.near_ref), channel_id=1, source_target_pairs={{0,4},{1,5},{2,6},{3,7},{4,0},{5,1},{6,2},{7,3},{8,12},{9,13},{10,... | collective-permute-start | bytes 393224 | tf_op jit(solution)/shard_map/ppermute | solution.py:357
  105.4 0.6 collective-permute-start.5
  105.9 2.1 %collective-permute-done.7.refs_2_ = bf16[512,128]{1,0:T(8,128)(2,1)S(1)} collective-permute-done((bf16[512,128]{1,0:T(8,128)(2,1)S(1)}, bf16[512,128]{1,0:T(8,128)(2,1)S(1)}, u32[]{:S(2)}, u32[]{:S(2)}) %collective-permute-start.7) | collective-permute-done | bytes 131104 | tf_op jit(solution)/shard_map/ppermute | solution.py:357
  108.0 2.7 %collective-permute-done.6.refs_1_ = bf16[512,128]{1,0:T(8,128)(2,1)S(1)} collective-permute-done((bf16[512,128]{1,0:T(8,128)(2,1)S(1)}, bf16[512,128]{1,0:T(8,128)(2,1)S(1)}, u32[]{:S(2)}, u32[]{:S(2)}) %collective-permute-start.6) | collective-permute-done | bytes 131104 | tf_op jit(solution)/shard_map/ppermute | solution.py:357
  110.7 1.4 %collective-permute-done.5.refs_0_ = bf16[512,128]{1,0:T(8,128)(2,1)S(1)} collective-permute-done((bf16[512,128]{1,0:T(8,128)(2,1)S(1)}, bf16[512,128]{1,0:T(8,128)(2,1)S(1)}, u32[]{:S(2)}, u32[]{:S(2)}) %collective-permute-start.5) | collective-permute-done | bytes 131104 | tf_op jit(solution)/shard_map/ppermute | solution.py:357
  112.0 0.8 lay.3
  (3 shorter events, 0.1 us)
Async XLA Ops:
  2.3 5.6 %collective-permute-start = (bf16[96,128]{1,0:T(8,128)(2,1)}, bf16[96,128]{1,0:T(8,128)(2,1)S(1)}, u32[]{:S(2)}, u32[]{:S(2)}) collective-permute-start(bf16[96,128]{1,0:T(8,128)(2,1)} %get-tuple-element.17), channel_id=1, source_target_pairs={{0,1},{1,0},{2,3},{3,2},{4,5},{5,4},{6,7},{7,6},{8,9},{9,8},{10,11... | collective-permute-start | bytes 73736 | tf_op jit(solution)/shard_map/ppermute | solution.py:359
  8.7 10.7 %copy-start.3 = (bf16[1280,128]{1,0:T(8,128)(2,1)S(1)}, bf16[1280,128]{1,0:T(8,128)(2,1)}, u32[]{:S(2)}) copy-start(bf16[1280,128]{1,0:T(8,128)(2,1)} %own_ref.1) | copy-start | bytes 983044
  8.7 10.7 %copy-start.4 = (s32[4096,1,4]{0,2,1:T(4,128)S(1)}, s32[4096,1,4]{0,2,1:T(4,128)}, u32[]{:S(2)}) copy-start(s32[4096,1,4]{0,2,1:T(4,128)} %param.17) | copy-start | bytes 196612
  8.7 10.7 %copy-start.5 = (s32[4096,1]{0,1:T(1,128)S(1)}, s32[4096,1]{0,1:T(1,128)}, u32[]{:S(2)}) copy-start(s32[4096,1]{0,1:T(1,128)} %param.18) | copy-start | bytes 49156
  8.7 10.7 %copy-start.6 = (s32[6]{0:T(128)S(1)}, s32[6]{0:T(128)}, u32[]{:S(2)}) copy-start(s32[6]{0:T(128)} %get-tuple-element.16.order_ref) | copy-start | bytes 76
  8.7 10.6 %collective-permute-start.3 = (bf16[192,128]{1,0:T(8,128)(2,1)S(1)}, bf16[192,128]{1,0:T(8,128)(2,1)S(1)}, u32[]{:S(2)}, u32[]{:S(2)}) collective-permute-start(bf16[192,128]{1,0:T(8,128)(2,1)S(1)} %pad_maximum_fusion.near_ref), channel_id=1, source_target_pairs={{0,6},{1,7},{2,0},{3,1},{4,2},{5,3},{6,4},{7,5},{8,14},{9,15},{10,... | collective-permute-start | bytes 147464 | tf_op jit(solution)/shard_map/ppermute | solution.py:357
  11.6 7.7 %collective-permute-start.2 = (bf16[192,128]{1,0:T(8,128)(2,1)S(1)}, bf16[192,128]{1,0:T(8,128)(2,1)S(1)}, u32[]{:S(2)}, u32[]{:S(2)}) collective-permute-start(bf16[192,128]{1,0:T(8,128)(2,1)S(1)} %pad_maximum_fusion.near_ref), channel_id=1, source_target_pairs={{0,4},{1,5},{2,6},{3,7},{4,0},{5,1},{6,2},{7,3},{8,12},{9,13},{10,... | collective-permute-start | bytes 147464 | tf_op jit(solution)/shard_map/ppermute | solution.py:357
  12.4 6.9 %collective-permute-start.1 = (bf16[192,128]{1,0:T(8,128)(2,1)S(1)}, bf16[192,128]{1,0:T(8,128)(2,1)S(1)}, u32[]{:S(2)}, u32[]{:S(2)}) collective-permute-start(bf16[192,128]{1,0:T(8,128)(2,1)S(1)} %pad_maximum_fusion.near_ref), channel_id=1, source_target_pairs={{0,2},{1,3},{2,4},{3,5},{4,6},{5,7},{6,0},{7,1},{8,10},{9,11},{10,... | collective-permute-start | bytes 147464 | tf_op jit(solution)/shard_map/ppermute | solution.py:357
  19.4 33.2 %copy-start.1 = (bf16[2048,1024]{1,0:T(8,128)(2,1)S(1)}, bf16[2048,1024]{1,0:T(8,128)(2,1)}, u32[]{:S(2)}) copy-start(bf16[2048,1024]{1,0:T(8,128)(2,1)} %top_ref.1) | copy-start | bytes 12582916
  19.4 33.2 %copy-start.2 = (bf16[256,1024]{1,0:T(8,128)(2,1)S(1)}, bf16[256,1024]{1,0:T(8,128)(2,1)}, u32[]{:S(2)}) copy-start(bf16[256,1024]{1,0:T(8,128)(2,1)} %cot_ref.1) | copy-start | bytes 1572868
  74.9 21.4 %copy-start = (f32[2,128]{1,0:T(2,128)S(1)}, f32[2,128]{1,0:T(2,128)}, u32[]{:S(2)}) copy-start(f32[2,128]{1,0:T(2,128)} %get-tuple-element.25.accum_ref) | copy-start | bytes 3076
  97.2 5.8 %collective-permute-start.4 = (bf16[256,128]{1,0:T(8,128)(2,1)S(1)}, bf16[256,128]{1,0:T(8,128)(2,1)S(1)}, u32[]{:S(2)}, u32[]{:S(2)}) collective-permute-start(bf16[256,128]{1,0:T(8,128)(2,1)S(1)} %get-tuple-element.26), channel_id=1, source_target_pairs={{0,1},{1,0},{2,3},{3,2},{4,5},{5,4},{6,7},{7,6},{8,9},{9,8},{10,11... | collective-permute-start | bytes 196616 | tf_op jit(solution)/shard_map/ppermute | solution.py:359
  103.0 5.0 %collective-permute-start.7 = (bf16[512,128]{1,0:T(8,128)(2,1)S(1)}, bf16[512,128]{1,0:T(8,128)(2,1)S(1)}, u32[]{:S(2)}, u32[]{:S(2)}) collective-permute-start(bf16[512,128]{1,0:T(8,128)(2,1)S(1)} %constant_dynamic-update-slice_fusion.near_ref), channel_id=1, source_target_pairs={{0,6},{1,7},{2,0},{3,1},{4,2},{5,3},{6,4},{7,5},{8,14},{9,15},{10,... | collective-permute-start | bytes 393224 | tf_op jit(solution)/shard_map/ppermute | solution.py:357
  104.2 6.5 %collective-permute-start.6 = (bf16[512,128]{1,0:T(8,128)(2,1)S(1)}, bf16[512,128]{1,0:T(8,128)(2,1)S(1)}, u32[]{:S(2)}, u32[]{:S(2)}) collective-permute-start(bf16[512,128]{1,0:T(8,128)(2,1)S(1)} %constant_dynamic-update-slice_fusion.near_ref), channel_id=1, source_target_pairs={{0,4},{1,5},{2,6},{3,7},{4,0},{5,1},{6,2},{7,3},{8,12},{9,13},{10,... | collective-permute-start | bytes 393224 | tf_op jit(solution)/shard_map/ppermute | solution.py:357
  105.4 6.7 %collective-permute-start.5 = (bf16[512,128]{1,0:T(8,128)(2,1)S(1)}, bf16[512,128]{1,0:T(8,128)(2,1)S(1)}, u32[]{:S(2)}, u32[]{:S(2)}) collective-permute-start(bf16[512,128]{1,0:T(8,128)(2,1)S(1)} %constant_dynamic-update-slice_fusion.near_ref), channel_id=1, source_target_pairs={{0,2},{1,3},{2,4},{3,5},{4,6},{5,7},{6,0},{7,1},{8,10},{9,11},{10,... | collective-permute-start | bytes 393224 | tf_op jit(solution)/shard_map/ppermute | solution.py:357
